TPU v7x, 32 devices: a whole 2x2x4 slice. The times are simulated.
32 devices in a mesh: seq: 8 (over z, y), vocab: 4 (over x, core).
Axes of the slice: x: 2, y: 2, z: 4, core: 2. Of those that a mesh axis runs over, the one named last changes fastest.
Arguments:
- q_noised: bfloat16 [1024, 4096], P('seq', 'vocab'), may hold values from -50 to 50
- key_clean: bfloat16 [1024, 1024], P('seq', 'vocab'), may hold values from -5 to 5
- value_clean: bfloat16 [1024, 1024], P('seq', 'vocab'), may hold values from -5 to 5
- key_noised: bfloat16 [1024, 1024], P('seq', 'vocab'), may hold values from -5 to 5
- value_noised: bfloat16 [1024, 1024], P('seq', 'vocab'), may hold values from -5 to 5
- out_weight: bfloat16 [4096, 4096], P('vocab'), may hold values from -0.09375 to 0.09375
- residual: bfloat16 [1024, 4096], P('seq'), may hold values from -52 to 52
- norm_gain: float32 [4096], replicated, may hold values from 0.5 to 1.5
- head_weight: bfloat16 [18944, 4096], P(('seq', 'vocab')), may hold values from -2 to 2
- targets: int32 [1024], replicated, may hold values from 0 to 18943
- mask_flags: int32 [1024], replicated, may hold values from 0 to 1, as said below
- levels: int32 [32], replicated, may hold values from 0 to 11, as said below
Outputs:
- token_loss: float32 [1024], P('seq')
Inputs may be any that keep to these rules, and one draw needn't show every extreme that they name: `mask_flags`: within every block of 32 positions exactly levels + 1 flags are 1; the 128 positions of one index of seq hold at most 48 ones, and some index holds exactly 48 in every draw. `levels`: every block of some index of seq has level 11.
All inputs are finite; a program needn't handle non-finite values.
Results may differ from a plain program's by a relative error of at most 0.00077.
Values may be sent and summed in bfloat16 or wider, within the bound.
No kernel may reach another device: no remote copies, remote signals or barrier semaphores. Data moves between devices by JAX's collectives and lax.ppermute only.
A program may use at most 128 MiB of HBM per device.

v0:
```python
import jax
import jax.numpy as jnp
from jax import lax
from jax.sharding import PartitionSpec as P

D = 4096
HEAD_DIM = 128
BLOCK = 32
CAP = 48


very_low = -1e30
norm_eps = 1e-06


def shifted(block, axis, distance):
    devices = range(lax.axis_size(axis))
    route = [(i - distance, i) for i in devices if i - distance in devices]
    return lax.ppermute(block, axis, route)


def shards(
    q_noised,
    key_clean,
    value_clean,
    key_noised,
    value_noised,
    out_weight,
    residual,
    norm_gain,
    head_weight,
    targets,
    mask_flags,
    levels,
):
    tok_rows = q_noised.shape[0]
    heads_local = q_noised.shape[1] // HEAD_DIM
    kv_local = key_clean.shape[1] // HEAD_DIM
    group = heads_local // kv_local
    seq_index = lax.axis_index("seq")
    seq_count = lax.axis_size("seq")
    vocab_index = lax.axis_index("vocab")
    vocab_count = lax.axis_size("vocab")
    first_row = seq_index * tok_rows
    scale = HEAD_DIM ** (-0.5)
    queries = q_noised.reshape(tok_rows, kv_local, group, HEAD_DIM)
    local_block = jnp.arange(tok_rows) // BLOCK
    query_block = first_row // BLOCK + local_block

    def attend(keys, visible):
        key_heads = keys.reshape(keys.shape[0], kv_local, HEAD_DIM)
        scores = (
            jnp.einsum("qhgd,khd->qhgk", queries, key_heads, preferred_element_type=jnp.float32)
            * scale
        )
        return jnp.where(visible[:, None, None, :], scores, very_low)

    def weigh(weights, values):
        value_heads = values.reshape(values.shape[0], kv_local, HEAD_DIM)
        return jnp.einsum(
            "qhgk,khd->qhgd",
            weights.astype(jnp.bfloat16),
            value_heads,
            preferred_element_type=jnp.float32,
        )

    own_scores = attend(key_noised, local_block[:, None] == local_block[None, :])
    own_top = jnp.max(own_scores, axis=-1)
    own_weights = jnp.exp(own_scores - own_top[..., None])
    start_state = (own_top, jnp.sum(own_weights, axis=-1), weigh(own_weights, value_noised))

    def absorb(running, keys, values, start):
        key_block = (start + jnp.arange(keys.shape[0])) // BLOCK
        visible = key_block[None, :] < query_block[:, None]
        scores = attend(keys, visible)
        new_top = jnp.maximum(running[0], jnp.max(scores, axis=-1))
        decay = jnp.exp(running[0] - new_top)
        weights = jnp.exp(scores - new_top[..., None])
        return (
            new_top,
            running[1] * decay + jnp.sum(weights, axis=-1),
            running[2] * decay[..., None] + weigh(weights, values),
        )

    running = absorb(start_state, key_clean, value_clean, first_row)

    def hop_step(hop_index, packed):
        held, moving = packed
        moving = shifted(moving, "seq", 1)
        source = seq_index - hop_index
        held = lax.cond(
            source >= 0,
            lambda state: absorb(state, moving[0], moving[1], source * tok_rows),
            lambda state: state,
            held,
        )
        return (held, moving)

    running, moving_last = lax.fori_loop(
        1, seq_count, hop_step, (running, jnp.stack([key_clean, value_clean]))
    )
    attention = (
        (running[2] / running[1][..., None])
        .reshape(tok_rows, heads_local * HEAD_DIM)
        .astype(jnp.bfloat16)
    )
    projected = jnp.dot(attention, out_weight, preferred_element_type=jnp.float32)
    my_mask = lax.dynamic_slice_in_dim(mask_flags, first_row, tok_rows)
    my_slot = jnp.cumsum(my_mask) - 1
    chosen = (my_mask[None, :] == 1) & (my_slot[None, :] == jnp.arange(CAP)[:, None])
    selector = chosen.astype(jnp.bfloat16)
    share = projected.shape[1] // vocab_count
    summed = lax.psum_scatter(
        projected.astype(jnp.bfloat16), "vocab", scatter_dimension=1, tiled=True
    ).astype(jnp.float32)
    hidden = (
        lax.dynamic_slice_in_dim(residual, vocab_index * share, share, 1).astype(jnp.float32)
        + summed
    )
    squares = lax.psum(jnp.sum(hidden * hidden, axis=1), "vocab")
    gains = lax.dynamic_slice_in_dim(norm_gain, vocab_index * share, share)
    normed = (hidden * lax.rsqrt(squares / D + norm_eps)[:, None] * gains).astype(jnp.bfloat16)
    picked_rows = jnp.dot(selector, normed, preferred_element_type=jnp.float32).astype(jnp.bfloat16)
    rows_full = lax.all_gather(picked_rows, "vocab", axis=1, tiled=True)
    all_mask = mask_flags.reshape(seq_count, tok_rows)
    all_slot = jnp.cumsum(all_mask, axis=1) - 1
    slot_hit = (all_mask[:, None, :] == 1) & (
        all_slot[:, None, :] == jnp.arange(CAP)[None, :, None]
    )
    slot_targets = jnp.sum(
        jnp.where(slot_hit, targets.reshape(seq_count, tok_rows)[:, None, :], 0), axis=2
    ).reshape(seq_count * CAP)
    vocab_rows = head_weight.shape[0]
    vocab_first = (seq_index * vocab_count + vocab_index) * vocab_rows
    vocab_ids = vocab_first + jnp.arange(vocab_rows)
    logits = jnp.einsum(
        "rd,vd->rv",
        lax.all_gather(rows_full, "seq", axis=0, tiled=True),
        head_weight,
        preferred_element_type=jnp.float32,
    )
    row_top = jnp.max(logits, axis=1)
    row_total = jnp.sum(jnp.exp(logits - row_top[:, None]), axis=1)
    row_pick = jnp.sum(jnp.where(vocab_ids[None, :] == slot_targets[:, None], logits, 0.0), axis=1)
    local_stats = (row_top, row_total, row_pick)
    best = lax.pmax(local_stats[0], ("seq", "vocab"))
    total, picked = lax.psum(
        (local_stats[1] * jnp.exp(local_stats[0] - best), local_stats[2]), ("seq", "vocab")
    )
    my_best = lax.dynamic_slice_in_dim(best, seq_index * CAP, CAP)
    my_total = lax.dynamic_slice_in_dim(total, seq_index * CAP, CAP)
    my_pick = lax.dynamic_slice_in_dim(picked, seq_index * CAP, CAP)
    nll = my_best + jnp.log(my_total) - my_pick
    token_nll = jnp.sum(jnp.where(chosen, nll[:, None], 0.0), axis=0)
    my_levels = lax.dynamic_slice_in_dim(levels, seq_index * (tok_rows // BLOCK), tok_rows // BLOCK)
    token_level = jnp.repeat(my_levels, BLOCK)
    return token_nll / (token_level + 1).astype(jnp.float32)


def solution(mesh):
    in_specs = (
        P("seq", "vocab"),
        P("seq", "vocab"),
        P("seq", "vocab"),
        P("seq", "vocab"),
        P("seq", "vocab"),
        P("vocab", None),
        P("seq", None),
        P(),
        P(("seq", "vocab"), None),
        P(),
        P(),
        P(),
    )
    out_specs = P("seq")
    return jax.shard_map(shards, mesh=mesh, in_specs=in_specs, out_specs=out_specs, check_vma=False)
```

profile of v0, /device:TPU:0, one launch (start us, length us, event | category | flops | bytes accessed | tf_op | source)
XLA Modules:
  0.0 276.1 jit_solution(18406250531270771695)
XLA Ops:
  6.5 0.9 reshape.230
  7.4 1.0 copy.51
  8.4 0.9 reshape.232
  9.3 1.0 copy.52
  10.3 1.1 copy.42
  11.4 0.9 reshape.228
  14.0 56.2 %while.20 = (s32[]{:T(128)}, f32[128,2,4]{0,2,1:T(4,128)S(1)}, f32[128,2,4]{0,2,1:T(4,128)S(1)}, f32[128,2,4,128]{3,0,2,1:T(8,128)S(1)}, bf16[2,128,256]{1,2,0:T...) while((s32[]{:T(128)}, f32[128,2,4]{0,2,1:T(4,128)S(1)}, ...), condition=%wide.region_10.11_spmd.clone, body=%wide.region_5.0_spmd.clone.sunk | while | flops 68310144 | bytes 4167011 | solution.py:99
  14.0 4.9 %collective-permute-start = (bf16[2,128,256]{1,2,0:T(8,128)(2,1)S(1)}, bf16[2,128,256]{1,2,0:T(8,128)(2,1)S(1)}, u32[]{:S(2)}, u32[]{:S(2)}) collective-permute-start(bf16[2,128,256]{1,2,0:T(8,128)(2,1)S(1)} %get-tuple-element.385), channel_id=1, source_target_pairs={{0,4},{4,8},{8,12},{12,16},{16,20},{20,24},{24,28},{1,5},{5,9},{9,... | collective-permute-start | bytes 393224 | tf_op jit(solution)/shard_map/while/body/eval_jaxpr/ppermute | solution.py:19
  18.9 2.7 collective-permute-done
  21.7 5.4 %collective-permute-start = (bf16[2,128,256]{1,2,0:T(8,128)(2,1)S(1)}, bf16[2,128,256]{1,2,0:T(8,128)(2,1)S(1)}, u32[]{:S(2)}, u32[]{:S(2)}) collective-permute-start(bf16[2,128,256]{1,2,0:T(8,128)(2,1)S(1)} %get-tuple-element.385), channel_id=1, source_target_pairs={{0,4},{4,8},{8,12},{12,16},{16,20},{20,24},{24,28},{1,5},{5,9},{9,... | collective-permute-start | bytes 393224 | tf_op jit(solution)/shard_map/while/body/eval_jaxpr/ppermute | solution.py:19
  27.1 2.5 collective-permute-done
  29.6 4.4 %collective-permute-start = (bf16[2,128,256]{1,2,0:T(8,128)(2,1)S(1)}, bf16[2,128,256]{1,2,0:T(8,128)(2,1)S(1)}, u32[]{:S(2)}, u32[]{:S(2)}) collective-permute-start(bf16[2,128,256]{1,2,0:T(8,128)(2,1)S(1)} %get-tuple-element.385), channel_id=1, source_target_pairs={{0,4},{4,8},{8,12},{12,16},{16,20},{20,24},{24,28},{1,5},{5,9},{9,... | collective-permute-start | bytes 393224 | tf_op jit(solution)/shard_map/while/body/eval_jaxpr/ppermute | solution.py:19
  34.0 2.5 collective-permute-done
  36.5 6.3 %collective-permute-start = (bf16[2,128,256]{1,2,0:T(8,128)(2,1)S(1)}, bf16[2,128,256]{1,2,0:T(8,128)(2,1)S(1)}, u32[]{:S(2)}, u32[]{:S(2)}) collective-permute-start(bf16[2,128,256]{1,2,0:T(8,128)(2,1)S(1)} %get-tuple-element.385), channel_id=1, source_target_pairs={{0,4},{4,8},{8,12},{12,16},{16,20},{20,24},{24,28},{1,5},{5,9},{9,... | collective-permute-start | bytes 393224 | tf_op jit(solution)/shard_map/while/body/eval_jaxpr/ppermute | solution.py:19
  42.8 2.5 collective-permute-done
  45.3 5.3 %collective-permute-start = (bf16[2,128,256]{1,2,0:T(8,128)(2,1)S(1)}, bf16[2,128,256]{1,2,0:T(8,128)(2,1)S(1)}, u32[]{:S(2)}, u32[]{:S(2)}) collective-permute-start(bf16[2,128,256]{1,2,0:T(8,128)(2,1)S(1)} %get-tuple-element.385), channel_id=1, source_target_pairs={{0,4},{4,8},{8,12},{12,16},{16,20},{20,24},{24,28},{1,5},{5,9},{9,... | collective-permute-start | bytes 393224 | tf_op jit(solution)/shard_map/while/body/eval_jaxpr/ppermute | solution.py:19
  50.6 2.5 collective-permute-done
  53.1 5.4 %collective-permute-start = (bf16[2,128,256]{1,2,0:T(8,128)(2,1)S(1)}, bf16[2,128,256]{1,2,0:T(8,128)(2,1)S(1)}, u32[]{:S(2)}, u32[]{:S(2)}) collective-permute-start(bf16[2,128,256]{1,2,0:T(8,128)(2,1)S(1)} %get-tuple-element.385), channel_id=1, source_target_pairs={{0,4},{4,8},{8,12},{12,16},{16,20},{20,24},{24,28},{1,5},{5,9},{9,... | collective-permute-start | bytes 393224 | tf_op jit(solution)/shard_map/while/body/eval_jaxpr/ppermute | solution.py:19
  58.6 3.5 %collective-permute-done = bf16[2,128,256]{1,2,0:T(8,128)(2,1)S(1)} collective-permute-done((bf16[2,128,256]{1,2,0:T(8,128)(2,1)S(1)}, bf16[2,128,256]{1,2,0:T(8,128)(2,1)S(1)}, u32[]{:S(2)}, u32[]{:S(2)}) %collective-permute-start) | collective-permute-done | bytes 131104 | tf_op jit(solution)/shard_map/while/body/eval_jaxpr/ppermute | solution.py:19
  62.1 5.6 %collective-permute-start = (bf16[2,128,256]{1,2,0:T(8,128)(2,1)S(1)}, bf16[2,128,256]{1,2,0:T(8,128)(2,1)S(1)}, u32[]{:S(2)}, u32[]{:S(2)}) collective-permute-start(bf16[2,128,256]{1,2,0:T(8,128)(2,1)S(1)} %get-tuple-element.385), channel_id=1, source_target_pairs={{0,4},{4,8},{8,12},{12,16},{16,20},{20,24},{24,28},{1,5},{5,9},{9,... | collective-permute-start | bytes 393224 | tf_op jit(solution)/shard_map/while/body/eval_jaxpr/ppermute | solution.py:19
  67.7 2.5 collective-permute-done
  70.5 5.8 %convolution_convert_fusion = bf16[128,4096]{1,0:T(8,128)(2,1)} fusion(bf16[128,1024]{0,1:T(8,128)(2,1)S(1)} %bitcast.78, bf16[1024,4096]{1,0:T(8,128)(2,1)} %param.21), kind=kOutput, calls=%fused_computation.21 | convolution fusion | flops 1074266112 | bytes 9699328 | tf_op jit(solution)/shard_map/dot_general | solution.py:107
  76.7 0.7 dynamic_slice.23
  77.6 30.5 %reduce-scatter.2.cloned.1.call-done = bf16[128,1024]{1,0:T(8,128)(2,1)} async-done(((bf16[128,4096]{1,0:T(8,128)(2,1)}), bf16[128,1024]{1,0:T(8,128)(2,1)}) %reduce-scatter.2.cloned.1.call-update) | async-done | bytes 262160 | tf_op jit(solution)/shard_map/reduce_scatter | solution.py:113
  108.1 1.1 multiply_reduce_fusion
  109.2 5.8 %psum.21 = f32[128]{0:T(128)S(1)} all-reduce(f32[128]{0:T(128)S(1)} %multiply_reduce_fusion), channel_id=1, replica_groups=mesh['seq'=8,'vocab'=4] {'vocab'}, use_global_device_ids=true, to_apply=%region_13.14 | all-reduce | flops 128 | bytes 1024 | tf_op jit(solution)/shard_map/psum | solution.py:120
  115.0 1.2 convolution_convert_fusion.1
  116.2 6.6 %all_gather.6 = bf16[48,4096]{1,0:T(8,128)(2,1)} all-gather(bf16[48,1024]{1,0:T(8,128)(2,1)S(1)} %convolution_convert_fusion.1), channel_id=1, replica_groups=mesh['seq'=8,'vocab'=4] {'vocab'}, dimensions={1}, use_global_device_ids=true | all-gather | bytes 491520 | tf_op jit(solution)/shard_map/all_gather | solution.py:124
  123.7 59.9 %all-gather.2.cloned.1.call-done = bf16[384,4096]{1,0:T(8,128)(2,1)} async-done(((bf16[48,4096]{1,0:T(8,128)(2,1)}), bf16[384,4096]{1,0:T(8,128)(2,1)}) %all-gather.2.cloned.1.call-update) | async-done | bytes 3145744 | tf_op jit(solution)/shard_map/all_gather | solution.py:138
  183.6 5.6 %fusion.42 = (f32[384]{0:T(512)S(1)}, f32[384,592]{0,1:T(8,128)S(1)}) fusion(bf16[384,4096]{1,0:T(8,128)(2,1)} %all-gather.2.cloned.1.call-done, bf16[592,4096]{1,0:T(8,128)(2,1)} %param.24), kind=kOutput, calls=%fused_computation.91 | convolution fusion | flops 1862497920 | bytes 8906240 | tf_op jit(solution)/shard_map/rd,vd->rv/dot_general | solution.py:136
  189.2 39.2 %pmax.7 = f32[384]{0:T(512)S(1)} all-reduce(f32[384]{0:T(512)S(1)} %get-tuple-element.302), channel_id=1, replica_groups=mesh['seq'=8,'vocab'=4] {'seq','vocab'}, use_global_device_ids=true, to_apply=%region_15.16 | all-reduce | flops 384 | bytes 3072 | tf_op jit(solution)/shard_map/pmax | solution.py:146
  228.6 39.9 %all-reduce = (f32[384]{0:T(512)S(1)}, f32[384]{0:T(512)S(1)}) all-reduce(f32[384]{0:T(512)S(1)} %get-tuple-element.269, f32[384]{0:T(512)S(1)} %exponential_multiply_fusion), channel_id=1, replica_groups=mesh['seq'=8,'vocab'=4] {'seq','vocab'}, use_global_device_ids=true, to_apply=%region_21.22 | all-reduce | flops 768 | bytes 6144 | tf_op jit(solution)/shard_map/psum | solution.py:147
  (79 shorter events, 4.4 us)
Async XLA Ops:
  6.5 7.1 %copy-start.1 = (bf16[128,256]{1,0:T(8,128)(2,1)S(1)}, bf16[128,256]{1,0:T(8,128)(2,1)}, u32[]{:S(2)}) copy-start(bf16[128,256]{1,0:T(8,128)(2,1)} %param.20) | copy-start | bytes 196612
  6.5 101.5 %reduce-scatter.2.cloned.1.call-start = ((), (), s32[]{:S(2)}) async-start(), calls=%async_computation.1 | async-start | bytes 1310720 | tf_op jit(solution)/shard_map/reduce_scatter | solution.py:113
  14.0 7.6 %collective-permute-start = (bf16[2,128,256]{1,2,0:T(8,128)(2,1)S(1)}, bf16[2,128,256]{1,2,0:T(8,128)(2,1)S(1)}, u32[]{:S(2)}, u32[]{:S(2)}) collective-permute-start(bf16[2,128,256]{1,2,0:T(8,128)(2,1)S(1)} %get-tuple-element.385), channel_id=1, source_target_pairs={{0,4},{4,8},{8,12},{12,16},{16,20},{20,24},{24,28},{1,5},{5,9},{9,... | collective-permute-start | bytes 393224 | tf_op jit(solution)/shard_map/while/body/eval_jaxpr/ppermute | solution.py:19
  21.7 7.9 %collective-permute-start = (bf16[2,128,256]{1,2,0:T(8,128)(2,1)S(1)}, bf16[2,128,256]{1,2,0:T(8,128)(2,1)S(1)}, u32[]{:S(2)}, u32[]{:S(2)}) collective-permute-start(bf16[2,128,256]{1,2,0:T(8,128)(2,1)S(1)} %get-tuple-element.385), channel_id=1, source_target_pairs={{0,4},{4,8},{8,12},{12,16},{16,20},{20,24},{24,28},{1,5},{5,9},{9,... | collective-permute-start | bytes 393224 | tf_op jit(solution)/shard_map/while/body/eval_jaxpr/ppermute | solution.py:19
  29.6 6.9 %collective-permute-start = (bf16[2,128,256]{1,2,0:T(8,128)(2,1)S(1)}, bf16[2,128,256]{1,2,0:T(8,128)(2,1)S(1)}, u32[]{:S(2)}, u32[]{:S(2)}) collective-permute-start(bf16[2,128,256]{1,2,0:T(8,128)(2,1)S(1)} %get-tuple-element.385), channel_id=1, source_target_pairs={{0,4},{4,8},{8,12},{12,16},{16,20},{20,24},{24,28},{1,5},{5,9},{9,... | collective-permute-start | bytes 393224 | tf_op jit(solution)/shard_map/while/body/eval_jaxpr/ppermute | solution.py:19
  36.5 8.8 %collective-permute-start = (bf16[2,128,256]{1,2,0:T(8,128)(2,1)S(1)}, bf16[2,128,256]{1,2,0:T(8,128)(2,1)S(1)}, u32[]{:S(2)}, u32[]{:S(2)}) collective-permute-start(bf16[2,128,256]{1,2,0:T(8,128)(2,1)S(1)} %get-tuple-element.385), channel_id=1, source_target_pairs={{0,4},{4,8},{8,12},{12,16},{16,20},{20,24},{24,28},{1,5},{5,9},{9,... | collective-permute-start | bytes 393224 | tf_op jit(solution)/shard_map/while/body/eval_jaxpr/ppermute | solution.py:19
  45.3 7.8 %collective-permute-start = (bf16[2,128,256]{1,2,0:T(8,128)(2,1)S(1)}, bf16[2,128,256]{1,2,0:T(8,128)(2,1)S(1)}, u32[]{:S(2)}, u32[]{:S(2)}) collective-permute-start(bf16[2,128,256]{1,2,0:T(8,128)(2,1)S(1)} %get-tuple-element.385), channel_id=1, source_target_pairs={{0,4},{4,8},{8,12},{12,16},{16,20},{20,24},{24,28},{1,5},{5,9},{9,... | collective-permute-start | bytes 393224 | tf_op jit(solution)/shard_map/while/body/eval_jaxpr/ppermute | solution.py:19
  53.1 8.9 %collective-permute-start = (bf16[2,128,256]{1,2,0:T(8,128)(2,1)S(1)}, bf16[2,128,256]{1,2,0:T(8,128)(2,1)S(1)}, u32[]{:S(2)}, u32[]{:S(2)}) collective-permute-start(bf16[2,128,256]{1,2,0:T(8,128)(2,1)S(1)} %get-tuple-element.385), channel_id=1, source_target_pairs={{0,4},{4,8},{8,12},{12,16},{16,20},{20,24},{24,28},{1,5},{5,9},{9,... | collective-permute-start | bytes 393224 | tf_op jit(solution)/shard_map/while/body/eval_jaxpr/ppermute | solution.py:19
  62.1 8.1 %collective-permute-start = (bf16[2,128,256]{1,2,0:T(8,128)(2,1)S(1)}, bf16[2,128,256]{1,2,0:T(8,128)(2,1)S(1)}, u32[]{:S(2)}, u32[]{:S(2)}) collective-permute-start(bf16[2,128,256]{1,2,0:T(8,128)(2,1)S(1)} %get-tuple-element.385), channel_id=1, source_target_pairs={{0,4},{4,8},{8,12},{12,16},{16,20},{20,24},{24,28},{1,5},{5,9},{9,... | collective-permute-start | bytes 393224 | tf_op jit(solution)/shard_map/while/body/eval_jaxpr/ppermute | solution.py:19
  70.5 5.9 %copy-start.2 = (s32[1024]{0:T(1024)S(1)}, s32[1024]{0:T(1024)}, u32[]{:S(2)}) copy-start(s32[1024]{0:T(1024)} %param.26) | copy-start | bytes 12292
  70.5 37.6 %copy-start = (bf16[128,4096]{1,0:T(8,128)(2,1)S(1)}, bf16[128,4096]{1,0:T(8,128)(2,1)}, u32[]{:S(2)}) copy-start(bf16[128,4096]{1,0:T(8,128)(2,1)} %param.22) | copy-start | bytes 3145732
  70.5 52.6 %copy-start.3 = (s32[1024]{0:T(1024)S(1)}, s32[1024]{0:T(1024)}, u32[]{:S(2)}) copy-start(s32[1024]{0:T(1024)} %param.25) | copy-start | bytes 12292
  70.5 52.9 %copy-start.4 = (s32[32]{0:T(128)S(1)}, s32[32]{0:T(128)}, u32[]{:S(2)}) copy-start(s32[32]{0:T(128)} %param.27) | copy-start | bytes 388
  76.3 107.3 %all-gather.2.cloned.1.call-start = ((), (), s32[]{:S(2)}) async-start(), calls=%async_computation.2 | async-start | bytes 3538944 | tf_op jit(solution)/shard_map/all_gather | solution.py:138
Sparse Core Ops, SparseCore 0:
  76.4 31.6 reduce-scatter.1
  122.9 60.6 all-gather.1
where the time goes:
time: 277 us; the launch traced here: 276 us
  waiting for transfers between devices  109 us (39%)
  blocking collectives  91.5 us (33%)
  starting transfers between devices  37.3 us (13%)
  matrix products  13.6 us (5%)
  between operations  13.6 us (5%)
  local copies, waits for them, and re-layouts  7.28 us (3%)
  other arithmetic  3.48 us (1%)
    all_gather x1, waiting for transfers between devices, shards(): lax.all_gather(rows_full, 'seq', axis=0, tiled=True)  59.9 us
    psum x1, blocking collectives, shards(): lax.psum((local_stats[1] * jnp.exp(local_stats[0] - best), local_stats[2]...  39.9 us
    pmax x1, blocking collectives, shards(): best = lax.pmax(local_stats[0], ('seq', 'vocab'))  39.2 us
    ppermute x7, starting transfers between devices, shifted(): return lax.ppermute(block, axis, route)  37.2 us
    reduce_scatter x1, waiting for transfers between devices, shards(): lax.psum_scatter(projected.astype(jnp.bfloat16), 'vocab', scatter_dimensi...  30.5 us
    ppermute x7, waiting for transfers between devices, shifted(): return lax.ppermute(block, axis, route)  18.6 us
    all_gather x1, blocking collectives, shards(): rows_full = lax.all_gather(picked_rows, 'vocab', axis=1, tiled=True)  6.63 us
    psum x1, blocking collectives, shards(): squares = lax.psum(jnp.sum(hidden * hidden, axis=1), 'vocab')  5.75 us
  transfers between devices with their start and end apart: 9, of which 9 were waited for; matrix products, arithmetic and copies ran while one was open for 1% of the time, Pallas kernels for 0%

commit v1 on v0

v1 whole, which is shorter than its diff:
```python
import jax
import jax.numpy as jnp
from jax import lax
from jax.sharding import PartitionSpec as P

D = 4096
HEAD_DIM = 128
BLOCK = 32
CAP = 48

very_low = -1e30
norm_eps = 1e-06


def shards(
    q_noised,
    key_clean,
    value_clean,
    key_noised,
    value_noised,
    out_weight,
    residual,
    norm_gain,
    head_weight,
    targets,
    mask_flags,
    levels,
):
    tok_rows, q_width = q_noised.shape
    width = residual.shape[1]
    heads_local = q_width // HEAD_DIM
    kv_local = key_clean.shape[1] // HEAD_DIM
    group = heads_local // kv_local
    vocab_rows = head_weight.shape[0]
    S = lax.axis_size("seq")
    V = lax.axis_size("vocab")
    C = 2
    X = V // C
    Y = 2
    Z = S // Y
    HALF = CAP // C
    share = width // X
    seq_index = lax.axis_index("seq")
    vocab_index = lax.axis_index("vocab")
    z, y = seq_index // Y, seq_index % Y
    x, c = vocab_index // C, vocab_index % C
    first_row = seq_index * tok_rows
    scale = HEAD_DIM ** (-0.5)

    def dev(zi, yi, xi, ci):
        return ((zi * Y + yi) * X + xi) * C + ci

    def permute(block, pairs):
        return lax.ppermute(block, ("seq", "vocab"), pairs)

    every = [(zi, yi, xi, ci) for zi in range(Z) for yi in range(Y) for xi in range(X) for ci in range(C)]

    def core_flip(block):
        return permute(block, [(dev(a, b, e, f), dev(a, b, e, 1 - f)) for a, b, e, f in every])

    def x_shift(block, k):
        return permute(block, [(dev(a, b, e, f), dev(a, b, (e + k) % X, f)) for a, b, e, f in every])

    def y_flip(block):
        return permute(block, [(dev(a, b, e, f), dev(a, 1 - b, e, f)) for a, b, e, f in every])

    def z_up(block, k):
        return permute(block, [(dev(a, b, e, f), dev(a + k, b, e, f)) for a, b, e, f in every if a + k < Z])

    def z_shift(block, k):
        return permute(block, [(dev(a, b, e, f), dev((a + k) % Z, b, e, f)) for a, b, e, f in every])

    def mixed_flip(block, first):
        pairs = []
        for a, b, e, f in every:
            if (f == 0) == first:
                pairs.append((dev(a, b, e, f), dev(a, b, 1 - e, f)))
            else:
                pairs.append((dev(a, b, e, f), dev(a, 1 - b, e, f)))
        return permute(block, pairs)

    own_kv = jnp.stack([key_clean, value_clean])
    pieces = [(own_kv, seq_index)]
    pieces.append((y_flip(own_kv), z * Y + 1 - y))
    for k in range(1, Z):
        got = z_up(own_kv, k)
        src = jnp.where(z >= k, (z - k) * Y, S)
        pieces.append((got, src + y))
        pieces.append((y_flip(got), src + 1 - y))
    other_head = core_flip(head_weight)

    all_mask = mask_flags.reshape(S, tok_rows)
    all_slot = jnp.cumsum(all_mask, axis=1) - 1
    slot_hit = (all_mask[:, None, :] == 1) & (all_slot[:, None, :] == jnp.arange(CAP)[None, :, None])
    slot_targets = jnp.sum(jnp.where(slot_hit, targets.reshape(S, 1, tok_rows), 0), axis=2)
    my_mask = lax.dynamic_slice_in_dim(mask_flags, first_row, tok_rows)
    my_slot = jnp.cumsum(my_mask) - 1
    chosen = (my_mask[None, :] == 1) & (my_slot[None, :] == jnp.arange(CAP)[:, None])
    selector = chosen.astype(jnp.bfloat16)
    local_block = jnp.arange(tok_rows) // BLOCK
    slot_block = jnp.sum(jnp.where(chosen, local_block[None, :], 0), axis=1)
    query_block = slot_block + first_row // BLOCK
    rows_block = jnp.tile(query_block, group)
    rows_local = jnp.tile(slot_block, group)
    queries = jnp.dot(selector, q_noised, preferred_element_type=jnp.float32).astype(jnp.bfloat16)
    residual_sel = jnp.dot(selector, residual, preferred_element_type=jnp.float32)

    heads_out = []
    for g in range(kv_local):
        cols = slice(g * HEAD_DIM, (g + 1) * HEAD_DIM)
        q_g = jnp.concatenate(
            [queries[:, (g * group + h) * HEAD_DIM : (g * group + h + 1) * HEAD_DIM] for h in range(group)]
        )

        def attend(keys, visible):
            scores = lax.dot_general(q_g, keys, (((1,), (1,)), ((), ())), preferred_element_type=jnp.float32)
            return jnp.where(visible, scores * scale, very_low)

        parts = [attend(key_noised[:, cols], local_block[None, :] == rows_local[:, None])]
        values = [value_noised[:, cols]]
        for kv, src in pieces:
            key_block = src * (tok_rows // BLOCK) + local_block
            parts.append(attend(kv[0][:, cols], key_block[None, :] < rows_block[:, None]))
            values.append(kv[1][:, cols])
        scores = jnp.concatenate(parts, axis=1)
        top = jnp.max(scores, axis=1, keepdims=True)
        weights = jnp.exp(scores - top)
        total = jnp.sum(weights, axis=1, keepdims=True)
        out = jnp.dot(weights.astype(jnp.bfloat16), jnp.concatenate(values), preferred_element_type=jnp.float32)
        out = (out / total).astype(jnp.bfloat16)
        heads_out += [out[h * CAP : (h + 1) * CAP] for h in range(group)]
    attention = jnp.concatenate(heads_out, axis=1)
    projected = jnp.dot(attention, out_weight, preferred_element_type=jnp.float32)

    mine = lax.dynamic_slice_in_dim(projected, c * HALF, HALF)
    theirs = lax.dynamic_slice_in_dim(projected, (1 - c) * HALF, HALF).astype(jnp.bfloat16)
    mine = mine + core_flip(theirs).astype(jnp.float32)
    sent = mine.astype(jnp.bfloat16)
    summed = sent.astype(jnp.float32)
    for k in range(1, X):
        summed = summed + x_shift(sent, k).astype(jnp.float32)
    hidden = lax.dynamic_slice_in_dim(residual_sel, c * HALF, HALF) + summed
    squares = jnp.sum(hidden * hidden, axis=1, keepdims=True)
    normed = (hidden * lax.rsqrt(squares / D + norm_eps) * norm_gain[None, :]).astype(jnp.bfloat16)

    own = lax.dynamic_slice_in_dim(normed, x * share, share, 1)
    slabs = [own] + [z_shift(own, k) for k in range(1, Z)]
    column = jnp.stack(slabs)
    if X == Y:
        step1 = mixed_flip(column, True)
        both = jnp.stack([column, step1])
        step2 = mixed_flip(both, False)
        quad = jnp.stack([both, step2])
        quad = jnp.where(c == 0, quad, jnp.swapaxes(quad, 0, 1))
        by_x = [quad[:, d] for d in range(X)]
    else:
        pair = jnp.stack([column, y_flip(column)])
        by_x = [pair] + [x_shift(pair, k) for k in range(1, X)]
    stackx = jnp.stack(by_x)
    n_rows = Y * Z * HALF
    order_x = (x - jnp.arange(X)) % X
    logits = []
    for w in (head_weight, other_head):
        total = None
        for k in range(X):
            w_k = lax.dynamic_slice_in_dim(w, ((x - k) % X) * share, share, 1)
            part = lax.dot_general(
                stackx[k].reshape(n_rows, share), w_k, (((1,), (1,)), ((), ())), preferred_element_type=jnp.float32
            )
            total = part if total is None else total + part
        logits.append(total)
    src_y = jnp.stack([y, 1 - y])
    src_z = (z - jnp.arange(Z)) % Z
    src_s = (src_z[None, :] * Y + src_y[:, None]).reshape(Y * Z)
    to_s = (src_s[None, :] == jnp.arange(S)[:, None])
    half_targets = lax.dynamic_slice_in_dim(slot_targets, c * HALF, HALF, 1)
    row_targets = jnp.sum(jnp.where(to_s[:, :, None], half_targets[:, None, :], 0), axis=0).reshape(n_rows)
    first = (seq_index * V + x * C) * vocab_rows
    base = [first + c * vocab_rows, first + (1 - c) * vocab_rows]
    row_top = jnp.maximum(jnp.max(logits[0], axis=1), jnp.max(logits[1], axis=1))
    row_total = 0.0
    row_pick = 0.0
    for b, lg in zip(base, logits):
        row_total = row_total + jnp.sum(jnp.exp(lg - row_top[:, None]), axis=1)
        ids = b + jnp.arange(vocab_rows)
        row_pick = row_pick + jnp.sum(jnp.where(ids[None, :] == row_targets[:, None], lg, 0.0), axis=1)
    row_lse = row_top + jnp.log(row_total)
    stats = jnp.concatenate([row_lse.reshape(S, HALF), row_pick.reshape(S, HALF)], axis=1)
    stats = jnp.sum(jnp.where(to_s[:, :, None], stats[None], 0.0), axis=1)
    stats = jnp.pad(stats, ((0, 0), (0, 128 - 2 * HALF)))
    send = jnp.broadcast_to(stats[:, None], (S, V, 128)).reshape(S * V, 128)
    got = lax.all_to_all(send, ("seq", "vocab"), 0, 0, tiled=True).reshape(S * X, C, 128)
    lse = got[:, :, :HALF]
    picked = jnp.sum(got[:, :, HALF : 2 * HALF], axis=0).reshape(CAP)
    best = jnp.max(lse, axis=0)
    nll = (best + jnp.log(jnp.sum(jnp.exp(lse - best[None]), axis=0))).reshape(CAP) - picked
    token_nll = jnp.sum(jnp.where(chosen, nll[:, None], 0.0), axis=0)
    my_levels = lax.dynamic_slice_in_dim(levels, seq_index * (tok_rows // BLOCK), tok_rows // BLOCK)
    token_level = jnp.repeat(my_levels, BLOCK)
    return token_nll / (token_level + 1).astype(jnp.float32)


def solution(mesh):
    in_specs = (
        P("seq", "vocab"),
        P("seq", "vocab"),
        P("seq", "vocab"),
        P("seq", "vocab"),
        P("seq", "vocab"),
        P("vocab", None),
        P("seq", None),
        P(),
        P(("seq", "vocab"), None),
        P(),
        P(),
        P(),
    )
    return jax.shard_map(shards, mesh=mesh, in_specs=in_specs, out_specs=P("seq"), check_vma=False)
```

time: 277 us -> 118 us (0.43)
  blocking collectives: 91.5 us -> 0 us
  waiting for transfers between devices: 109 us -> 38 us
  matrix products: 13.6 us -> 30.9 us
  between operations: 13.6 us -> 0.79 us
  starting transfers between devices: 37.3 us -> 27.3 us
  other arithmetic: 3.48 us -> 10.5 us
    all_gather x1 -> x0, waiting for transfers between devices: 59.9 us -> none  [shards(): lax.all_gather(rows_full, 'seq', axis=0, tiled=True)]
    psum x2 -> x0, blocking collectives: 45.6 us -> none  [the longest x1 39.9 us: shards(): lax.psum((local_stats[1] * jnp.exp(local_stats[0] - best), local_stats[2]...]
    pmax x1 -> x0, blocking collectives: 39.2 us -> none  [shards(): best = lax.pmax(local_stats[0], ('seq', 'vocab'))]
    reduce_scatter x1 -> x0, waiting for transfers between devices: 30.5 us -> none  [shards(): lax.psum_scatter(projected.astype(jnp.bfloat16), 'vocab', scatter_dimensi...]
    dot_general x6 -> x26, matrix products: 7.82 us -> 25.9 us  [the longest x18 16.1 us: attend(): lax.dot_general(q_g, keys, (((1,), (1,)), ((), ())), preferred_element_ty...]
    ppermute x7 -> x15, starting transfers between devices: 37.2 us -> 24.4 us  [permute(): return lax.ppermute(block, ('seq', 'vocab'), pairs)]
    ppermute x7 -> x15, waiting for transfers between devices: 18.6 us -> 31 us  [permute(): return lax.ppermute(block, ('seq', 'vocab'), pairs)]
    all_to_all x0 -> x1, waiting for transfers between devices: none -> 6.92 us  [shards(): lax.all_to_all(send, ('seq', 'vocab'), 0, 0, tiled=True)]
  transfers between devices with their start and end apart: 9 -> 16, of which waited for: 9 -> 8; matrix products, arithmetic and copies ran while one was open for 1% -> 35% of each run, Pallas kernels for 0% -> 0%
where the time goes in v1:
time: 118 us; the launch traced here: 117 us
  waiting for transfers between devices  38 us (32%)
  matrix products  30.9 us (26%)
  starting transfers between devices  27.3 us (23%)
  other arithmetic  10.5 us (9%)
  local copies, waits for them, and re-layouts  9.14 us (8%)
    ppermute x15, waiting for transfers between devices, permute(): return lax.ppermute(block, ('seq', 'vocab'), pairs)  31 us
    ppermute x15, starting transfers between devices, permute(): return lax.ppermute(block, ('seq', 'vocab'), pairs)  24.4 us
    dot_general x18, matrix products, attend(): lax.dot_general(q_g, keys, (((1,), (1,)), ((), ())), preferred_element_ty...  16.1 us
    dot_general x4, matrix products, shards(): lax.dot_general(stackx[k].reshape(n_rows, share), w_k, (((1,), (1,)), (()...  7.72 us
    all_to_all x1, waiting for transfers between devices, shards(): lax.all_to_all(send, ('seq', 'vocab'), 0, 0, tiled=True)  6.92 us
    dot_general x1, matrix products, shards(): jnp.dot(attention, out_weight, preferred_element_type=jnp.float32)  4.95 us
    squeeze x7, local copies, waits for them, and re-layouts, shards(): kv[0][:, cols]  3.56 us
    all_to_all x1, starting transfers between devices, shards(): lax.all_to_all(send, ('seq', 'vocab'), 0, 0, tiled=True)  2.9 us
  transfers between devices with their start and end apart: 16, of which 8 were waited for; matrix products, arithmetic and copies ran while one was open for 35% of the time, Pallas kernels for 0%

profile of v1, /device:TPU:0, one launch (start us, length us, event | category | flops | bytes accessed | tf_op | source)
XLA Modules:
  0.0 116.5 jit_solution(11058838603805081573)
XLA Ops:
  0.0 1.6 %pad_maximum_fusion.3 = bf16[2,128,256]{2,1,0:T(8,128)(2,1)} fusion(bf16[1,128,256]{2,1,0:T(8,128)(2,1)} %bitcast.73, bf16[1,128,256]{2,1,0:T(8,128)(2,1)} %bitcast.77), kind=kLoop, calls=%fused_computation.77 | loop fusion | flops 65536 | bytes 262144 | tf_op jit(solution)/shard_map/stack | solution.py:82
  1.6 3.0 %collective-permute-start = (bf16[2,128,256]{2,1,0:T(8,128)(2,1)}, bf16[2,128,256]{2,1,0:T(8,128)(2,1)}, u32[]{:S(2)}, u32[]{:S(2)}) collective-permute-start(bf16[2,128,256]{2,1,0:T(8,128)(2,1)} %pad_maximum_fusion.3), channel_id=1, source_target_pairs={{0,4},{1,5},{2,6},{3,7},{4,0},{5,1},{6,2},{7,3},{8,12},{9,13},{10,... | collective-permute-start | bytes 393224 | tf_op jit(solution)/shard_map/ppermute | solution.py:54
  4.6 4.1 %collective-permute-start.1 = (bf16[2,128,256]{2,1,0:T(8,128)(2,1)}, bf16[2,128,256]{2,1,0:T(8,128)(2,1)}, u32[]{:S(2)}, u32[]{:S(2)}) collective-permute-start(bf16[2,128,256]{2,1,0:T(8,128)(2,1)} %pad_maximum_fusion.3), channel_id=1, source_target_pairs={{0,8},{1,9},{2,10},{3,11},{4,12},{5,13},{6,14},{7,15},{8,16},{9,17... | collective-permute-start | bytes 393224 | tf_op jit(solution)/shard_map/ppermute | solution.py:54
  8.8 4.5 %collective-permute-start.3 = (bf16[2,128,256]{2,1,0:T(8,128)(2,1)}, bf16[2,128,256]{2,1,0:T(8,128)(2,1)}, u32[]{:S(2)}, u32[]{:S(2)}) collective-permute-start(bf16[2,128,256]{2,1,0:T(8,128)(2,1)} %pad_maximum_fusion.3), channel_id=1, source_target_pairs={{0,16},{1,17},{2,18},{3,19},{4,20},{5,21},{6,22},{7,23},{8,24},{9,... | collective-permute-start | bytes 393224 | tf_op jit(solution)/shard_map/ppermute | solution.py:54
  13.3 1.9 %collective-permute-start.5 = (bf16[2,128,256]{2,1,0:T(8,128)(2,1)}, bf16[2,128,256]{2,1,0:T(8,128)(2,1)}, u32[]{:S(2)}, u32[]{:S(2)}) collective-permute-start(bf16[2,128,256]{2,1,0:T(8,128)(2,1)} %pad_maximum_fusion.3), channel_id=1, source_target_pairs={{0,24},{1,25},{2,26},{3,27},{4,28},{5,29},{6,30},{7,31}} | collective-permute-start | bytes 393224 | tf_op jit(solution)/shard_map/ppermute | solution.py:54
  17.1 1.1 convolution_convert_fusion
  22.8 1.6 %fusion.81 = (f32[192]{0:T(256)}, f32[192,1152]{1,0:T(8,128)S(1)}) fusion(bf16[128,256]{1,0:T(8,128)(2,1)} %param.15, bf16[48,128]{1,0:T(8,128)(2,1)S(1)} %get-tuple-element.54, bf16[48,128]{1,0:T(8,128)(2,1)S(1)} %get-tuple-element.55, bf16[48,128]{1,0:T(8,128)(2,1)S(1)} %get-tuple-element.56, bf16[48,128]{1,0:T(8,128)(2,1)S(1)} %get-tuple-element.53, ...), kind=kOutput, calls=%fused_computation.214 | convolution fusion | flops 6586175 | bytes 182272 | tf_op jit(solution)/shard_map/dot_general | solution.py:116
  24.4 1.6 %fusion.80 = (f32[192]{0:T(256)}, f32[192,1152]{1,0:T(8,128)S(1)}) fusion(f32[192,1152]{1,0:T(8,128)S(1)} %get-tuple-element.38, bf16[128,256]{1,0:T(8,128)(2,1)} %param.13, bf16[48,128]{1,0:T(8,128)(2,1)S(1)} %get-tuple-element.54, bf16[48,128]{1,0:T(8,128)(2,1)S(1)} %get-tuple-element.55, bf16[48,128]{1,0:T(8,128)(2,1)S(1)} %get-tuple-element.56, ...), kind=kOutput, calls=%fused_computation.213 | convolution fusion | flops 6586176 | bytes 182528 | tf_op jit(solution)/shard_map/dot_general | solution.py:116
  26.1 1.7 %fusion.91 = (f32[192]{0:T(256)}, f32[192,1152]{1,0:T(8,128)S(1)}) fusion(bf16[128,256]{1,0:T(8,128)(2,1)} %param.15, bf16[48,128]{1,0:T(8,128)(2,1)} %get-tuple-element.57, bf16[48,128]{1,0:T(8,128)(2,1)} %get-tuple-element.58, bf16[48,128]{1,0:T(8,128)(2,1)} %get-tuple-element.59, bf16[48,128]{1,0:T(8,128)(2,1)} %get-tuple-element.60, ...), kind=kOutput, calls=%fused_computation.224 | convolution fusion | flops 6586175 | bytes 182528 | tf_op jit(solution)/shard_map/dot_general | solution.py:116
  27.7 1.6 %fusion.90 = (f32[192]{0:T(256)}, f32[192,1152]{1,0:T(8,128)S(1)}) fusion(f32[192,1152]{1,0:T(8,128)S(1)} %get-tuple-element.64, bf16[128,256]{1,0:T(8,128)(2,1)S(1)} %copy-done.2, bf16[48,128]{1,0:T(8,128)(2,1)} %get-tuple-element.57, bf16[48,128]{1,0:T(8,128)(2,1)} %get-tuple-element.58, bf16[48,128]{1,0:T(8,128)(2,1)} %get-tuple-element.59, ...), kind=kOutput, calls=%fused_computation.223 | convolution fusion | flops 6586176 | bytes 182272 | tf_op jit(solution)/shard_map/dot_general | solution.py:116
  31.4 1.0 fusion.82
  32.4 1.0 fusion.92
  34.4 1.0 fusion.83
  37.9 1.6 %collective-permute-start.4 = (bf16[2,128,256]{2,1,0:T(8,128)(2,1)}, bf16[2,128,256]{2,1,0:T(8,128)(2,1)S(1)}, u32[]{:S(2)}, u32[]{:S(2)}) collective-permute-start(bf16[2,128,256]{2,1,0:T(8,128)(2,1)} %collective-permute-done.3), channel_id=1, source_target_pairs={{0,4},{1,5},{2,6},{3,7},{4,0},{5,1},{6,2},{7,3},{8,12},{9,13},{10,... | collective-permute-start | bytes 393224 | tf_op jit(solution)/shard_map/ppermute | solution.py:54
  41.0 1.1 collective-permute-done.2
  43.0 1.0 fusion.94
  49.3 5.0 %fusion.101 = f32[48,4096]{1,0:T(8,128)S(1)} fusion(bf16[48,1024]{1,0:T(8,128)(2,1)S(1)} %constant_dynamic-update-slice_fusion.36, bf16[1024,4096]{1,0:T(8,128)(2,1)} %param.17), kind=kOutput, calls=%fused_computation.234 | convolution fusion | flops 402653184 | bytes 9273344 | tf_op jit(solution)/shard_map/dot_general | solution.py:133
  54.5 1.3 %collective-permute-done.7 = bf16[24,4096]{1,0:T(8,128)(2,1)S(1)} collective-permute-done((bf16[24,4096]{1,0:T(8,128)(2,1)S(1)}, bf16[24,4096]{1,0:T(8,128)(2,1)S(1)}, u32[]{:S(2)}, u32[]{:S(2)}) %collective-permute-start.7) | collective-permute-done | bytes 196640 | tf_op jit(solution)/shard_map/ppermute | solution.py:54
  55.8 1.6 %collective-permute-start.8 = (bf16[24,4096]{1,0:T(8,128)(2,1)S(1)}, bf16[24,4096]{1,0:T(8,128)(2,1)S(1)}, u32[]{:S(2)}, u32[]{:S(2)}) collective-permute-start(bf16[24,4096]{1,0:T(8,128)(2,1)S(1)} %add_convert_fusion), channel_id=1, source_target_pairs={{0,2},{1,3},{2,0},{3,1},{4,6},{5,7},{6,4},{7,5},{8,10},{9,11},{10,... | collective-permute-start | bytes 589832 | tf_op jit(solution)/shard_map/ppermute | solution.py:54
  57.7 5.1 %collective-permute-done.8 = bf16[24,4096]{1,0:T(8,128)(2,1)S(1)} collective-permute-done((bf16[24,4096]{1,0:T(8,128)(2,1)S(1)}, bf16[24,4096]{1,0:T(8,128)(2,1)S(1)}, u32[]{:S(2)}, u32[]{:S(2)}) %collective-permute-start.8) | collective-permute-done | bytes 196640 | tf_op jit(solution)/shard_map/ppermute | solution.py:54
  63.3 3.7 %collective-permute-start.11 = (bf16[24,2048]{1,0:T(8,128)(2,1)S(1)}, bf16[24,2048]{1,0:T(8,128)(2,1)S(1)}, u32[]{:S(2)}, u32[]{:S(2)}) collective-permute-start(bf16[24,2048]{1,0:T(8,128)(2,1)S(1)} %fusion.43), channel_id=1, source_target_pairs={{0,24},{1,25},{2,26},{3,27},{4,28},{5,29},{6,30},{7,31},{8,0},{9,1... | collective-permute-start | bytes 294920 | tf_op jit(solution)/shard_map/ppermute | solution.py:54
  67.1 3.5 %collective-permute-done.9 = bf16[24,2048]{1,0:T(8,128)(2,1)S(1)} collective-permute-done((bf16[24,2048]{1,0:T(8,128)(2,1)S(1)}, bf16[24,2048]{1,0:T(8,128)(2,1)S(1)}, u32[]{:S(2)}, u32[]{:S(2)}) %collective-permute-start.9) | collective-permute-done | bytes 98336 | tf_op jit(solution)/shard_map/ppermute | solution.py:54
  70.7 2.6 %collective-permute-done.10 = bf16[24,2048]{1,0:T(8,128)(2,1)S(1)} collective-permute-done((bf16[24,2048]{1,0:T(8,128)(2,1)S(1)}, bf16[24,2048]{1,0:T(8,128)(2,1)S(1)}, u32[]{:S(2)}, u32[]{:S(2)}) %collective-permute-start.10) | collective-permute-done | bytes 98336 | tf_op jit(solution)/shard_map/ppermute | solution.py:54
  73.4 1.6 %collective-permute-start.12 = (bf16[4,24,2048]{2,1,0:T(8,128)(2,1)S(1)}, bf16[4,24,2048]{2,1,0:T(8,128)(2,1)S(1)}, u32[]{:S(2)}, u32[]{:S(2)}) collective-permute-start(bf16[4,24,2048]{2,1,0:T(8,128)(2,1)S(1)} %get-tuple-element.20), channel_id=1, source_target_pairs={{0,2},{1,5},{2,0},{3,7},{4,6},{5,1},{6,4},{7,3},{8,10},{9,13},{10,... | collective-permute-start | bytes 1179656 | tf_op jit(solution)/shard_map/ppermute | solution.py:54
  74.9 6.8 %collective-permute-done.12 = bf16[4,24,2048]{2,1,0:T(8,128)(2,1)S(1)} collective-permute-done((bf16[4,24,2048]{2,1,0:T(8,128)(2,1)S(1)}, bf16[4,24,2048]{2,1,0:T(8,128)(2,1)S(1)}, u32[]{:S(2)}, u32[]{:S(2)}) %collective-permute-start.12) | collective-permute-done | bytes 393248 | tf_op jit(solution)/shard_map/ppermute | solution.py:54
  83.5 10.5 %collective-permute-done.13 = bf16[2,4,24,2048]{3,2,1,0:T(8,128)(2,1)} collective-permute-done((bf16[2,4,24,2048]{3,2,1,0:T(8,128)(2,1)S(1)}, bf16[2,4,24,2048]{3,2,1,0:T(8,128)(2,1)}, u32[]{:S(2)}, u32[]{:S(2)}) %collective-permute-start.13) | collective-permute-done | bytes 786464 | tf_op jit(solution)/shard_map/ppermute | solution.py:54
  94.0 1.4 %pad_maximum_fusion = bf16[2,2,4,24,2048]{4,3,2,1,0:T(8,128)(2,1)S(1)} fusion(bf16[1,2,4,24,2048]{4,3,2,1,0:T(8,128)(2,1)} %bitcast.26, bf16[1,2,4,24,2048]{4,3,2,1,0:T(8,128)(2,1)S(1)} %get-tuple-element.17), kind=kLoop, calls=%fused_computation.8 | loop fusion | flops 786432 | bytes 3145728 | tf_op jit(solution)/shard_map/stack | solution.py:153
  97.4 1.2 %fusion.99 = (f32[192]{0:T(256)S(1)}, f32[192,592]{1,0:T(8,128)S(1)}) fusion(f32[192,592]{1,0:T(8,128)S(1)} %fusion.4, bf16[192,2048]{1,0:T(8,128)(2,1)S(1)} %bitcast.64, bf16[592,4096]{1,0:T(8,128)(2,1)S(1)} %bitcast.69, s32[]{:T(128)S(6)} %select_n.255), kind=kOutput, calls=%fused_computation.232 | convolution fusion | flops 465794880 | bytes 4158212 | tf_op jit(solution)/shard_map/dot_general | solution.py:167
  98.6 2.7 %fusion = f32[192,592]{1,0:T(8,128)S(1)} fusion(bf16[192,2048]{1,0:T(8,128)(2,1)S(1)} %bitcast.67, bf16[592,4096]{1,0:T(8,128)(2,1)} %collective-permute-done.14, s32[]{:T(128)S(6)} %select_n.257), kind=kOutput, calls=%fused_computation | convolution fusion | flops 465567744 | bytes 3665924 | tf_op jit(solution)/shard_map/dot_general | solution.py:167
  101.3 2.8 %fusion.100 = (f32[192]{0:T(256)S(1)}, f32[192,592]{1,0:T(8,128)S(1)}) fusion(f32[192,592]{1,0:T(8,128)S(1)} %fusion, bf16[192,2048]{1,0:T(8,128)(2,1)S(1)} %bitcast.65, bf16[592,4096]{1,0:T(8,128)(2,1)} %collective-permute-done.14, s32[]{:T(128)S(6)} %select_n.255), kind=kOutput, calls=%fused_computation.233 | convolution fusion | flops 465794880 | bytes 4121348 | tf_op jit(solution)/shard_map/dot_general | solution.py:167
  105.6 2.9 %all-to-all-start = ((f32[32,1,128]{2,1,0:T(1,128)}), f32[32,1,128]{2,1,0:T(1,128)S(1)}, u32[]{:S(2)}, u32[]{:S(2)}) async-start(f32[32,1,128]{2,1,0:T(1,128)} %bitcast.32), calls=%async_computation | async-start | bytes 32768 | tf_op jit(solution)/shard_map/all_to_all | solution.py:192
  108.8 6.9 %all-to-all-done = f32[32,1,128]{2,1,0:T(1,128)S(1)} async-done(((f32[32,1,128]{2,1,0:T(1,128)}), f32[32,1,128]{2,1,0:T(1,128)S(1)}, u32[]{:S(2)}, u32[]{:S(2)}) %all-to-all-start) | async-done | bytes 16416 | tf_op jit(solution)/shard_map/all_to_all | solution.py:192
  (181 shorter events, 26.4 us)
Async XLA Ops:
  0.0 57.4 %copy-start = (bf16[128,4096]{1,0:T(8,128)(2,1)S(1)}, bf16[128,4096]{1,0:T(8,128)(2,1)}, u32[]{:S(2)}) copy-start(bf16[128,4096]{1,0:T(8,128)(2,1)} %param.18) | copy-start | bytes 3145732
  0.0 27.7 %copy-start.2 = (bf16[128,256]{1,0:T(8,128)(2,1)S(1)}, bf16[128,256]{1,0:T(8,128)(2,1)}, u32[]{:S(2)}) copy-start(bf16[128,256]{1,0:T(8,128)(2,1)} %param.13) | copy-start | bytes 196612
  0.0 29.4 %copy-start.1 = (bf16[128,256]{1,0:T(8,128)(2,1)S(1)}, bf16[128,256]{1,0:T(8,128)(2,1)}, u32[]{:S(2)}) copy-start(bf16[128,256]{1,0:T(8,128)(2,1)} %param.14) | copy-start | bytes 196612
  0.0 29.5 %copy-start.3 = (s32[1024]{0:T(1024)S(1)}, s32[1024]{0:T(1024)}, u32[]{:S(2)}) copy-start(s32[1024]{0:T(1024)} %param.22) | copy-start | bytes 12292
  1.6 28.8 %collective-permute-start = (bf16[2,128,256]{2,1,0:T(8,128)(2,1)}, bf16[2,128,256]{2,1,0:T(8,128)(2,1)}, u32[]{:S(2)}, u32[]{:S(2)}) collective-permute-start(bf16[2,128,256]{2,1,0:T(8,128)(2,1)} %pad_maximum_fusion.3), channel_id=1, source_target_pairs={{0,4},{1,5},{2,6},{3,7},{4,0},{5,1},{6,2},{7,3},{8,12},{9,13},{10,... | collective-permute-start | bytes 393224 | tf_op jit(solution)/shard_map/ppermute | solution.py:54
  4.6 28.8 %collective-permute-start.1 = (bf16[2,128,256]{2,1,0:T(8,128)(2,1)}, bf16[2,128,256]{2,1,0:T(8,128)(2,1)}, u32[]{:S(2)}, u32[]{:S(2)}) collective-permute-start(bf16[2,128,256]{2,1,0:T(8,128)(2,1)} %pad_maximum_fusion.3), channel_id=1, source_target_pairs={{0,8},{1,9},{2,10},{3,11},{4,12},{5,13},{6,14},{7,15},{8,16},{9,17... | collective-permute-start | bytes 393224 | tf_op jit(solution)/shard_map/ppermute | solution.py:54
  8.8 28.2 %collective-permute-start.3 = (bf16[2,128,256]{2,1,0:T(8,128)(2,1)}, bf16[2,128,256]{2,1,0:T(8,128)(2,1)}, u32[]{:S(2)}, u32[]{:S(2)}) collective-permute-start(bf16[2,128,256]{2,1,0:T(8,128)(2,1)} %pad_maximum_fusion.3), channel_id=1, source_target_pairs={{0,16},{1,17},{2,18},{3,19},{4,20},{5,21},{6,22},{7,23},{8,24},{9,... | collective-permute-start | bytes 393224 | tf_op jit(solution)/shard_map/ppermute | solution.py:54
  13.3 26.2 %collective-permute-start.5 = (bf16[2,128,256]{2,1,0:T(8,128)(2,1)}, bf16[2,128,256]{2,1,0:T(8,128)(2,1)}, u32[]{:S(2)}, u32[]{:S(2)}) collective-permute-start(bf16[2,128,256]{2,1,0:T(8,128)(2,1)} %pad_maximum_fusion.3), channel_id=1, source_target_pairs={{0,24},{1,25},{2,26},{3,27},{4,28},{5,29},{6,30},{7,31}} | collective-permute-start | bytes 393224 | tf_op jit(solution)/shard_map/ppermute | solution.py:54
  15.2 83.4 %collective-permute-start.14 = (bf16[592,4096]{1,0:T(8,128)(2,1)}, bf16[592,4096]{1,0:T(8,128)(2,1)}, u32[]{:S(2)}, u32[]{:S(2)}) collective-permute-start(bf16[592,4096]{1,0:T(8,128)(2,1)} %param.20), channel_id=1, source_target_pairs={{0,1},{1,0},{2,3},{3,2},{4,5},{5,4},{6,7},{7,6},{8,9},{9,8},{10,11... | collective-permute-start | bytes 14549000 | tf_op jit(solution)/shard_map/ppermute | solution.py:54
  29.4 12.7 %copy-start.9 = (bf16[48,128]{1,0:T(8,128)(2,1)S(1)}, bf16[48,128]{1,0:T(8,128)(2,1)}, u32[]{:S(2)}) copy-start(bf16[48,128]{1,0:T(8,128)(2,1)} %copy-done.8) | copy-start | bytes 36868
  29.4 12.7 %copy-start.11 = (bf16[48,128]{1,0:T(8,128)(2,1)S(1)}, bf16[48,128]{1,0:T(8,128)(2,1)}, u32[]{:S(2)}) copy-start(bf16[48,128]{1,0:T(8,128)(2,1)} %copy-done.10) | copy-start | bytes 36868
  29.4 12.7 %copy-start.13 = (bf16[48,128]{1,0:T(8,128)(2,1)S(1)}, bf16[48,128]{1,0:T(8,128)(2,1)}, u32[]{:S(2)}) copy-start(bf16[48,128]{1,0:T(8,128)(2,1)} %copy-done.12) | copy-start | bytes 36868
  29.4 12.7 %copy-start.15 = (bf16[48,128]{1,0:T(8,128)(2,1)S(1)}, bf16[48,128]{1,0:T(8,128)(2,1)}, u32[]{:S(2)}) copy-start(bf16[48,128]{1,0:T(8,128)(2,1)} %copy-done.14) | copy-start | bytes 36868
  29.4 12.7 %copy-start.20 = (s32[192]{0:T(256)S(1)}, s32[192]{0:T(256)}, u32[]{:S(2)}) copy-start(s32[192]{0:T(256)} %copy-done.19) | copy-start | bytes 2308
  29.4 16.6 %copy-start.27 = (s32[128]{0:T(128)S(1)}, s32[128]{0:T(128)}, u32[]{:S(2)}) copy-start(s32[128]{0:T(128)} %broadcast_add_fusion.4) | copy-start | bytes 1540
  31.4 15.0 %copy-start.4 = (bf16[48,128]{1,0:T(8,128)(2,1)S(1)}, bf16[48,128]{1,0:T(8,128)(2,1)}, u32[]{:S(2)}) copy-start(bf16[48,128]{1,0:T(8,128)(2,1)} %get-tuple-element.57) | copy-start | bytes 36868
  31.4 15.0 %copy-start.5 = (bf16[48,128]{1,0:T(8,128)(2,1)S(1)}, bf16[48,128]{1,0:T(8,128)(2,1)}, u32[]{:S(2)}) copy-start(bf16[48,128]{1,0:T(8,128)(2,1)} %get-tuple-element.58) | copy-start | bytes 36868
  31.4 15.0 %copy-start.6 = (bf16[48,128]{1,0:T(8,128)(2,1)S(1)}, bf16[48,128]{1,0:T(8,128)(2,1)}, u32[]{:S(2)}) copy-start(bf16[48,128]{1,0:T(8,128)(2,1)} %get-tuple-element.59) | copy-start | bytes 36868
  31.4 15.0 %copy-start.7 = (bf16[48,128]{1,0:T(8,128)(2,1)S(1)}, bf16[48,128]{1,0:T(8,128)(2,1)}, u32[]{:S(2)}) copy-start(bf16[48,128]{1,0:T(8,128)(2,1)} %get-tuple-element.60) | copy-start | bytes 36868
  35.4 6.6 %collective-permute-start.2 = (bf16[2,128,256]{2,1,0:T(8,128)(2,1)}, bf16[2,128,256]{2,1,0:T(8,128)(2,1)S(1)}, u32[]{:S(2)}, u32[]{:S(2)}) collective-permute-start(bf16[2,128,256]{2,1,0:T(8,128)(2,1)} %collective-permute-done.1), channel_id=1, source_target_pairs={{0,4},{1,5},{2,6},{3,7},{4,0},{5,1},{6,2},{7,3},{8,12},{9,13},{10,... | collective-permute-start | bytes 393224 | tf_op jit(solution)/shard_map/ppermute | solution.py:54
  37.9 8.1 %collective-permute-start.4 = (bf16[2,128,256]{2,1,0:T(8,128)(2,1)}, bf16[2,128,256]{2,1,0:T(8,128)(2,1)S(1)}, u32[]{:S(2)}, u32[]{:S(2)}) collective-permute-start(bf16[2,128,256]{2,1,0:T(8,128)(2,1)} %collective-permute-done.3), channel_id=1, source_target_pairs={{0,4},{1,5},{2,6},{3,7},{4,0},{5,1},{6,2},{7,3},{8,12},{9,13},{10,... | collective-permute-start | bytes 393224 | tf_op jit(solution)/shard_map/ppermute | solution.py:54
  40.4 6.8 %collective-permute-start.6 = (bf16[2,128,256]{2,1,0:T(8,128)(2,1)}, bf16[2,128,256]{2,1,0:T(8,128)(2,1)S(1)}, u32[]{:S(2)}, u32[]{:S(2)}) collective-permute-start(bf16[2,128,256]{2,1,0:T(8,128)(2,1)} %collective-permute-done.5), channel_id=1, source_target_pairs={{0,4},{1,5},{2,6},{3,7},{4,0},{5,1},{6,2},{7,3},{8,12},{9,13},{10,... | collective-permute-start | bytes 393224 | tf_op jit(solution)/shard_map/ppermute | solution.py:54
  54.3 1.5 %collective-permute-start.7 = (bf16[24,4096]{1,0:T(8,128)(2,1)S(1)}, bf16[24,4096]{1,0:T(8,128)(2,1)S(1)}, u32[]{:S(2)}, u32[]{:S(2)}) collective-permute-start(bf16[24,4096]{1,0:T(8,128)(2,1)S(1)} %dynamic-slice_convert_fusion), channel_id=1, source_target_pairs={{0,1},{1,0},{2,3},{3,2},{4,5},{5,4},{6,7},{7,6},{8,9},{9,8},{10,11... | collective-permute-start | bytes 589832 | tf_op jit(solution)/shard_map/ppermute | solution.py:54
  55.8 7.0 %collective-permute-start.8 = (bf16[24,4096]{1,0:T(8,128)(2,1)S(1)}, bf16[24,4096]{1,0:T(8,128)(2,1)S(1)}, u32[]{:S(2)}, u32[]{:S(2)}) collective-permute-start(bf16[24,4096]{1,0:T(8,128)(2,1)S(1)} %add_convert_fusion), channel_id=1, source_target_pairs={{0,2},{1,3},{2,0},{3,1},{4,6},{5,7},{6,4},{7,5},{8,10},{9,11},{10,... | collective-permute-start | bytes 589832 | tf_op jit(solution)/shard_map/ppermute | solution.py:54
  57.7 25.3 %copy-start.16 = (s32[1024]{0:T(1024)S(1)}, s32[1024]{0:T(1024)}, u32[]{:S(2)}) copy-start(s32[1024]{0:T(1024)} %param.21) | copy-start | bytes 12292
  63.2 7.5 %collective-permute-start.9 = (bf16[24,2048]{1,0:T(8,128)(2,1)S(1)}, bf16[24,2048]{1,0:T(8,128)(2,1)S(1)}, u32[]{:S(2)}, u32[]{:S(2)}) collective-permute-start(bf16[24,2048]{1,0:T(8,128)(2,1)S(1)} %fusion.43), channel_id=1, source_target_pairs={{0,8},{1,9},{2,10},{3,11},{4,12},{5,13},{6,14},{7,15},{8,16},{9,17... | collective-permute-start | bytes 294920 | tf_op jit(solution)/shard_map/ppermute | solution.py:54
  63.2 10.1 %collective-permute-start.10 = (bf16[24,2048]{1,0:T(8,128)(2,1)S(1)}, bf16[24,2048]{1,0:T(8,128)(2,1)S(1)}, u32[]{:S(2)}, u32[]{:S(2)}) collective-permute-start(bf16[24,2048]{1,0:T(8,128)(2,1)S(1)} %fusion.43), channel_id=1, source_target_pairs={{0,16},{1,17},{2,18},{3,19},{4,20},{5,21},{6,22},{7,23},{8,24},{9,... | collective-permute-start | bytes 294920 | tf_op jit(solution)/shard_map/ppermute | solution.py:54
  63.3 10.0 %collective-permute-start.11 = (bf16[24,2048]{1,0:T(8,128)(2,1)S(1)}, bf16[24,2048]{1,0:T(8,128)(2,1)S(1)}, u32[]{:S(2)}, u32[]{:S(2)}) collective-permute-start(bf16[24,2048]{1,0:T(8,128)(2,1)S(1)} %fusion.43), channel_id=1, source_target_pairs={{0,24},{1,25},{2,26},{3,27},{4,28},{5,29},{6,30},{7,31},{8,0},{9,1... | collective-permute-start | bytes 294920 | tf_op jit(solution)/shard_map/ppermute | solution.py:54
  73.3 22.4 %slice-start = ((s8[4849664]{0:T(1024)(128)(4,1)}), s8[655360]{0:T(1024)(128)(4,1)S(1)}, s32[]{:S(2)}) async-start(s8[4849664]{0:T(1024)(128)(4,1)} %bitcast.68), calls=%async_computation.1 | async-start | bytes 1310720
  73.4 8.3 %collective-permute-start.12 = (bf16[4,24,2048]{2,1,0:T(8,128)(2,1)S(1)}, bf16[4,24,2048]{2,1,0:T(8,128)(2,1)S(1)}, u32[]{:S(2)}, u32[]{:S(2)}) collective-permute-start(bf16[4,24,2048]{2,1,0:T(8,128)(2,1)S(1)} %get-tuple-element.20), channel_id=1, source_target_pairs={{0,2},{1,5},{2,0},{3,7},{4,6},{5,1},{6,4},{7,3},{8,10},{9,13},{10,... | collective-permute-start | bytes 1179656 | tf_op jit(solution)/shard_map/ppermute | solution.py:54
  81.8 12.2 %collective-permute-start.13 = (bf16[2,4,24,2048]{3,2,1,0:T(8,128)(2,1)S(1)}, bf16[2,4,24,2048]{3,2,1,0:T(8,128)(2,1)}, u32[]{:S(2)}, u32[]{:S(2)}) collective-permute-start(bf16[2,4,24,2048]{3,2,1,0:T(8,128)(2,1)S(1)} %get-tuple-element.18), channel_id=1, source_target_pairs={{0,4},{1,3},{2,6},{3,1},{4,0},{5,7},{6,2},{7,5},{8,12},{9,11},{10,... | collective-permute-start | bytes 2359304 | tf_op jit(solution)/shard_map/ppermute | solution.py:54
  105.6 10.1 %all-to-all-start = ((f32[32,1,128]{2,1,0:T(1,128)}), f32[32,1,128]{2,1,0:T(1,128)S(1)}, u32[]{:S(2)}, u32[]{:S(2)}) async-start(f32[32,1,128]{2,1,0:T(1,128)} %bitcast.32), calls=%async_computation | async-start | bytes 32768 | tf_op jit(solution)/shard_map/all_to_all | solution.py:192
  (14 other events, 86.9 us)

commit v2 on v1

v2 whole, which is shorter than its diff:
```python
import functools

import jax
import jax.numpy as jnp
from jax import lax
from jax.experimental import pallas as pl
from jax.experimental.pallas import tpu as pltpu
from jax.sharding import PartitionSpec as P

D = 4096
HEAD_DIM = 128
BLOCK = 32
CAP = 48
LANES = 128
SHIFT = BLOCK.bit_length() - 1

very_low = -1e30
norm_eps = 1e-06

VMEM = pl.BlockSpec(memory_space=pltpu.VMEM)
SMEM = pl.BlockSpec(memory_space=pltpu.SMEM)
NT = (((1,), (1,)), ((), ()))


def call(kernel, name, outs, n_smem, args, mib, flops=0, scratch=()):
    n_bytes = sum(a.size * a.dtype.itemsize for a in args)
    return pl.pallas_call(
        kernel,
        out_shape=outs,
        in_specs=[SMEM] * n_smem + [VMEM] * (len(args) - n_smem),
        out_specs=jax.tree.map(lambda _: VMEM, outs),
        scratch_shapes=list(scratch),
        compiler_params=pltpu.CompilerParams(vmem_limit_bytes=mib << 20),
        cost_estimate=pl.CostEstimate(flops=flops, bytes_accessed=n_bytes, transcendentals=0),
        name=name,
    )(*args)


def select_kernel(where_ref, mask_ref, q_ref, res_ref, q_out, res_out, blk_out):
    tok = mask_ref.shape[1]
    before = lax.broadcasted_iota(jnp.int32, (tok, tok), 0) <= lax.broadcasted_iota(jnp.int32, (tok, tok), 1)
    upto = before.astype(jnp.float32)
    slots = lax.broadcasted_iota(jnp.int32, (CAP, tok), 0).astype(jnp.float32)
    block = lax.shift_right_logical(lax.broadcasted_iota(jnp.int32, (CAP, tok), 1), SHIFT).astype(jnp.float32)
    for which in range(2):
        row = mask_ref[pl.ds(where_ref[which], 1), :].astype(jnp.float32)
        count = jnp.dot(jnp.broadcast_to(row, (8, tok)), upto, preferred_element_type=jnp.float32)[0:1]
        chosen = ((count - 1.0) == slots) & (row == 1.0)
        pick = jnp.where(chosen, 1.0, 0.0)
        blk_out[which] = jnp.broadcast_to(jnp.sum(pick * block, axis=1, keepdims=True), (CAP, LANES))
        if which == 0:
            pick = pick.astype(jnp.bfloat16)
            q_out[...] = jnp.dot(pick, q_ref[...], preferred_element_type=jnp.float32).astype(jnp.bfloat16)
            res_out[...] = jnp.dot(pick, res_ref[...], preferred_element_type=jnp.float32).astype(jnp.bfloat16)


def split3(value):
    high = value.astype(jnp.bfloat16).astype(jnp.float32)
    rest = value - high
    mid = rest.astype(jnp.bfloat16).astype(jnp.float32)
    return high, mid, rest - mid


def attend_kernel(n_pieces, heads, kv_heads, where_ref, blk_ref, q_own, q_other, kn_ref, vn_ref, *refs):
    pieces, (own_out, own_lse, other_out) = refs[:n_pieces], refs[n_pieces:]
    group = heads // kv_heads
    tok = kn_ref.shape[0]
    per_dev = tok // BLOCK
    scale = HEAD_DIM ** (-0.5)
    lane = lax.broadcasted_iota(jnp.int32, (CAP, LANES), 1)
    key_block = lax.shift_right_logical(lax.broadcasted_iota(jnp.int32, (CAP, tok), 1), SHIFT)
    for which in range(2):
        q_ref = (q_own, q_other)[which]
        slot_block = blk_ref[which][:, :1].astype(jnp.int32)
        row_block = slot_block + where_ref[which] * per_dev
        bias = []
        for k in range(n_pieces):
            seen = (key_block + where_ref[2 + k] * per_dev) < row_block
            bias.append(jnp.concatenate([jnp.where(seen, 0.0, very_low)] * group, axis=0))
        if which == 0:
            bias.append(jnp.concatenate([jnp.where(key_block == slot_block, 0.0, very_low)] * group, axis=0))
        lse_all = jnp.zeros((CAP, LANES), jnp.float32)
        for g in range(kv_heads):
            cols = slice(g * HEAD_DIM, (g + 1) * HEAD_DIM)
            q_g = jnp.concatenate(
                [q_ref[:, (g * group + h) * HEAD_DIM : (g * group + h + 1) * HEAD_DIM] for h in range(group)], axis=0
            )
            keys = [p[0][:, cols] for p in pieces]
            values = [p[1][:, cols] for p in pieces]
            if which == 0:
                keys.append(kn_ref[:, cols])
                values.append(vn_ref[:, cols])
            scores = [
                lax.dot_general(q_g, k, NT, preferred_element_type=jnp.float32) * scale + b for k, b in zip(keys, bias)
            ]
            top = functools.reduce(jnp.maximum, scores)
            top = jnp.max(top, axis=1, keepdims=True)
            weights = [jnp.exp(s - top) for s in scores]
            total = jnp.sum(functools.reduce(jnp.add, weights), axis=1, keepdims=True)
            mixed = functools.reduce(
                jnp.add,
                [jnp.dot(w.astype(jnp.bfloat16), v, preferred_element_type=jnp.float32) for w, v in zip(weights, values)],
            )
            mixed = mixed / total
            lse = top + jnp.log(total)
            for h in range(group):
                head = g * group + h
                rows = slice(h * CAP, (h + 1) * CAP)
                at = slice(head * HEAD_DIM, (head + 1) * HEAD_DIM)
                lse_all = jnp.where(lane == head, lse[rows], lse_all)
                if which == 0:
                    own_out[:, at] = mixed[rows]
                else:
                    other_out[:, at] = mixed[rows].astype(jnp.bfloat16)
        if which == 0:
            own_lse[...] = lse_all
        else:
            high, mid, low = split3(lse_all)
            packed = high + pltpu.roll(mid, 32, 1) + pltpu.roll(low, 64, 1)
            other_out[:, heads * HEAD_DIM :] = packed.astype(jnp.bfloat16)


def project_kernel(heads, where_ref, own_ref, lse_ref, got_ref, w_ref, mine_out, theirs_out):
    half = CAP // 2
    packed = got_ref[:, heads * HEAD_DIM :].astype(jnp.float32)
    got_lse = packed + pltpu.roll(packed, LANES - 32, 1) + pltpu.roll(packed, LANES - 64, 1)
    own_lse = lse_ref[...]
    top = jnp.maximum(own_lse, got_lse)
    w_own, w_got = jnp.exp(own_lse - top), jnp.exp(got_lse - top)
    total = w_own + w_got
    w_own, w_got = w_own / total, w_got / total
    parts = []
    for h in range(heads):
        at = slice(h * HEAD_DIM, (h + 1) * HEAD_DIM)
        joined = own_ref[:, at] * w_own[:, h : h + 1] + got_ref[:, at].astype(jnp.float32) * w_got[:, h : h + 1]
        parts.append(joined.astype(jnp.bfloat16))
    attention = jnp.concatenate(parts, axis=1)
    first = where_ref[0] == 0
    width = w_ref.shape[1]
    step = min(1024, width)
    for j in range(0, width, step):
        out = jnp.dot(attention, w_ref[:, j : j + step], preferred_element_type=jnp.float32)
        upper, lower = out[:half], out[half:]
        mine_out[:, j : j + step] = jnp.where(first, upper, lower)
        theirs_out[:, j : j + step] = jnp.where(first, lower, upper).astype(jnp.bfloat16)


def logits_kernel(mixed, X, Y, Z, V, where_ref, target_ref, *refs):
    half = CAP // 2
    share = refs[0].shape[1]
    n_rows = Y * Z * half
    quarter = Z * half
    if mixed:
        column, step1, step2, w_own, w_other, out_ref, near, far = refs

        @pl.when(where_ref[1] == 0)
        def _():
            near[quarter:] = step2[:quarter]
            far[:quarter] = step1[...]

        @pl.when(where_ref[1] != 0)
        def _():
            near[quarter:] = step1[...]
            far[:quarter] = step2[:quarter]

        near[:quarter] = column[...]
        far[quarter:] = step2[quarter:]
        rows = [near, far]
    else:
        rows = refs[:X]
        w_own, w_other, out_ref = refs[X:]
    logits = []
    for w in (w_own, w_other):
        total = None
        for k in range(X):
            at = pl.multiple_of(lax.rem(where_ref[0] + (X - k), X) * share, LANES)
            part = lax.dot_general(w[:, pl.ds(at, share)], rows[k][...], NT, preferred_element_type=jnp.float32)
            total = part if total is None else total + part
        logits.append(total)
    top = jnp.maximum(jnp.max(logits[0], axis=0, keepdims=True), jnp.max(logits[1], axis=0, keepdims=True))
    summed = 0.0
    picked = 0.0
    for i, lg in enumerate(logits):
        ids = lax.broadcasted_iota(jnp.int32, lg.shape, 0) + where_ref[2 + i]
        summed = summed + jnp.sum(jnp.exp(lg - top), axis=0, keepdims=True)
        picked = picked + jnp.sum(jnp.where(ids == target_ref[...], lg, 0.0), axis=0, keepdims=True)
    lse = top + jnp.log(summed)
    wide = -(-n_rows // LANES) * LANES
    pad = [jnp.zeros((1, wide - n_rows), jnp.float32)] if wide > n_rows else []
    lse = jnp.broadcast_to(jnp.concatenate([lse, *pad], axis=1), (8, wide))
    picked = jnp.broadcast_to(jnp.concatenate([picked, *pad], axis=1), (8, wide))
    lane = lax.broadcasted_iota(jnp.int32, (8, LANES), 1)
    for p in range(Y * Z):
        a = pltpu.roll(lse, (wide - p * half) % wide, 1)[:, :LANES]
        b = pltpu.roll(picked, (wide - p * half + half) % wide, 1)[:, :LANES]
        row = jnp.where(lane < half, a, b)[0:1]
        first = where_ref[4 + p] * V
        for v in range(V):
            out_ref[first + v] = row


def shards(
    q_noised,
    key_clean,
    value_clean,
    key_noised,
    value_noised,
    out_weight,
    residual,
    norm_gain,
    head_weight,
    targets,
    mask_flags,
    levels,
):
    tok_rows, q_width = q_noised.shape
    width = residual.shape[1]
    heads_local = q_width // HEAD_DIM
    kv_local = key_clean.shape[1] // HEAD_DIM
    vocab_rows = head_weight.shape[0]
    S = lax.axis_size("seq")
    V = lax.axis_size("vocab")
    C = 2
    X = V // C
    Y = 2
    Z = S // Y
    HALF = CAP // C
    share = width // X
    seq_index = lax.axis_index("seq")
    vocab_index = lax.axis_index("vocab")
    z, y = seq_index // Y, seq_index % Y
    x, c = vocab_index // C, vocab_index % C
    first_row = seq_index * tok_rows

    def dev(zi, yi, xi, ci):
        return ((zi * Y + yi) * X + xi) * C + ci

    def permute(block, pairs):
        return lax.ppermute(block, ("seq", "vocab"), pairs)

    every = [(zi, yi, xi, ci) for zi in range(Z) for yi in range(Y) for xi in range(X) for ci in range(C)]

    def core_flip(block):
        return permute(block, [(dev(a, b, e, f), dev(a, b, e, 1 - f)) for a, b, e, f in every])

    def x_shift(block, k):
        return permute(block, [(dev(a, b, e, f), dev(a, b, (e + k) % X, f)) for a, b, e, f in every])

    def y_flip(block):
        return permute(block, [(dev(a, b, e, f), dev(a, 1 - b, e, f)) for a, b, e, f in every])

    def z_up(block, k):
        return permute(block, [(dev(a, b, e, f), dev(a + k, b, e, f)) for a, b, e, f in every if a + k < Z])

    def z_shift(block, k):
        return permute(block, [(dev(a, b, e, f), dev((a + k) % Z, b, e, f)) for a, b, e, f in every])

    def mixed_flip(block, first):
        pairs = []
        for a, b, e, f in every:
            if (f == 0) == first:
                pairs.append((dev(a, b, e, f), dev(a, b, 1 - e, f)))
            else:
                pairs.append((dev(a, b, e, f), dev(a, 1 - b, e, f)))
        return permute(block, pairs)

    def scalars(*values):
        return jnp.stack([jnp.asarray(v, jnp.int32) for v in values])

    own_kv = jnp.stack([key_clean, value_clean])
    pieces, sources = [own_kv], [seq_index]
    for k in range(1, Z):
        pieces.append(z_up(own_kv, k))
        sources.append(jnp.where(z >= k, (z - k) * Y + y, S))
    partner = z * Y + 1 - y
    all_mask = mask_flags.reshape(S, tok_rows)
    queries, residual_sel, slot_blocks = call(
        select_kernel,
        "select_rows",
        (
            jax.ShapeDtypeStruct((CAP, q_width), jnp.bfloat16),
            jax.ShapeDtypeStruct((CAP, width), jnp.bfloat16),
            jax.ShapeDtypeStruct((2, CAP, LANES), jnp.float32),
        ),
        1,
        (scalars(seq_index, partner), all_mask, q_noised, residual),
        8,
    )
    other_queries = y_flip(queries)
    other_head = core_flip(head_weight)
    own_sum, own_lse, other_sum = call(
        functools.partial(attend_kernel, Z, heads_local, kv_local),
        "attend",
        (
            jax.ShapeDtypeStruct((CAP, q_width), jnp.float32),
            jax.ShapeDtypeStruct((CAP, LANES), jnp.float32),
            jax.ShapeDtypeStruct((CAP, q_width + LANES), jnp.bfloat16),
        ),
        1,
        (scalars(seq_index, partner, *sources), slot_blocks, queries, other_queries, key_noised, value_noised, *pieces),
        16,
    )
    got_sum = y_flip(other_sum)
    mine, theirs = call(
        functools.partial(project_kernel, heads_local),
        "project",
        (jax.ShapeDtypeStruct((HALF, width), jnp.float32), jax.ShapeDtypeStruct((HALF, width), jnp.bfloat16)),
        1,
        (scalars(c), own_sum, own_lse, got_sum, out_weight),
        16,
    )

    all_slot = jnp.cumsum(all_mask, axis=1) - 1
    slot_hit = (all_mask[:, None, :] == 1) & (all_slot[:, None, :] == jnp.arange(CAP)[None, :, None])
    slot_targets = jnp.sum(jnp.where(slot_hit, targets.reshape(S, 1, tok_rows), 0), axis=2)
    my_mask = lax.dynamic_slice_in_dim(mask_flags, first_row, tok_rows)
    my_slot = jnp.cumsum(my_mask) - 1
    chosen = (my_mask[None, :] == 1) & (my_slot[None, :] == jnp.arange(CAP)[:, None])

    mine = mine + core_flip(theirs).astype(jnp.float32)
    sent = mine.astype(jnp.bfloat16)
    summed = mine
    for k in range(1, X):
        summed = summed + x_shift(sent, k).astype(jnp.float32)
    hidden = lax.dynamic_slice_in_dim(residual_sel, c * HALF, HALF).astype(jnp.float32) + summed
    squares = jnp.sum(hidden * hidden, axis=1, keepdims=True)
    normed = (hidden * lax.rsqrt(squares / D + norm_eps) * norm_gain[None, :]).astype(jnp.bfloat16)

    own = lax.dynamic_slice_in_dim(normed, x * share, share, 1)
    slabs = [own] + [z_shift(own, k) for k in range(1, Z)]
    column = jnp.stack(slabs)
    n_rows = Y * Z * HALF
    mixed = X == Y
    if mixed:
        step1 = mixed_flip(column, True)
        step2 = mixed_flip(jnp.stack([column, step1]), False)
        rows = [column.reshape(Z * HALF, share), step1.reshape(Z * HALF, share), step2.reshape(n_rows, share)]
        scratch = [pltpu.VMEM((n_rows, share), jnp.bfloat16)] * 2
    else:
        pair = jnp.stack([column, y_flip(column)])
        rows = [pair.reshape(n_rows, share)] + [x_shift(pair, k).reshape(n_rows, share) for k in range(1, X)]
        scratch = []
    src_z = (z - jnp.arange(Z)) % Z
    src_s = (src_z[None, :] * Y + jnp.stack([y, 1 - y])[:, None]).reshape(Y * Z)
    from_s = src_s[None, :] == jnp.arange(S)[:, None]
    half_targets = lax.dynamic_slice_in_dim(slot_targets, c * HALF, HALF, 1)
    row_targets = jnp.sum(jnp.where(from_s[:, :, None], half_targets[:, None, :], 0), axis=0).reshape(1, n_rows)
    first = (seq_index * V + x * C) * vocab_rows
    send = call(
        functools.partial(logits_kernel, mixed, X, Y, Z, V),
        "logits",
        jax.ShapeDtypeStruct((S * V, 1, LANES), jnp.float32),
        1,
        (
            jnp.concatenate([scalars(x, c, first + c * vocab_rows, first + (1 - c) * vocab_rows), src_s.astype(jnp.int32)]),
            row_targets,
            *rows,
            head_weight,
            other_head,
        ),
        24,
        4 * n_rows * width * vocab_rows,
        scratch,
    ).reshape(S * V, LANES)
    got = lax.all_to_all(send, ("seq", "vocab"), 0, 0, tiled=True).reshape(S * X, C, LANES)
    lse = got[:, :, :HALF]
    picked = jnp.sum(got[:, :, HALF : 2 * HALF], axis=0).reshape(CAP)
    best = jnp.max(lse, axis=0)
    nll = (best + jnp.log(jnp.sum(jnp.exp(lse - best[None]), axis=0))).reshape(CAP) - picked
    token_nll = jnp.sum(jnp.where(chosen, nll[:, None], 0.0), axis=0)
    my_levels = lax.dynamic_slice_in_dim(levels, seq_index * (tok_rows // BLOCK), tok_rows // BLOCK)
    token_level = jnp.repeat(my_levels, BLOCK)
    return token_nll / (token_level + 1).astype(jnp.float32)


def solution(mesh):
    in_specs = (
        P("seq", "vocab"),
        P("seq", "vocab"),
        P("seq", "vocab"),
        P("seq", "vocab"),
        P("seq", "vocab"),
        P("vocab", None),
        P("seq", None),
        P(),
        P(("seq", "vocab"), None),
        P(),
        P(),
        P(),
    )
    return jax.shard_map(shards, mesh=mesh, in_specs=in_specs, out_specs=P("seq"), check_vma=False)
```

time: 118 us -> 94.6 us (0.80)
  matrix products: 30.9 us -> 0 us
  Pallas kernels: 0 us -> 10.8 us
  other arithmetic: 10.5 us -> 3.39 us
  waiting for transfers between devices: 38 us -> 42.4 us
  local copies, waits for them, and re-layouts: 9.14 us -> 11.1 us
  starting transfers between devices: 27.3 us -> 26.1 us
    dot_general x27 -> x0, matrix products: 30.9 us -> none  [the longest x18 16.1 us: attend(): lax.dot_general(q_g, keys, (((1,), (1,)), ((), ())), preferred_element_ty...]
    pallas_call x0 -> x4, Pallas kernels: none -> 10.8 us  [call(): pl.pallas_call(kernel, out_shape=outs, in_specs=[SMEM] * n_smem + [VMEM]...]
    unnamed x75 -> x22, local copies, waits for them, and re-layouts: 1.74 us -> 10.3 us
    ppermute x15 -> x13, waiting for transfers between devices: 31 us -> 35.5 us  [permute(): return lax.ppermute(block, ('seq', 'vocab'), pairs)]
    squeeze x7 -> x0, local copies, waits for them, and re-layouts: 3.56 us -> none  [shards(): kv[0][:, cols]]
    add x12 -> x1, other arithmetic: 2.84 us -> 0.07 us  [shards(): src_s = (src_z[None, :] * Y + jnp.stack([y, 1 - y])[:, None]).reshape(Y * Z)]
    ppermute x15 -> x13, starting transfers between devices: 24.4 us -> 22.6 us  [permute(): return lax.ppermute(block, ('seq', 'vocab'), pairs)]
    another operation x5 -> x4, other arithmetic: 1.85 us -> 0.39 us  [the longest x2 1.53 us: shards(): quad = jnp.stack([both, step2])]
  transfers between devices with their start and end apart: 16 -> 14, of which waited for: 8 -> 9; matrix products, arithmetic and copies ran while one was open for 35% -> 3% of each run, Pallas kernels for 0% -> 5%
where the time goes in v2:
time: 94.6 us; the launch traced here: 94.1 us
  waiting for transfers between devices  42.4 us (45%)
  starting transfers between devices  26.1 us (28%)
  local copies, waits for them, and re-layouts  11.1 us (12%)
  Pallas kernels  10.8 us (11%)
  other arithmetic  3.39 us (4%)
    ppermute x13, waiting for transfers between devices, permute(): return lax.ppermute(block, ('seq', 'vocab'), pairs)  35.5 us
    ppermute x13, starting transfers between devices, permute(): return lax.ppermute(block, ('seq', 'vocab'), pairs)  22.6 us
    pallas_call x4, Pallas kernels, call(): pl.pallas_call(kernel, out_shape=outs, in_specs=[SMEM] * n_smem + [VMEM]...  10.8 us
    unnamed x22, local copies, waits for them, and re-layouts  10.3 us
    all_to_all x1, waiting for transfers between devices, shards(): lax.all_to_all(send, ('seq', 'vocab'), 0, 0, tiled=True)  6.91 us
    all_to_all x1, starting transfers between devices, shards(): lax.all_to_all(send, ('seq', 'vocab'), 0, 0, tiled=True)  3.47 us
  transfers between devices with their start and end apart: 14, of which 9 were waited for; matrix products, arithmetic and copies ran while one was open for 3% of the time, Pallas kernels for 5%

profile of v2, /device:TPU:0, one launch (start us, length us, event | category | flops | bytes accessed | tf_op | source)
XLA Modules:
  0.0 94.1 jit_solution(4989319604993712415)
XLA Ops:
  0.0 0.9 pad_maximum_fusion.2.refs_0_
  0.9 5.0 %collective-permute-start.1 = (bf16[2,128,256]{2,1,0:T(8,128)(2,1)S(1)}, bf16[2,128,256]{2,1,0:T(8,128)(2,1)S(1)}, u32[]{:S(2)}, u32[]{:S(2)}) collective-permute-start(bf16[2,128,256]{2,1,0:T(8,128)(2,1)S(1)} %pad_maximum_fusion.2.refs_0_), channel_id=1, source_target_pairs={{0,8},{1,9},{2,10},{3,11},{4,12},{5,13},{6,14},{7,15},{8,16},{9,17... | collective-permute-start | bytes 393224 | tf_op jit(solution)/shard_map/ppermute | solution.py:239
  5.9 4.5 %collective-permute-start.2 = (bf16[2,128,256]{2,1,0:T(8,128)(2,1)S(1)}, bf16[2,128,256]{2,1,0:T(8,128)(2,1)S(1)}, u32[]{:S(2)}, u32[]{:S(2)}) collective-permute-start(bf16[2,128,256]{2,1,0:T(8,128)(2,1)S(1)} %pad_maximum_fusion.2.refs_0_), channel_id=1, source_target_pairs={{0,16},{1,17},{2,18},{3,19},{4,20},{5,21},{6,22},{7,23},{8,24},{9,... | collective-permute-start | bytes 393224 | tf_op jit(solution)/shard_map/ppermute | solution.py:239
  10.4 1.3 %collective-permute-start.3 = (bf16[2,128,256]{2,1,0:T(8,128)(2,1)S(1)}, bf16[2,128,256]{2,1,0:T(8,128)(2,1)S(1)}, u32[]{:S(2)}, u32[]{:S(2)}) collective-permute-start(bf16[2,128,256]{2,1,0:T(8,128)(2,1)S(1)} %pad_maximum_fusion.2.refs_0_), channel_id=1, source_target_pairs={{0,24},{1,25},{2,26},{3,27},{4,28},{5,29},{6,30},{7,31}} | collective-permute-start | bytes 393224 | tf_op jit(solution)/shard_map/ppermute | solution.py:239
  11.9 1.2 %copy-done.2 = bf16[128,4096]{1,0:T(8,128)(2,1)S(1)} copy-done((bf16[128,4096]{1,0:T(8,128)(2,1)S(1)}, bf16[128,4096]{1,0:T(8,128)(2,1)}, u32[]{:S(2)}) %copy-start.2) | copy-done | bytes 1048600
  13.1 0.9 %copy-done.3 = bf16[128,1024]{1,0:T(8,128)(2,1)S(1)} copy-done((bf16[128,1024]{1,0:T(8,128)(2,1)S(1)}, bf16[128,1024]{1,0:T(8,128)(2,1)}, u32[]{:S(2)}) %copy-start.3) | copy-done | bytes 262168
  14.0 0.7 copy-done.6
  14.7 1.1 %select_rows.1 = (bf16[48,1024]{1,0:T(8,128)(2,1)S(1)}, bf16[48,4096]{1,0:T(8,128)(2,1)S(1)}, f32[2,48,128]{2,1,0:T(8,128)S(1)}) custom-call(s32[2]{0:T(128)S(1)} %get-tuple-element.28.where_ref, s32[8,128]{1,0:T(8,128)S(1)} %bitcast.34, bf16[128,1024]{1,0:T(8,128)(2,1)S(1)} %copy-done.3, bf16[128,4096]{1,0:T(8,128)(2,1)S(1)} %copy-done.2), custom_call_target="tpu_custom_call" | custom-call | bytes 1314824 | tf_op jit(solution)/shard_map/select_rows/pallas_call | solution.py:27
  15.8 1.5 %collective-permute-start = (bf16[48,1024]{1,0:T(8,128)(2,1)S(1)}, bf16[48,1024]{1,0:T(8,128)(2,1)S(1)}, u32[]{:S(2)}, u32[]{:S(2)}) collective-permute-start(bf16[48,1024]{1,0:T(8,128)(2,1)S(1)} %get-tuple-element.15.q_own), channel_id=1, source_target_pairs={{0,4},{1,5},{2,6},{3,7},{4,0},{5,1},{6,2},{7,3},{8,12},{9,13},{10,... | collective-permute-start | bytes 294920 | tf_op jit(solution)/shard_map/ppermute | solution.py:239
  17.4 3.6 %collective-permute-done.q_other = bf16[48,1024]{1,0:T(8,128)(2,1)S(1)} collective-permute-done((bf16[48,1024]{1,0:T(8,128)(2,1)S(1)}, bf16[48,1024]{1,0:T(8,128)(2,1)S(1)}, u32[]{:S(2)}, u32[]{:S(2)}) %collective-permute-start) | collective-permute-done | bytes 98336 | tf_op jit(solution)/shard_map/ppermute | solution.py:239
  21.0 0.8 copy-done.4
  21.8 0.8 copy-done.5
  22.6 2.0 %attend.1 = (f32[48,1024]{1,0:T(8,128)S(1)}, f32[48,128]{1,0:T(8,128)S(1)}, bf16[48,1152]{1,0:T(8,128)(2,1)S(1)}) custom-call(s32[6]{0:T(128)S(1)} %stack.92.where_ref, f32[2,48,128]{2,1,0:T(8,128)S(1)} %get-tuple-element.14.blk_ref, bf16[48,1024]{1,0:T(8,128)(2,1)S(1)} %get-tuple-element.15.q_own, bf16[48,1024]{1,0:T(8,128)(2,1)S(1)} %collective-permute-done.q_other, ...), custom_call_target="tpu_custom_call" | custom-call | bytes 901144 | tf_op jit(solution)/shard_map/attend/pallas_call | solution.py:27
  24.6 1.6 %collective-permute-start.4 = (bf16[48,1152]{1,0:T(8,128)(2,1)S(1)}, bf16[48,1152]{1,0:T(8,128)(2,1)S(1)}, u32[]{:S(2)}, u32[]{:S(2)}) collective-permute-start(bf16[48,1152]{1,0:T(8,128)(2,1)S(1)} %get-tuple-element.18), channel_id=1, source_target_pairs={{0,4},{1,5},{2,6},{3,7},{4,0},{5,1},{6,2},{7,3},{8,12},{9,13},{10,... | collective-permute-start | bytes 331784 | tf_op jit(solution)/shard_map/ppermute | solution.py:239
  26.2 3.2 %collective-permute-done.4.got_ref = bf16[48,1152]{1,0:T(8,128)(2,1)S(1)} collective-permute-done((bf16[48,1152]{1,0:T(8,128)(2,1)S(1)}, bf16[48,1152]{1,0:T(8,128)(2,1)S(1)}, u32[]{:S(2)}, u32[]{:S(2)}) %collective-permute-start.4) | collective-permute-done | bytes 110624 | tf_op jit(solution)/shard_map/ppermute | solution.py:239
  29.5 3.4 %copy-done = bf16[1024,4096]{1,0:T(8,128)(2,1)S(1)} copy-done((bf16[1024,4096]{1,0:T(8,128)(2,1)S(1)}, bf16[1024,4096]{1,0:T(8,128)(2,1)}, u32[]{:S(2)}) %copy-start) | copy-done | bytes 8388632
  32.8 1.7 %project.1 = (f32[24,4096]{1,0:T(8,128)S(1)}, bf16[24,4096]{1,0:T(8,128)(2,1)S(1)}) custom-call(s32[1]{0:T(128)} %bitcast.2.where_ref, f32[48,1024]{1,0:T(8,128)S(1)} %get-tuple-element.16.own_ref, f32[48,128]{1,0:T(8,128)S(1)} %get-tuple-element.17.lse_ref, bf16[48,1152]{1,0:T(8,128)(2,1)S(1)} %collective-permute-done.4.got_ref, bf16[1024,4096]{1,0:T(8,128)(2,1)S(1)} %copy-done), custom_call_target="tpu_custom_call" | custom-call | bytes 8720388 | tf_op jit(solution)/shard_map/project/pallas_call | solution.py:27
  34.7 1.4 %collective-permute-done.5 = bf16[24,4096]{1,0:T(8,128)(2,1)S(1)} collective-permute-done((bf16[24,4096]{1,0:T(8,128)(2,1)S(1)}, bf16[24,4096]{1,0:T(8,128)(2,1)S(1)}, u32[]{:S(2)}, u32[]{:S(2)}) %collective-permute-start.5) | collective-permute-done | bytes 196640 | tf_op jit(solution)/shard_map/ppermute | solution.py:239
  36.1 1.6 %collective-permute-start.6 = (bf16[24,4096]{1,0:T(8,128)(2,1)S(1)}, bf16[24,4096]{1,0:T(8,128)(2,1)S(1)}, u32[]{:S(2)}, u32[]{:S(2)}) collective-permute-start(bf16[24,4096]{1,0:T(8,128)(2,1)S(1)} %fusion), channel_id=1, source_target_pairs={{0,2},{1,3},{2,0},{3,1},{4,6},{5,7},{6,4},{7,5},{8,10},{9,11},{10,... | collective-permute-start | bytes 589832 | tf_op jit(solution)/shard_map/ppermute | solution.py:239
  37.6 5.4 %collective-permute-done.6 = bf16[24,4096]{1,0:T(8,128)(2,1)S(1)} collective-permute-done((bf16[24,4096]{1,0:T(8,128)(2,1)S(1)}, bf16[24,4096]{1,0:T(8,128)(2,1)S(1)}, u32[]{:S(2)}, u32[]{:S(2)}) %collective-permute-start.6) | collective-permute-done | bytes 196640 | tf_op jit(solution)/shard_map/ppermute | solution.py:239
  43.5 1.0 %collective-permute-start.8 = (bf16[24,2048]{1,0:T(8,128)(2,1)S(1)}, bf16[24,2048]{1,0:T(8,128)(2,1)S(1)}, u32[]{:S(2)}, u32[]{:S(2)}) collective-permute-start(bf16[24,2048]{1,0:T(8,128)(2,1)S(1)} %fusion.2), channel_id=1, source_target_pairs={{0,16},{1,17},{2,18},{3,19},{4,20},{5,21},{6,22},{7,23},{8,24},{9,... | collective-permute-start | bytes 294920 | tf_op jit(solution)/shard_map/ppermute | solution.py:239
  44.5 2.8 %collective-permute-start.9 = (bf16[24,2048]{1,0:T(8,128)(2,1)S(1)}, bf16[24,2048]{1,0:T(8,128)(2,1)S(1)}, u32[]{:S(2)}, u32[]{:S(2)}) collective-permute-start(bf16[24,2048]{1,0:T(8,128)(2,1)S(1)} %fusion.2), channel_id=1, source_target_pairs={{0,24},{1,25},{2,26},{3,27},{4,28},{5,29},{6,30},{7,31},{8,0},{9,1... | collective-permute-start | bytes 294920 | tf_op jit(solution)/shard_map/ppermute | solution.py:239
  47.4 3.5 %collective-permute-done.7 = bf16[24,2048]{1,0:T(8,128)(2,1)S(1)} collective-permute-done((bf16[24,2048]{1,0:T(8,128)(2,1)S(1)}, bf16[24,2048]{1,0:T(8,128)(2,1)S(1)}, u32[]{:S(2)}, u32[]{:S(2)}) %collective-permute-start.7) | collective-permute-done | bytes 98336 | tf_op jit(solution)/shard_map/ppermute | solution.py:239
  50.9 2.6 %collective-permute-done.8 = bf16[24,2048]{1,0:T(8,128)(2,1)S(1)} collective-permute-done((bf16[24,2048]{1,0:T(8,128)(2,1)S(1)}, bf16[24,2048]{1,0:T(8,128)(2,1)S(1)}, u32[]{:S(2)}, u32[]{:S(2)}) %collective-permute-start.8) | collective-permute-done | bytes 98336 | tf_op jit(solution)/shard_map/ppermute | solution.py:239
  53.6 1.6 %collective-permute-start.10 = (bf16[4,24,2048]{2,1,0:T(8,128)(2,1)S(1)}, bf16[4,24,2048]{2,1,0:T(8,128)(2,1)S(1)}, u32[]{:S(2)}, u32[]{:S(2)}) collective-permute-start(bf16[4,24,2048]{2,1,0:T(8,128)(2,1)S(1)} %get-tuple-element.26), channel_id=1, source_target_pairs={{0,2},{1,5},{2,0},{3,7},{4,6},{5,1},{6,4},{7,3},{8,10},{9,13},{10,... | collective-permute-start | bytes 1179656 | tf_op jit(solution)/shard_map/ppermute | solution.py:239
  55.8 6.2 %collective-permute-done.10 = bf16[4,24,2048]{2,1,0:T(8,128)(2,1)S(1)} collective-permute-done((bf16[4,24,2048]{2,1,0:T(8,128)(2,1)S(1)}, bf16[4,24,2048]{2,1,0:T(8,128)(2,1)S(1)}, u32[]{:S(2)}, u32[]{:S(2)}) %collective-permute-start.10) | collective-permute-done | bytes 393248 | tf_op jit(solution)/shard_map/ppermute | solution.py:239
  62.1 1.6 %collective-permute-start.11 = (bf16[2,4,24,2048]{3,2,1,0:T(8,128)(2,1)S(1)}, bf16[2,4,24,2048]{3,2,1,0:T(8,128)(2,1)S(1)}, u32[]{:S(2)}, u32[]{:S(2)}) collective-permute-start(bf16[2,4,24,2048]{3,2,1,0:T(8,128)(2,1)S(1)} %pad_maximum_fusion), channel_id=1, source_target_pairs={{0,4},{1,3},{2,6},{3,1},{4,0},{5,7},{6,2},{7,5},{8,12},{9,11},{10,... | collective-permute-start | bytes 2359304 | tf_op jit(solution)/shard_map/ppermute | solution.py:239
  64.5 9.6 %collective-permute-done.11 = bf16[2,4,24,2048]{3,2,1,0:T(8,128)(2,1)S(1)} collective-permute-done((bf16[2,4,24,2048]{3,2,1,0:T(8,128)(2,1)S(1)}, bf16[2,4,24,2048]{3,2,1,0:T(8,128)(2,1)S(1)}, u32[]{:S(2)}, u32[]{:S(2)}) %collective-permute-start.11) | collective-permute-done | bytes 786464 | tf_op jit(solution)/shard_map/ppermute | solution.py:239
  74.1 2.4 %copy-done.1 = bf16[592,4096]{1,0:T(8,128)(2,1)S(1)} copy-done((bf16[592,4096]{1,0:T(8,128)(2,1)S(1)}, bf16[592,4096]{1,0:T(8,128)(2,1)}, u32[]{:S(2)}) %copy-start.1) | copy-done | bytes 4849688
  76.5 6.1 %logits.1 = f32[32,1,128]{2,1,0:T(1,128)} custom-call(s32[12]{0:T(128)S(1)} %concatenate.3.where_ref, s32[1,192]{1,0:T(1,128)S(1)} %reshape.159.target_ref, bf16[96,2048]{1,0:T(8,128)(2,1)S(1)} %bitcast.30, bf16[96,2048]{1,0:T(8,128)(2,1)S(1)} %bitcast.32, bf16[192,2048]{1,0:T(8,128)(2,1)S(1)} %bitcast.33, bf16[592,4096]{1,0:T(8,128)(2,1)S(1)} %copy-done.1, ...), custom_call_target="tpu_custom_call" | custom-call | flops 1862270976 | bytes 11273008 | tf_op jit(solution)/shard_map/logits/pallas_call | solution.py:27
  82.6 3.5 %all-to-all-start = ((f32[32,1,128]{2,1,0:T(1,128)}), f32[32,1,128]{2,1,0:T(1,128)S(1)}, u32[]{:S(2)}, u32[]{:S(2)}) async-start(f32[32,1,128]{2,1,0:T(1,128)} %logits.1), calls=%async_computation | async-start | bytes 32768 | tf_op jit(solution)/shard_map/all_to_all | solution.py:365
  86.4 6.9 %all-to-all-done = f32[32,1,128]{2,1,0:T(1,128)S(1)} async-done(((f32[32,1,128]{2,1,0:T(1,128)}), f32[32,1,128]{2,1,0:T(1,128)S(1)}, u32[]{:S(2)}, u32[]{:S(2)}) %all-to-all-start) | async-done | bytes 16416 | tf_op jit(solution)/shard_map/all_to_all | solution.py:365
  (59 shorter events, 3.6 us)
Async XLA Ops:
  0.9 20.1 %collective-permute-start.1 = (bf16[2,128,256]{2,1,0:T(8,128)(2,1)S(1)}, bf16[2,128,256]{2,1,0:T(8,128)(2,1)S(1)}, u32[]{:S(2)}, u32[]{:S(2)}) collective-permute-start(bf16[2,128,256]{2,1,0:T(8,128)(2,1)S(1)} %pad_maximum_fusion.2.refs_0_), channel_id=1, source_target_pairs={{0,8},{1,9},{2,10},{3,11},{4,12},{5,13},{6,14},{7,15},{8,16},{9,17... | collective-permute-start | bytes 393224 | tf_op jit(solution)/shard_map/ppermute | solution.py:239
  5.9 15.1 %collective-permute-start.2 = (bf16[2,128,256]{2,1,0:T(8,128)(2,1)S(1)}, bf16[2,128,256]{2,1,0:T(8,128)(2,1)S(1)}, u32[]{:S(2)}, u32[]{:S(2)}) collective-permute-start(bf16[2,128,256]{2,1,0:T(8,128)(2,1)S(1)} %pad_maximum_fusion.2.refs_0_), channel_id=1, source_target_pairs={{0,16},{1,17},{2,18},{3,19},{4,20},{5,21},{6,22},{7,23},{8,24},{9,... | collective-permute-start | bytes 393224 | tf_op jit(solution)/shard_map/ppermute | solution.py:239
  10.4 10.6 %collective-permute-start.3 = (bf16[2,128,256]{2,1,0:T(8,128)(2,1)S(1)}, bf16[2,128,256]{2,1,0:T(8,128)(2,1)S(1)}, u32[]{:S(2)}, u32[]{:S(2)}) collective-permute-start(bf16[2,128,256]{2,1,0:T(8,128)(2,1)S(1)} %pad_maximum_fusion.2.refs_0_), channel_id=1, source_target_pairs={{0,24},{1,25},{2,26},{3,27},{4,28},{5,29},{6,30},{7,31}} | collective-permute-start | bytes 393224 | tf_op jit(solution)/shard_map/ppermute | solution.py:239
  11.7 62.5 %collective-permute-start.12 = (bf16[592,4096]{1,0:T(8,128)(2,1)}, bf16[592,4096]{1,0:T(8,128)(2,1)}, u32[]{:S(2)}, u32[]{:S(2)}) collective-permute-start(bf16[592,4096]{1,0:T(8,128)(2,1)} %refs_3_.1), channel_id=1, source_target_pairs={{0,1},{1,0},{2,3},{3,2},{4,5},{5,4},{6,7},{7,6},{8,9},{9,8},{10,11... | collective-permute-start | bytes 14549000 | tf_op jit(solution)/shard_map/ppermute | solution.py:239
  11.9 1.2 %copy-start.2 = (bf16[128,4096]{1,0:T(8,128)(2,1)S(1)}, bf16[128,4096]{1,0:T(8,128)(2,1)}, u32[]{:S(2)}) copy-start(bf16[128,4096]{1,0:T(8,128)(2,1)} %res_ref.1) | copy-start | bytes 3145732
  13.1 0.9 %copy-start.3 = (bf16[128,1024]{1,0:T(8,128)(2,1)S(1)}, bf16[128,1024]{1,0:T(8,128)(2,1)}, u32[]{:S(2)}) copy-start(bf16[128,1024]{1,0:T(8,128)(2,1)} %q_ref.1) | copy-start | bytes 786436
  14.0 0.7 copy-start.6
  15.8 5.2 %collective-permute-start = (bf16[48,1024]{1,0:T(8,128)(2,1)S(1)}, bf16[48,1024]{1,0:T(8,128)(2,1)S(1)}, u32[]{:S(2)}, u32[]{:S(2)}) collective-permute-start(bf16[48,1024]{1,0:T(8,128)(2,1)S(1)} %get-tuple-element.15.q_own), channel_id=1, source_target_pairs={{0,4},{1,5},{2,6},{3,7},{4,0},{5,1},{6,2},{7,3},{8,12},{9,13},{10,... | collective-permute-start | bytes 294920 | tf_op jit(solution)/shard_map/ppermute | solution.py:239
  17.3 17.3 %copy-start.8 = (f32[4096]{0:T(1024)S(1)}, f32[4096]{0:T(1024)}, u32[]{:S(2)}) copy-start(f32[4096]{0:T(1024)} %param.19) | copy-start | bytes 49156
  21.0 0.8 copy-start.4
  21.8 0.8 copy-start.5
  24.6 13.0 %copy-start.7 = (s32[1024]{0:T(1024)S(1)}, s32[1024]{0:T(1024)}, u32[]{:S(2)}) copy-start(s32[1024]{0:T(1024)} %param.22) | copy-start | bytes 12292
  24.6 4.8 %collective-permute-start.4 = (bf16[48,1152]{1,0:T(8,128)(2,1)S(1)}, bf16[48,1152]{1,0:T(8,128)(2,1)S(1)}, u32[]{:S(2)}, u32[]{:S(2)}) collective-permute-start(bf16[48,1152]{1,0:T(8,128)(2,1)S(1)} %get-tuple-element.18), channel_id=1, source_target_pairs={{0,4},{1,5},{2,6},{3,7},{4,0},{5,1},{6,2},{7,3},{8,12},{9,13},{10,... | collective-permute-start | bytes 331784 | tf_op jit(solution)/shard_map/ppermute | solution.py:239
  29.5 3.4 %copy-start = (bf16[1024,4096]{1,0:T(8,128)(2,1)S(1)}, bf16[1024,4096]{1,0:T(8,128)(2,1)}, u32[]{:S(2)}) copy-start(bf16[1024,4096]{1,0:T(8,128)(2,1)} %w_ref.1) | copy-start | bytes 25165828
  32.8 22.8 %copy-start.9 = (s32[1024]{0:T(1024)S(1)}, s32[1024]{0:T(1024)}, u32[]{:S(2)}) copy-start(s32[1024]{0:T(1024)} %param.21) | copy-start | bytes 12292
  34.5 1.5 %collective-permute-start.5 = (bf16[24,4096]{1,0:T(8,128)(2,1)S(1)}, bf16[24,4096]{1,0:T(8,128)(2,1)S(1)}, u32[]{:S(2)}, u32[]{:S(2)}) collective-permute-start(bf16[24,4096]{1,0:T(8,128)(2,1)S(1)} %get-tuple-element.20), channel_id=1, source_target_pairs={{0,1},{1,0},{2,3},{3,2},{4,5},{5,4},{6,7},{7,6},{8,9},{9,8},{10,11... | collective-permute-start | bytes 589832 | tf_op jit(solution)/shard_map/ppermute | solution.py:239
  36.1 7.0 %collective-permute-start.6 = (bf16[24,4096]{1,0:T(8,128)(2,1)S(1)}, bf16[24,4096]{1,0:T(8,128)(2,1)S(1)}, u32[]{:S(2)}, u32[]{:S(2)}) collective-permute-start(bf16[24,4096]{1,0:T(8,128)(2,1)S(1)} %fusion), channel_id=1, source_target_pairs={{0,2},{1,3},{2,0},{3,1},{4,6},{5,7},{6,4},{7,5},{8,10},{9,11},{10,... | collective-permute-start | bytes 589832 | tf_op jit(solution)/shard_map/ppermute | solution.py:239
  43.4 7.5 %collective-permute-start.7 = (bf16[24,2048]{1,0:T(8,128)(2,1)S(1)}, bf16[24,2048]{1,0:T(8,128)(2,1)S(1)}, u32[]{:S(2)}, u32[]{:S(2)}) collective-permute-start(bf16[24,2048]{1,0:T(8,128)(2,1)S(1)} %fusion.2), channel_id=1, source_target_pairs={{0,8},{1,9},{2,10},{3,11},{4,12},{5,13},{6,14},{7,15},{8,16},{9,17... | collective-permute-start | bytes 294920 | tf_op jit(solution)/shard_map/ppermute | solution.py:239
  43.5 10.1 %collective-permute-start.8 = (bf16[24,2048]{1,0:T(8,128)(2,1)S(1)}, bf16[24,2048]{1,0:T(8,128)(2,1)S(1)}, u32[]{:S(2)}, u32[]{:S(2)}) collective-permute-start(bf16[24,2048]{1,0:T(8,128)(2,1)S(1)} %fusion.2), channel_id=1, source_target_pairs={{0,16},{1,17},{2,18},{3,19},{4,20},{5,21},{6,22},{7,23},{8,24},{9,... | collective-permute-start | bytes 294920 | tf_op jit(solution)/shard_map/ppermute | solution.py:239
  44.5 9.1 %collective-permute-start.9 = (bf16[24,2048]{1,0:T(8,128)(2,1)S(1)}, bf16[24,2048]{1,0:T(8,128)(2,1)S(1)}, u32[]{:S(2)}, u32[]{:S(2)}) collective-permute-start(bf16[24,2048]{1,0:T(8,128)(2,1)S(1)} %fusion.2), channel_id=1, source_target_pairs={{0,24},{1,25},{2,26},{3,27},{4,28},{5,29},{6,30},{7,31},{8,0},{9,1... | collective-permute-start | bytes 294920 | tf_op jit(solution)/shard_map/ppermute | solution.py:239
  53.6 8.4 %collective-permute-start.10 = (bf16[4,24,2048]{2,1,0:T(8,128)(2,1)S(1)}, bf16[4,24,2048]{2,1,0:T(8,128)(2,1)S(1)}, u32[]{:S(2)}, u32[]{:S(2)}) collective-permute-start(bf16[4,24,2048]{2,1,0:T(8,128)(2,1)S(1)} %get-tuple-element.26), channel_id=1, source_target_pairs={{0,2},{1,5},{2,0},{3,7},{4,6},{5,1},{6,4},{7,3},{8,10},{9,13},{10,... | collective-permute-start | bytes 1179656 | tf_op jit(solution)/shard_map/ppermute | solution.py:239
  62.1 12.1 %collective-permute-start.11 = (bf16[2,4,24,2048]{3,2,1,0:T(8,128)(2,1)S(1)}, bf16[2,4,24,2048]{3,2,1,0:T(8,128)(2,1)S(1)}, u32[]{:S(2)}, u32[]{:S(2)}) collective-permute-start(bf16[2,4,24,2048]{3,2,1,0:T(8,128)(2,1)S(1)} %pad_maximum_fusion), channel_id=1, source_target_pairs={{0,4},{1,3},{2,6},{3,1},{4,0},{5,7},{6,2},{7,5},{8,12},{9,11},{10,... | collective-permute-start | bytes 2359304 | tf_op jit(solution)/shard_map/ppermute | solution.py:239
  74.1 2.4 %copy-start.1 = (bf16[592,4096]{1,0:T(8,128)(2,1)S(1)}, bf16[592,4096]{1,0:T(8,128)(2,1)}, u32[]{:S(2)}) copy-start(bf16[592,4096]{1,0:T(8,128)(2,1)} %refs_3_.1) | copy-start | bytes 14548996
  76.5 9.6 %copy-start.10 = (s32[32]{0:T(128)S(1)}, s32[32]{0:T(128)}, u32[]{:S(2)}) copy-start(s32[32]{0:T(128)} %param.23) | copy-start | bytes 388
  82.6 10.6 %all-to-all-start = ((f32[32,1,128]{2,1,0:T(1,128)}), f32[32,1,128]{2,1,0:T(1,128)S(1)}, u32[]{:S(2)}, u32[]{:S(2)}) async-start(f32[32,1,128]{2,1,0:T(1,128)} %logits.1), calls=%async_computation | async-start | bytes 32768 | tf_op jit(solution)/shard_map/all_to_all | solution.py:365

commit v3 on v2

--- a/solution.py
+++ b/solution.py
@@ -19,39 +19,74 @@
 
 VMEM = pl.BlockSpec(memory_space=pltpu.VMEM)
 SMEM = pl.BlockSpec(memory_space=pltpu.SMEM)
+ANY = pl.BlockSpec(memory_space=pl.ANY)
 NT = (((1,), (1,)), ((), ()))
-
-
-def call(kernel, name, outs, n_smem, args, mib, flops=0, scratch=()):
+MIB = 1 << 20
+
+
+def call(kernel, name, outs, n_smem, args, mib, flops=0, scratch=(), n_any=0):
     n_bytes = sum(a.size * a.dtype.itemsize for a in args)
     return pl.pallas_call(
         kernel,
         out_shape=outs,
-        in_specs=[SMEM] * n_smem + [VMEM] * (len(args) - n_smem),
+        in_specs=[SMEM] * n_smem + [VMEM] * (len(args) - n_smem - n_any) + [ANY] * n_any,
         out_specs=jax.tree.map(lambda _: VMEM, outs),
         scratch_shapes=list(scratch),
-        compiler_params=pltpu.CompilerParams(vmem_limit_bytes=mib << 20),
+        compiler_params=pltpu.CompilerParams(vmem_limit_bytes=mib * MIB),
         cost_estimate=pl.CostEstimate(flops=flops, bytes_accessed=n_bytes, transcendentals=0),
         name=name,
     )(*args)
 
 
-def select_kernel(where_ref, mask_ref, q_ref, res_ref, q_out, res_out, blk_out):
+def slots_of(row):
+    tok = row.shape[1]
+    upto = lax.broadcasted_iota(jnp.int32, (tok, tok), 0) <= lax.broadcasted_iota(jnp.int32, (tok, tok), 1)
+    row = row.astype(jnp.float32)
+    count = jnp.dot(jnp.broadcast_to(row, (8, tok)), upto.astype(jnp.float32), preferred_element_type=jnp.float32)[0:1]
+    slots = lax.broadcasted_iota(jnp.int32, (CAP, tok), 0).astype(jnp.float32)
+    return ((count - 1.0) == slots) & (row == 1.0)
+
+
+def select_kernel(where_ref, mask_ref, q_hbm, kn_hbm, vn_hbm, q_out, blk_out, kn_out, vn_out, q_ref, sems):
+    copies = [
+        pltpu.make_async_copy(src, dst, sems.at[i])
+        for i, (src, dst) in enumerate(((q_hbm, q_ref), (kn_hbm, kn_out), (vn_hbm, vn_out)))
+    ]
+    for copy in copies:
+        copy.start()
     tok = mask_ref.shape[1]
-    before = lax.broadcasted_iota(jnp.int32, (tok, tok), 0) <= lax.broadcasted_iota(jnp.int32, (tok, tok), 1)
-    upto = before.astype(jnp.float32)
-    slots = lax.broadcasted_iota(jnp.int32, (CAP, tok), 0).astype(jnp.float32)
     block = lax.shift_right_logical(lax.broadcasted_iota(jnp.int32, (CAP, tok), 1), SHIFT).astype(jnp.float32)
+    picks = []
     for which in range(2):
-        row = mask_ref[pl.ds(where_ref[which], 1), :].astype(jnp.float32)
-        count = jnp.dot(jnp.broadcast_to(row, (8, tok)), upto, preferred_element_type=jnp.float32)[0:1]
-        chosen = ((count - 1.0) == slots) & (row == 1.0)
-        pick = jnp.where(chosen, 1.0, 0.0)
+        pick = jnp.where(slots_of(mask_ref[pl.ds(where_ref[which], 1), :]), 1.0, 0.0)
         blk_out[which] = jnp.broadcast_to(jnp.sum(pick * block, axis=1, keepdims=True), (CAP, LANES))
-        if which == 0:
-            pick = pick.astype(jnp.bfloat16)
-            q_out[...] = jnp.dot(pick, q_ref[...], preferred_element_type=jnp.float32).astype(jnp.bfloat16)
-            res_out[...] = jnp.dot(pick, res_ref[...], preferred_element_type=jnp.float32).astype(jnp.bfloat16)
+        picks.append(pick)
+    copies[0].wait()
+    q_out[...] = jnp.dot(picks[0].astype(jnp.bfloat16), q_ref[...], preferred_element_type=jnp.float32).astype(jnp.bfloat16)
+    copies[1].wait()
+    copies[2].wait()
+
+
+def stage_out_kernel(where_ref, mask_ref, res_hbm, w_hbm, after, res_out, w_out, res_ref, sems):
+    whole = pltpu.make_async_copy(w_hbm, w_out, sems.at[0])
+    whole.start()
+    copy = pltpu.make_async_copy(res_hbm, res_ref, sems.at[1])
+    copy.start()
+    pick = jnp.where(slots_of(mask_ref[pl.ds(where_ref[0], 1), :]), 1.0, 0.0).astype(jnp.bfloat16)
+    copy.wait()
+    res_out[...] = jnp.dot(pick, res_ref[...], preferred_element_type=jnp.float32).astype(jnp.bfloat16)
+    whole.wait()
+
+
+def stage_head_kernel(own_hbm, other_hbm, after, own_out, other_out, sems):
+    copies = [
+        pltpu.make_async_copy(src, dst, sems.at[i])
+        for i, (src, dst) in enumerate(((own_hbm, own_out), (other_hbm, other_out)))
+    ]
+    for copy in copies:
+        copy.start()
+    for copy in copies:
+        copy.wait()
 
 
 def split3(value):
@@ -145,30 +180,34 @@
         theirs_out[:, j : j + step] = jnp.where(first, lower, upper).astype(jnp.bfloat16)
 
 
-def logits_kernel(mixed, X, Y, Z, V, where_ref, target_ref, *refs):
+def logits_kernel(mixed, X, Y, sizes, V, where_ref, target_ref, *refs):
     half = CAP // 2
     share = refs[0].shape[1]
-    n_rows = Y * Z * half
-    quarter = Z * half
-    if mixed:
-        column, step1, step2, w_own, w_other, out_ref, near, far = refs
-
-        @pl.when(where_ref[1] == 0)
-        def _():
-            near[quarter:] = step2[:quarter]
-            far[:quarter] = step1[...]
-
-        @pl.when(where_ref[1] != 0)
-        def _():
-            near[quarter:] = step1[...]
-            far[:quarter] = step2[:quarter]
-
-        near[:quarter] = column[...]
-        far[quarter:] = step2[quarter:]
-        rows = [near, far]
-    else:
-        rows = refs[:X]
-        w_own, w_other, out_ref = refs[X:]
+    n_rows = Y * sum(sizes) * half
+    n_refs = (3 if mixed else X) * len(sizes)
+    pieces, (w_own, w_other, out_ref, *rows) = refs[:n_refs], refs[n_refs:]
+    base = 0
+    for i, size in enumerate(sizes):
+        n = size * half
+        if mixed:
+            column, step1, step2 = pieces[3 * i : 3 * i + 3]
+            near, far = rows
+            near[base : base + n] = column[...]
+            far[base + n : base + 2 * n] = step2[n:]
+
+            @pl.when(where_ref[1] == 0)
+            def _(base=base, n=n, step1=step1, step2=step2):
+                near[base + n : base + 2 * n] = step2[:n]
+                far[base : base + n] = step1[...]
+
+            @pl.when(where_ref[1] != 0)
+            def _(base=base, n=n, step1=step1, step2=step2):
+                near[base + n : base + 2 * n] = step1[...]
+                far[base : base + n] = step2[:n]
+        else:
+            for k in range(X):
+                rows[k][base : base + Y * n] = pieces[X * i + k][...]
+        base += Y * n
     logits = []
     for w in (w_own, w_other):
         total = None
@@ -190,7 +229,7 @@
     lse = jnp.broadcast_to(jnp.concatenate([lse, *pad], axis=1), (8, wide))
     picked = jnp.broadcast_to(jnp.concatenate([picked, *pad], axis=1), (8, wide))
     lane = lax.broadcasted_iota(jnp.int32, (8, LANES), 1)
-    for p in range(Y * Z):
+    for p in range(Y * sum(sizes)):
         a = pltpu.roll(lse, (wide - p * half) % wide, 1)[:, :LANES]
         b = pltpu.roll(picked, (wide - p * half + half) % wide, 1)[:, :LANES]
         row = jnp.where(lane < half, a, b)[0:1]
@@ -252,8 +291,13 @@
     def z_up(block, k):
         return permute(block, [(dev(a, b, e, f), dev(a + k, b, e, f)) for a, b, e, f in every if a + k < Z])
 
-    def z_shift(block, k):
-        return permute(block, [(dev(a, b, e, f), dev((a + k) % Z, b, e, f)) for a, b, e, f in every])
+    paired = Z & (Z - 1) == 0
+
+    def z_swap(block, k):
+        return permute(block, [(dev(a, b, e, f), dev(a ^ k if paired else (a + k) % Z, b, e, f)) for a, b, e, f in every])
+
+    def from_z(k):
+        return z ^ k if paired else (z - k) % Z
 
     def mixed_flip(block, first):
         pairs = []
@@ -274,17 +318,33 @@
         sources.append(jnp.where(z >= k, (z - k) * Y + y, S))
     partner = z * Y + 1 - y
     all_mask = mask_flags.reshape(S, tok_rows)
-    queries, residual_sel, slot_blocks = call(
+    queries, slot_blocks, keys_here, values_here = call(
         select_kernel,
         "select_rows",
         (
             jax.ShapeDtypeStruct((CAP, q_width), jnp.bfloat16),
-            jax.ShapeDtypeStruct((CAP, width), jnp.bfloat16),
             jax.ShapeDtypeStruct((2, CAP, LANES), jnp.float32),
+            jax.ShapeDtypeStruct(key_noised.shape, jnp.bfloat16),
+            jax.ShapeDtypeStruct(value_noised.shape, jnp.bfloat16),
         ),
         1,
-        (scalars(seq_index, partner), all_mask, q_noised, residual),
-        8,
+        (scalars(seq_index, partner), all_mask, q_noised, key_noised, value_noised),
+        58,
+        scratch=[pltpu.VMEM(q_noised.shape, jnp.bfloat16), pltpu.SemaphoreType.DMA((3,))],
+        n_any=3,
+    )
+    residual_sel, staged_out = call(
+        stage_out_kernel,
+        "stage_out",
+        (
+            jax.ShapeDtypeStruct((CAP, width), jnp.bfloat16),
+            jax.ShapeDtypeStruct(out_weight.shape, jnp.bfloat16),
+        ),
+        1,
+        (scalars(seq_index), all_mask, residual, out_weight, slot_blocks),
+        50,
+        scratch=[pltpu.VMEM(residual.shape, jnp.bfloat16), pltpu.SemaphoreType.DMA((2,))],
+        n_any=3,
     )
     other_queries = y_flip(queries)
     other_head = core_flip(head_weight)
@@ -297,7 +357,7 @@
             jax.ShapeDtypeStruct((CAP, q_width + LANES), jnp.bfloat16),
         ),
         1,
-        (scalars(seq_index, partner, *sources), slot_blocks, queries, other_queries, key_noised, value_noised, *pieces),
+        (scalars(seq_index, partner, *sources), slot_blocks, queries, other_queries, keys_here, values_here, *pieces),
         16,
     )
     got_sum = y_flip(other_sum)
@@ -306,7 +366,7 @@
         "project",
         (jax.ShapeDtypeStruct((HALF, width), jnp.float32), jax.ShapeDtypeStruct((HALF, width), jnp.bfloat16)),
         1,
-        (scalars(c), own_sum, own_lse, got_sum, out_weight),
+        (scalars(c), own_sum, own_lse, got_sum, staged_out),
         16,
     )
 
@@ -327,27 +387,40 @@
     normed = (hidden * lax.rsqrt(squares / D + norm_eps) * norm_gain[None, :]).astype(jnp.bfloat16)
 
     own = lax.dynamic_slice_in_dim(normed, x * share, share, 1)
-    slabs = [own] + [z_shift(own, k) for k in range(1, Z)]
-    column = jnp.stack(slabs)
+    slabs = [own] + [z_swap(own, k) for k in range(1, Z)]
     n_rows = Y * Z * HALF
     mixed = X == Y
-    if mixed:
-        step1 = mixed_flip(column, True)
-        step2 = mixed_flip(jnp.stack([column, step1]), False)
-        rows = [column.reshape(Z * HALF, share), step1.reshape(Z * HALF, share), step2.reshape(n_rows, share)]
-        scratch = [pltpu.VMEM((n_rows, share), jnp.bfloat16)] * 2
-    else:
-        pair = jnp.stack([column, y_flip(column)])
-        rows = [pair.reshape(n_rows, share)] + [x_shift(pair, k).reshape(n_rows, share) for k in range(1, X)]
-        scratch = []
-    src_z = (z - jnp.arange(Z)) % Z
-    src_s = (src_z[None, :] * Y + jnp.stack([y, 1 - y])[:, None]).reshape(Y * Z)
+    groups = [g for g in (list(range(min(2, Z))), list(range(2, Z))) if g]
+    rows, src_s = [], []
+    for group in groups:
+        n = len(group) * HALF
+        column = jnp.stack([slabs[k] for k in group])
+        if mixed:
+            step1 = mixed_flip(column, True)
+            step2 = mixed_flip(jnp.stack([column, step1]), False)
+            rows += [column.reshape(n, share), step1.reshape(n, share), step2.reshape(Y * n, share)]
+        else:
+            pair = jnp.stack([column, y_flip(column)])
+            rows += [pair.reshape(Y * n, share)] + [x_shift(pair, k).reshape(Y * n, share) for k in range(1, X)]
+        src_z = jnp.stack([from_z(k) for k in group])
+        src_s.append((src_z[None, :] * Y + jnp.stack([y, 1 - y])[:, None]).reshape(-1))
+    src_s = jnp.concatenate(src_s)
     from_s = src_s[None, :] == jnp.arange(S)[:, None]
     half_targets = lax.dynamic_slice_in_dim(slot_targets, c * HALF, HALF, 1)
     row_targets = jnp.sum(jnp.where(from_s[:, :, None], half_targets[:, None, :], 0), axis=0).reshape(1, n_rows)
     first = (seq_index * V + x * C) * vocab_rows
+    staged = call(
+        stage_head_kernel,
+        "stage_head",
+        (jax.ShapeDtypeStruct(head_weight.shape, jnp.bfloat16),) * 2,
+        0,
+        (head_weight, other_head, own),
+        50,
+        scratch=[pltpu.SemaphoreType.DMA((2,))],
+        n_any=3,
+    )
     send = call(
-        functools.partial(logits_kernel, mixed, X, Y, Z, V),
+        functools.partial(logits_kernel, mixed, X, Y, [len(g) for g in groups], V),
         "logits",
         jax.ShapeDtypeStruct((S * V, 1, LANES), jnp.float32),
         1,
@@ -355,12 +428,11 @@
             jnp.concatenate([scalars(x, c, first + c * vocab_rows, first + (1 - c) * vocab_rows), src_s.astype(jnp.int32)]),
             row_targets,
             *rows,
-            head_weight,
-            other_head,
+            *staged,
         ),
         24,
         4 * n_rows * width * vocab_rows,
-        scratch,
+        [pltpu.VMEM((n_rows, share), jnp.bfloat16)] * X,
     ).reshape(S * V, LANES)
     got = lax.all_to_all(send, ("seq", "vocab"), 0, 0, tiled=True).reshape(S * X, C, LANES)
     lse = got[:, :, :HALF]

time: 94.6 us -> 101 us (1.068)
  waiting for transfers between devices: 42.4 us -> 27.4 us
  Pallas kernels: 10.8 us -> 24.9 us
  other arithmetic: 3.39 us -> 6.11 us
  starting transfers between devices: 26.1 us -> 28.6 us
  local copies, waits for them, and re-layouts: 11.1 us -> 13.2 us
    ppermute x13 -> x15, waiting for transfers between devices: 35.5 us -> 20.5 us  [permute(): return lax.ppermute(block, ('seq', 'vocab'), pairs)]
    pallas_call x4 -> x6, Pallas kernels: 10.8 us -> 24.9 us  [call(): pl.pallas_call(kernel, out_shape=outs, in_specs=[SMEM] * n_smem + [VMEM]...]
    all_to_all x1, starting transfers between devices: 3.47 us -> 6.36 us  [shards(): lax.all_to_all(send, ('seq', 'vocab'), 0, 0, tiled=True)]
    unnamed x22 -> x24, local copies, waits for them, and re-layouts: 10.3 us -> 10.9 us
    ppermute x13 -> x15, starting transfers between devices: 22.6 us -> 22.3 us  [permute(): return lax.ppermute(block, ('seq', 'vocab'), pairs)]
  transfers between devices with their start and end apart: 14 -> 16, of which waited for: 9 -> 7; matrix products, arithmetic and copies ran while one was open for 3% -> 7% of each run, Pallas kernels for 5% -> 20%
where the time goes in v3:
time: 101 us; the launch traced here: 100 us
  starting transfers between devices  28.6 us (28%)
  waiting for transfers between devices  27.4 us (27%)
  Pallas kernels  24.9 us (25%)
  local copies, waits for them, and re-layouts  13.2 us (13%)
  other arithmetic  6.11 us (6%)
    pallas_call x6, Pallas kernels, call(): pl.pallas_call(kernel, out_shape=outs, in_specs=[SMEM] * n_smem + [VMEM]...  24.9 us
    ppermute x15, starting transfers between devices, permute(): return lax.ppermute(block, ('seq', 'vocab'), pairs)  22.3 us
    ppermute x15, waiting for transfers between devices, permute(): return lax.ppermute(block, ('seq', 'vocab'), pairs)  20.5 us
    unnamed x24, local copies, waits for them, and re-layouts  10.9 us
    all_to_all x1, waiting for transfers between devices, shards(): lax.all_to_all(send, ('seq', 'vocab'), 0, 0, tiled=True)  6.92 us
    all_to_all x1, starting transfers between devices, shards(): lax.all_to_all(send, ('seq', 'vocab'), 0, 0, tiled=True)  6.36 us
  transfers between devices with their start and end apart: 16, of which 7 were waited for; matrix products, arithmetic and copies ran while one was open for 7% of the time, Pallas kernels for 20%

profile of v3, /device:TPU:0, one launch (start us, length us, event | category | flops | bytes accessed | tf_op | source)
XLA Modules:
  0.0 100.5 jit_solution(17357162912799025765)
XLA Ops:
  0.0 0.9 pad_maximum_fusion.4.refs_0_
  0.9 5.0 %collective-permute-start.1 = (bf16[2,128,256]{2,1,0:T(8,128)(2,1)S(1)}, bf16[2,128,256]{2,1,0:T(8,128)(2,1)S(1)}, u32[]{:S(2)}, u32[]{:S(2)}) collective-permute-start(bf16[2,128,256]{2,1,0:T(8,128)(2,1)S(1)} %pad_maximum_fusion.4.refs_0_), channel_id=1, source_target_pairs={{0,8},{1,9},{2,10},{3,11},{4,12},{5,13},{6,14},{7,15},{8,16},{9,17... | collective-permute-start | bytes 393224 | tf_op jit(solution)/shard_map/ppermute | solution.py:278
  5.9 4.5 %collective-permute-start.2 = (bf16[2,128,256]{2,1,0:T(8,128)(2,1)S(1)}, bf16[2,128,256]{2,1,0:T(8,128)(2,1)S(1)}, u32[]{:S(2)}, u32[]{:S(2)}) collective-permute-start(bf16[2,128,256]{2,1,0:T(8,128)(2,1)S(1)} %pad_maximum_fusion.4.refs_0_), channel_id=1, source_target_pairs={{0,16},{1,17},{2,18},{3,19},{4,20},{5,21},{6,22},{7,23},{8,24},{9,... | collective-permute-start | bytes 393224 | tf_op jit(solution)/shard_map/ppermute | solution.py:278
  10.4 1.3 %collective-permute-start.3 = (bf16[2,128,256]{2,1,0:T(8,128)(2,1)S(1)}, bf16[2,128,256]{2,1,0:T(8,128)(2,1)S(1)}, u32[]{:S(2)}, u32[]{:S(2)}) collective-permute-start(bf16[2,128,256]{2,1,0:T(8,128)(2,1)S(1)} %pad_maximum_fusion.4.refs_0_), channel_id=1, source_target_pairs={{0,24},{1,25},{2,26},{3,27},{4,28},{5,29},{6,30},{7,31}} | collective-permute-start | bytes 393224 | tf_op jit(solution)/shard_map/ppermute | solution.py:278
  12.3 2.6 %select_rows.1 = (bf16[48,1024]{1,0:T(8,128)(2,1)}, f32[2,48,128]{2,1,0:T(8,128)}, bf16[128,256]{1,0:T(8,128)(2,1)}, bf16[128,256]{1,0:T(8,128)(2,1)}) custom-call(s32[2]{0:T(128)} %get-tuple-element.44.where_ref, s32[8,128]{1,0:T(8,128)} %bitcast.48, bf16[128,1024]{1,0:T(8,128)(2,1)} %q_hbm.1, bf16[128,256]{1,0:T(8,128)(2,1)} %kn_hbm.1, bf16[128,256]{1,0:T(8,128)(2,1)} %vn_hbm.1), custom_call_target="tpu_custom_call" | custom-call | bytes 397320 | tf_op jit(solution)/shard_map/select_rows/pallas_call | solution.py:29
  14.9 1.6 %collective-permute-start = (bf16[48,1024]{1,0:T(8,128)(2,1)}, bf16[48,1024]{1,0:T(8,128)(2,1)S(1)}, u32[]{:S(2)}, u32[]{:S(2)}) collective-permute-start(bf16[48,1024]{1,0:T(8,128)(2,1)} %get-tuple-element.20.q_own), channel_id=1, source_target_pairs={{0,4},{1,5},{2,6},{3,7},{4,0},{5,1},{6,2},{7,3},{8,12},{9,13},{10,... | collective-permute-start | bytes 294920 | tf_op jit(solution)/shard_map/ppermute | solution.py:278
  17.2 1.0 reduce_window_sum.18
  19.2 1.2 %copy-done.3 = bf16[128,4096]{1,0:T(8,128)(2,1)S(1)} copy-done((bf16[128,4096]{1,0:T(8,128)(2,1)S(1)}, bf16[128,4096]{1,0:T(8,128)(2,1)}, u32[]{:S(2)}) %copy-start.3) | copy-done | bytes 1048600
  20.4 0.8 copy-done.4
  21.9 6.8 %stage_out.1 = (bf16[48,4096]{1,0:T(8,128)(2,1)S(1)}, bf16[1024,4096]{1,0:T(8,128)(2,1)}) custom-call(s32[1]{0:T(128)} %bitcast.13.where_ref, s32[8,128]{1,0:T(8,128)S(1)} %bitcast.50, bf16[128,4096]{1,0:T(8,128)(2,1)S(1)} %copy-done.3, bf16[1024,4096]{1,0:T(8,128)(2,1)} %w_hbm.1, f32[2,48,128]{2,1,0:T(8,128)S(1)} %copy-done.4), custom_call_target="tpu_custom_call" | custom-call | bytes 9490436 | tf_op jit(solution)/shard_map/stage_out/pallas_call | solution.py:29
  28.8 2.0 %attend.1 = (f32[48,1024]{1,0:T(8,128)S(1)}, f32[48,128]{1,0:T(8,128)S(1)}, bf16[48,1152]{1,0:T(8,128)(2,1)S(1)}) custom-call(s32[6]{0:T(128)S(1)} %stack.132.where_ref, f32[2,48,128]{2,1,0:T(8,128)S(1)} %copy-done.5, bf16[48,1024]{1,0:T(8,128)(2,1)S(1)} %copy-done.6, bf16[48,1024]{1,0:T(8,128)(2,1)S(1)} %collective-permute-done.q_other, ...), custom_call_target="tpu_custom_call" | custom-call | bytes 901144 | tf_op jit(solution)/shard_map/attend/pallas_call | solution.py:29
  31.6 4.7 %collective-permute-done.4.got_ref = bf16[48,1152]{1,0:T(8,128)(2,1)S(1)} collective-permute-done((bf16[48,1152]{1,0:T(8,128)(2,1)S(1)}, bf16[48,1152]{1,0:T(8,128)(2,1)S(1)}, u32[]{:S(2)}, u32[]{:S(2)}) %collective-permute-start.4) | collective-permute-done | bytes 110624 | tf_op jit(solution)/shard_map/ppermute | solution.py:278
  36.3 3.4 %copy-done = bf16[1024,4096]{1,0:T(8,128)(2,1)S(1)} copy-done((bf16[1024,4096]{1,0:T(8,128)(2,1)S(1)}, bf16[1024,4096]{1,0:T(8,128)(2,1)}, u32[]{:S(2)}) %copy-start) | copy-done | bytes 8388632
  39.7 1.7 %project.1 = (f32[24,4096]{1,0:T(8,128)S(1)}, bf16[24,4096]{1,0:T(8,128)(2,1)S(1)}) custom-call(s32[1]{0:T(128)} %bitcast.2.where_ref, f32[48,1024]{1,0:T(8,128)S(1)} %get-tuple-element.23.own_ref, f32[48,128]{1,0:T(8,128)S(1)} %get-tuple-element.24.lse_ref, bf16[48,1152]{1,0:T(8,128)(2,1)S(1)} %collective-permute-done.4.got_ref, bf16[1024,4096]{1,0:T(8,128)(2,1)S(1)} %copy-done), custom_call_target="tpu_custom_call" | custom-call | bytes 8720388 | tf_op jit(solution)/shard_map/project/pallas_call | solution.py:29
  41.6 1.3 %collective-permute-done.5 = bf16[24,4096]{1,0:T(8,128)(2,1)S(1)} collective-permute-done((bf16[24,4096]{1,0:T(8,128)(2,1)S(1)}, bf16[24,4096]{1,0:T(8,128)(2,1)S(1)}, u32[]{:S(2)}, u32[]{:S(2)}) %collective-permute-start.5) | collective-permute-done | bytes 196640 | tf_op jit(solution)/shard_map/ppermute | solution.py:278
  42.9 1.6 %collective-permute-start.6 = (bf16[24,4096]{1,0:T(8,128)(2,1)S(1)}, bf16[24,4096]{1,0:T(8,128)(2,1)S(1)}, u32[]{:S(2)}, u32[]{:S(2)}) collective-permute-start(bf16[24,4096]{1,0:T(8,128)(2,1)S(1)} %fusion), channel_id=1, source_target_pairs={{0,2},{1,3},{2,0},{3,1},{4,6},{5,7},{6,4},{7,5},{8,10},{9,11},{10,... | collective-permute-start | bytes 589832 | tf_op jit(solution)/shard_map/ppermute | solution.py:278
  44.5 5.4 %collective-permute-done.6 = bf16[24,4096]{1,0:T(8,128)(2,1)S(1)} collective-permute-done((bf16[24,4096]{1,0:T(8,128)(2,1)S(1)}, bf16[24,4096]{1,0:T(8,128)(2,1)S(1)}, u32[]{:S(2)}, u32[]{:S(2)}) %collective-permute-start.6) | collective-permute-done | bytes 196640 | tf_op jit(solution)/shard_map/ppermute | solution.py:278
  50.4 1.1 %collective-permute-start.11 = (bf16[24,2048]{1,0:T(8,128)(2,1)S(1)}, bf16[24,2048]{1,0:T(8,128)(2,1)S(1)}, u32[]{:S(2)}, u32[]{:S(2)}) collective-permute-start(bf16[24,2048]{1,0:T(8,128)(2,1)S(1)} %fusion.2.after), channel_id=1, source_target_pairs={{0,24},{1,25},{2,26},{3,27},{4,28},{5,29},{6,30},{7,31},{8,16},{9,... | collective-permute-start | bytes 294920 | tf_op jit(solution)/shard_map/ppermute | solution.py:278
  51.6 2.4 %collective-permute-start.7 = (bf16[24,2048]{1,0:T(8,128)(2,1)S(1)}, bf16[24,2048]{1,0:T(8,128)(2,1)S(1)}, u32[]{:S(2)}, u32[]{:S(2)}) collective-permute-start(bf16[24,2048]{1,0:T(8,128)(2,1)S(1)} %fusion.2.after), channel_id=1, source_target_pairs={{0,8},{1,9},{2,10},{3,11},{4,12},{5,13},{6,14},{7,15},{8,0},{9,1},... | collective-permute-start | bytes 294920 | tf_op jit(solution)/shard_map/ppermute | solution.py:278
  54.0 4.4 %collective-permute-done.10 = bf16[24,2048]{1,0:T(8,128)(2,1)S(1)} collective-permute-done((bf16[24,2048]{1,0:T(8,128)(2,1)S(1)}, bf16[24,2048]{1,0:T(8,128)(2,1)S(1)}, u32[]{:S(2)}, u32[]{:S(2)}) %collective-permute-start.10) | collective-permute-done | bytes 98336 | tf_op jit(solution)/shard_map/ppermute | solution.py:278
  58.4 1.6 %collective-permute-start.12 = (bf16[2,24,2048]{2,1,0:T(8,128)(2,1)S(1)}, bf16[2,24,2048]{2,1,0:T(8,128)(2,1)S(1)}, u32[]{:S(2)}, u32[]{:S(2)}) collective-permute-start(bf16[2,24,2048]{2,1,0:T(8,128)(2,1)S(1)} %get-tuple-element.36), channel_id=1, source_target_pairs={{0,2},{1,5},{2,0},{3,7},{4,6},{5,1},{6,4},{7,3},{8,10},{9,13},{10,... | collective-permute-start | bytes 589832 | tf_op jit(solution)/shard_map/ppermute | solution.py:278
  60.0 1.4 %collective-permute-start.8 = (bf16[2,24,2048]{2,1,0:T(8,128)(2,1)S(1)}, bf16[2,24,2048]{2,1,0:T(8,128)(2,1)S(1)}, u32[]{:S(2)}, u32[]{:S(2)}) collective-permute-start(bf16[2,24,2048]{2,1,0:T(8,128)(2,1)S(1)} %get-tuple-element.38), channel_id=1, source_target_pairs={{0,2},{1,5},{2,0},{3,7},{4,6},{5,1},{6,4},{7,3},{8,10},{9,13},{10,... | collective-permute-start | bytes 589832 | tf_op jit(solution)/shard_map/ppermute | solution.py:278
  61.4 2.7 %collective-permute-done.12 = bf16[2,24,2048]{2,1,0:T(8,128)(2,1)S(1)} collective-permute-done((bf16[2,24,2048]{2,1,0:T(8,128)(2,1)S(1)}, bf16[2,24,2048]{2,1,0:T(8,128)(2,1)S(1)}, u32[]{:S(2)}, u32[]{:S(2)}) %collective-permute-start.12) | collective-permute-done | bytes 196640 | tf_op jit(solution)/shard_map/ppermute | solution.py:278
  64.8 1.8 %collective-permute-done.8 = bf16[2,24,2048]{2,1,0:T(8,128)(2,1)S(1)} collective-permute-done((bf16[2,24,2048]{2,1,0:T(8,128)(2,1)S(1)}, bf16[2,24,2048]{2,1,0:T(8,128)(2,1)S(1)}, u32[]{:S(2)}, u32[]{:S(2)}) %collective-permute-start.8) | collective-permute-done | bytes 196640 | tf_op jit(solution)/shard_map/ppermute | solution.py:278
  67.4 0.8 dynamic-slice_bitcast_fusion
  68.5 0.8 broadcast_compare_fusion.1
  69.4 7.6 %stage_head.1 = (bf16[592,4096]{1,0:T(8,128)(2,1)}, bf16[592,4096]{1,0:T(8,128)(2,1)}) custom-call(bf16[592,4096]{1,0:T(8,128)(2,1)} %own_hbm.1, bf16[592,4096]{1,0:T(8,128)(2,1)} %collective-permute-done.14.other_hbm, bf16[24,2048]{1,0:T(8,128)(2,1)S(1)} %fusion.2.after), custom_call_target="tpu_custom_call" | custom-call | bytes 9797632 | tf_op jit(solution)/shard_map/stage_head/pallas_call | solution.py:29
  77.0 2.4 %copy-done.1 = bf16[592,4096]{1,0:T(8,128)(2,1)S(1)} copy-done((bf16[592,4096]{1,0:T(8,128)(2,1)S(1)}, bf16[592,4096]{1,0:T(8,128)(2,1)}, u32[]{:S(2)}) %copy-start.1) | copy-done | bytes 4849688
  79.4 2.4 %copy-done.2 = bf16[592,4096]{1,0:T(8,128)(2,1)S(1)} copy-done((bf16[592,4096]{1,0:T(8,128)(2,1)S(1)}, bf16[592,4096]{1,0:T(8,128)(2,1)}, u32[]{:S(2)}) %copy-start.2) | copy-done | bytes 4849688
  81.8 4.3 %logits.1 = f32[32,1,128]{2,1,0:T(1,128)} custom-call(s32[12]{0:T(128)S(1)} %concatenate.15.where_ref, s32[1,192]{1,0:T(1,128)S(1)} %reshape.177.target_ref, bf16[48,2048]{1,0:T(8,128)(2,1)S(1)} %bitcast.43, bf16[48,2048]{1,0:T(8,128)(2,1)S(1)} %bitcast.45, bf16[96,2048]{1,0:T(8,128)(2,1)S(1)} %bitcast.47, bf16[48,2048]{1,0:T(8,128)(2,1)S(1)} %bitcast.40, ...), custom_call_target="tpu_custom_call" | custom-call | flops 1862270976 | bytes 11273008 | tf_op jit(solution)/shard_map/logits/pallas_call | solution.py:29
  86.1 6.4 %all-to-all-start = ((f32[32,1,128]{2,1,0:T(1,128)}), f32[32,1,128]{2,1,0:T(1,128)S(1)}, u32[]{:S(2)}, u32[]{:S(2)}) async-start(f32[32,1,128]{2,1,0:T(1,128)} %logits.1), calls=%async_computation | async-start | bytes 32768 | tf_op jit(solution)/shard_map/all_to_all | solution.py:437
  92.7 6.9 %all-to-all-done = f32[32,1,128]{2,1,0:T(1,128)S(1)} async-done(((f32[32,1,128]{2,1,0:T(1,128)}), f32[32,1,128]{2,1,0:T(1,128)S(1)}, u32[]{:S(2)}, u32[]{:S(2)}) %all-to-all-start) | async-done | bytes 16416 | tf_op jit(solution)/shard_map/all_to_all | solution.py:437
  (71 shorter events, 7.7 us)
Async XLA Ops:
  0.9 27.9 %collective-permute-start.1 = (bf16[2,128,256]{2,1,0:T(8,128)(2,1)S(1)}, bf16[2,128,256]{2,1,0:T(8,128)(2,1)S(1)}, u32[]{:S(2)}, u32[]{:S(2)}) collective-permute-start(bf16[2,128,256]{2,1,0:T(8,128)(2,1)S(1)} %pad_maximum_fusion.4.refs_0_), channel_id=1, source_target_pairs={{0,8},{1,9},{2,10},{3,11},{4,12},{5,13},{6,14},{7,15},{8,16},{9,17... | collective-permute-start | bytes 393224 | tf_op jit(solution)/shard_map/ppermute | solution.py:278
  5.9 22.9 %collective-permute-start.2 = (bf16[2,128,256]{2,1,0:T(8,128)(2,1)S(1)}, bf16[2,128,256]{2,1,0:T(8,128)(2,1)S(1)}, u32[]{:S(2)}, u32[]{:S(2)}) collective-permute-start(bf16[2,128,256]{2,1,0:T(8,128)(2,1)S(1)} %pad_maximum_fusion.4.refs_0_), channel_id=1, source_target_pairs={{0,16},{1,17},{2,18},{3,19},{4,20},{5,21},{6,22},{7,23},{8,24},{9,... | collective-permute-start | bytes 393224 | tf_op jit(solution)/shard_map/ppermute | solution.py:278
  10.4 18.4 %collective-permute-start.3 = (bf16[2,128,256]{2,1,0:T(8,128)(2,1)S(1)}, bf16[2,128,256]{2,1,0:T(8,128)(2,1)S(1)}, u32[]{:S(2)}, u32[]{:S(2)}) collective-permute-start(bf16[2,128,256]{2,1,0:T(8,128)(2,1)S(1)} %pad_maximum_fusion.4.refs_0_), channel_id=1, source_target_pairs={{0,24},{1,25},{2,26},{3,27},{4,28},{5,29},{6,30},{7,31}} | collective-permute-start | bytes 393224 | tf_op jit(solution)/shard_map/ppermute | solution.py:278
  14.9 13.9 %copy-start.5 = (f32[2,48,128]{2,1,0:T(8,128)S(1)}, f32[2,48,128]{2,1,0:T(8,128)}, u32[]{:S(2)}) copy-start(f32[2,48,128]{2,1,0:T(8,128)} %get-tuple-element.18.after.blk_ref) | copy-start | bytes 147460
  14.9 13.9 %copy-start.6 = (bf16[48,1024]{1,0:T(8,128)(2,1)S(1)}, bf16[48,1024]{1,0:T(8,128)(2,1)}, u32[]{:S(2)}) copy-start(bf16[48,1024]{1,0:T(8,128)(2,1)} %get-tuple-element.20.q_own) | copy-start | bytes 294916
  14.9 13.8 %collective-permute-start = (bf16[48,1024]{1,0:T(8,128)(2,1)}, bf16[48,1024]{1,0:T(8,128)(2,1)S(1)}, u32[]{:S(2)}, u32[]{:S(2)}) collective-permute-start(bf16[48,1024]{1,0:T(8,128)(2,1)} %get-tuple-element.20.q_own), channel_id=1, source_target_pairs={{0,4},{1,5},{2,6},{3,7},{4,0},{5,1},{6,2},{7,3},{8,12},{9,13},{10,... | collective-permute-start | bytes 294920 | tf_op jit(solution)/shard_map/ppermute | solution.py:278
  16.5 52.9 %collective-permute-start.14 = (bf16[592,4096]{1,0:T(8,128)(2,1)}, bf16[592,4096]{1,0:T(8,128)(2,1)}, u32[]{:S(2)}, u32[]{:S(2)}) collective-permute-start(bf16[592,4096]{1,0:T(8,128)(2,1)} %own_hbm.1), channel_id=1, source_target_pairs={{0,1},{1,0},{2,3},{3,2},{4,5},{5,4},{6,7},{7,6},{8,9},{9,8},{10,11... | collective-permute-start | bytes 14549000 | tf_op jit(solution)/shard_map/ppermute | solution.py:278
  19.2 1.2 %copy-start.3 = (bf16[128,4096]{1,0:T(8,128)(2,1)S(1)}, bf16[128,4096]{1,0:T(8,128)(2,1)}, u32[]{:S(2)}) copy-start(bf16[128,4096]{1,0:T(8,128)(2,1)} %res_hbm.1) | copy-start | bytes 3145732
  20.4 0.8 copy-start.4
  21.2 0.7 copy-start.7
  21.9 6.9 %copy-start.8 = (bf16[128,256]{1,0:T(8,128)(2,1)S(1)}, bf16[128,256]{1,0:T(8,128)(2,1)}, u32[]{:S(2)}) copy-start(bf16[128,256]{1,0:T(8,128)(2,1)} %get-tuple-element.21.kn_ref) | copy-start | bytes 196612
  21.9 6.9 %copy-start.9 = (bf16[128,256]{1,0:T(8,128)(2,1)S(1)}, bf16[128,256]{1,0:T(8,128)(2,1)}, u32[]{:S(2)}) copy-start(bf16[128,256]{1,0:T(8,128)(2,1)} %get-tuple-element.22.vn_ref) | copy-start | bytes 196612
  21.9 9.5 %copy-start.10 = (s32[1024]{0:T(1024)S(1)}, s32[1024]{0:T(1024)}, u32[]{:S(2)}) copy-start(s32[1024]{0:T(1024)} %param.21) | copy-start | bytes 12292
  30.8 5.5 %collective-permute-start.4 = (bf16[48,1152]{1,0:T(8,128)(2,1)S(1)}, bf16[48,1152]{1,0:T(8,128)(2,1)S(1)}, u32[]{:S(2)}, u32[]{:S(2)}) collective-permute-start(bf16[48,1152]{1,0:T(8,128)(2,1)S(1)} %get-tuple-element.25), channel_id=1, source_target_pairs={{0,4},{1,5},{2,6},{3,7},{4,0},{5,1},{6,2},{7,3},{8,12},{9,13},{10,... | collective-permute-start | bytes 331784 | tf_op jit(solution)/shard_map/ppermute | solution.py:278
  36.3 3.4 %copy-start = (bf16[1024,4096]{1,0:T(8,128)(2,1)S(1)}, bf16[1024,4096]{1,0:T(8,128)(2,1)}, u32[]{:S(2)}) copy-start(bf16[1024,4096]{1,0:T(8,128)(2,1)} %get-tuple-element.26.w_ref) | copy-start | bytes 25165828
  41.4 1.5 %collective-permute-start.5 = (bf16[24,4096]{1,0:T(8,128)(2,1)S(1)}, bf16[24,4096]{1,0:T(8,128)(2,1)S(1)}, u32[]{:S(2)}, u32[]{:S(2)}) collective-permute-start(bf16[24,4096]{1,0:T(8,128)(2,1)S(1)} %get-tuple-element.28), channel_id=1, source_target_pairs={{0,1},{1,0},{2,3},{3,2},{4,5},{5,4},{6,7},{7,6},{8,9},{9,8},{10,11... | collective-permute-start | bytes 589832 | tf_op jit(solution)/shard_map/ppermute | solution.py:278
  42.9 7.0 %collective-permute-start.6 = (bf16[24,4096]{1,0:T(8,128)(2,1)S(1)}, bf16[24,4096]{1,0:T(8,128)(2,1)S(1)}, u32[]{:S(2)}, u32[]{:S(2)}) collective-permute-start(bf16[24,4096]{1,0:T(8,128)(2,1)S(1)} %fusion), channel_id=1, source_target_pairs={{0,2},{1,3},{2,0},{3,1},{4,6},{5,7},{6,4},{7,5},{8,10},{9,11},{10,... | collective-permute-start | bytes 589832 | tf_op jit(solution)/shard_map/ppermute | solution.py:278
  50.3 8.1 %collective-permute-start.10 = (bf16[24,2048]{1,0:T(8,128)(2,1)S(1)}, bf16[24,2048]{1,0:T(8,128)(2,1)S(1)}, u32[]{:S(2)}, u32[]{:S(2)}) collective-permute-start(bf16[24,2048]{1,0:T(8,128)(2,1)S(1)} %fusion.2.after), channel_id=1, source_target_pairs={{0,16},{1,17},{2,18},{3,19},{4,20},{5,21},{6,22},{7,23},{8,24},{9,... | collective-permute-start | bytes 294920 | tf_op jit(solution)/shard_map/ppermute | solution.py:278
  50.4 8.0 %collective-permute-start.11 = (bf16[24,2048]{1,0:T(8,128)(2,1)S(1)}, bf16[24,2048]{1,0:T(8,128)(2,1)S(1)}, u32[]{:S(2)}, u32[]{:S(2)}) collective-permute-start(bf16[24,2048]{1,0:T(8,128)(2,1)S(1)} %fusion.2.after), channel_id=1, source_target_pairs={{0,24},{1,25},{2,26},{3,27},{4,28},{5,29},{6,30},{7,31},{8,16},{9,... | collective-permute-start | bytes 294920 | tf_op jit(solution)/shard_map/ppermute | solution.py:278
  51.6 8.4 %collective-permute-start.7 = (bf16[24,2048]{1,0:T(8,128)(2,1)S(1)}, bf16[24,2048]{1,0:T(8,128)(2,1)S(1)}, u32[]{:S(2)}, u32[]{:S(2)}) collective-permute-start(bf16[24,2048]{1,0:T(8,128)(2,1)S(1)} %fusion.2.after), channel_id=1, source_target_pairs={{0,8},{1,9},{2,10},{3,11},{4,12},{5,13},{6,14},{7,15},{8,0},{9,1},... | collective-permute-start | bytes 294920 | tf_op jit(solution)/shard_map/ppermute | solution.py:278
  58.4 5.7 %collective-permute-start.12 = (bf16[2,24,2048]{2,1,0:T(8,128)(2,1)S(1)}, bf16[2,24,2048]{2,1,0:T(8,128)(2,1)S(1)}, u32[]{:S(2)}, u32[]{:S(2)}) collective-permute-start(bf16[2,24,2048]{2,1,0:T(8,128)(2,1)S(1)} %get-tuple-element.36), channel_id=1, source_target_pairs={{0,2},{1,5},{2,0},{3,7},{4,6},{5,1},{6,4},{7,3},{8,10},{9,13},{10,... | collective-permute-start | bytes 589832 | tf_op jit(solution)/shard_map/ppermute | solution.py:278
  60.0 6.6 %collective-permute-start.8 = (bf16[2,24,2048]{2,1,0:T(8,128)(2,1)S(1)}, bf16[2,24,2048]{2,1,0:T(8,128)(2,1)S(1)}, u32[]{:S(2)}, u32[]{:S(2)}) collective-permute-start(bf16[2,24,2048]{2,1,0:T(8,128)(2,1)S(1)} %get-tuple-element.38), channel_id=1, source_target_pairs={{0,2},{1,5},{2,0},{3,7},{4,6},{5,1},{6,4},{7,3},{8,10},{9,13},{10,... | collective-permute-start | bytes 589832 | tf_op jit(solution)/shard_map/ppermute | solution.py:278
  64.2 12.8 %collective-permute-start.13 = (bf16[2,2,24,2048]{3,2,1,0:T(8,128)(2,1)S(1)}, bf16[2,2,24,2048]{3,2,1,0:T(8,128)(2,1)S(1)}, u32[]{:S(2)}, u32[]{:S(2)}) collective-permute-start(bf16[2,2,24,2048]{3,2,1,0:T(8,128)(2,1)S(1)} %pad_maximum_fusion.1), channel_id=1, source_target_pairs={{0,4},{1,3},{2,6},{3,1},{4,0},{5,7},{6,2},{7,5},{8,12},{9,11},{10,... | collective-permute-start | bytes 1179656 | tf_op jit(solution)/shard_map/ppermute | solution.py:278
  66.7 10.4 %collective-permute-start.9 = (bf16[2,2,24,2048]{3,2,1,0:T(8,128)(2,1)S(1)}, bf16[2,2,24,2048]{3,2,1,0:T(8,128)(2,1)S(1)}, u32[]{:S(2)}, u32[]{:S(2)}) collective-permute-start(bf16[2,2,24,2048]{3,2,1,0:T(8,128)(2,1)S(1)} %pad_maximum_fusion), channel_id=1, source_target_pairs={{0,4},{1,3},{2,6},{3,1},{4,0},{5,7},{6,2},{7,5},{8,12},{9,11},{10,... | collective-permute-start | bytes 1179656 | tf_op jit(solution)/shard_map/ppermute | solution.py:278
  77.0 2.4 %copy-start.1 = (bf16[592,4096]{1,0:T(8,128)(2,1)S(1)}, bf16[592,4096]{1,0:T(8,128)(2,1)}, u32[]{:S(2)}) copy-start(bf16[592,4096]{1,0:T(8,128)(2,1)} %get-tuple-element.29.refs_6_) | copy-start | bytes 14548996
  79.4 2.4 %copy-start.2 = (bf16[592,4096]{1,0:T(8,128)(2,1)S(1)}, bf16[592,4096]{1,0:T(8,128)(2,1)}, u32[]{:S(2)}) copy-start(bf16[592,4096]{1,0:T(8,128)(2,1)} %get-tuple-element.30.refs_7_) | copy-start | bytes 14548996
  81.8 10.7 %copy-start.11 = (s32[32]{0:T(128)S(1)}, s32[32]{0:T(128)}, u32[]{:S(2)}) copy-start(s32[32]{0:T(128)} %param.23) | copy-start | bytes 388
  86.1 13.5 %all-to-all-start = ((f32[32,1,128]{2,1,0:T(1,128)}), f32[32,1,128]{2,1,0:T(1,128)S(1)}, u32[]{:S(2)}, u32[]{:S(2)}) async-start(f32[32,1,128]{2,1,0:T(1,128)} %logits.1), calls=%async_computation | async-start | bytes 32768 | tf_op jit(solution)/shard_map/all_to_all | solution.py:437

commit v4 on v3

v4 whole, which is shorter than its diff:
```python
import functools

import jax
import jax.numpy as jnp
from jax import lax
from jax.experimental import pallas as pl
from jax.experimental.pallas import tpu as pltpu
from jax.sharding import PartitionSpec as P


D = 4096
HEAD_DIM = 128
BLOCK = 32
CAP = 48
HALF = CAP // 2
LANES = 128
SHIFT = BLOCK.bit_length() - 1
C = 2
Y = 2

very_low = -1e30
norm_eps = 1e-06

VMEM = pl.BlockSpec(memory_space=pltpu.VMEM)
SMEM = pl.BlockSpec(memory_space=pltpu.SMEM)
ANY = pl.BlockSpec(memory_space=pl.ANY)
NT = (((1,), (1,)), ((), ()))
MIB = 1 << 20


def call(kernel, outs, args, mib, flops=0, scratch=(), specs=None, out_specs=None):
    n_bytes = sum(a.size * a.dtype.itemsize for a in args)
    return pl.pallas_call(
        kernel,
        out_shape=outs,
        in_specs=specs or [VMEM] * len(args),
        out_specs=out_specs or jax.tree.map(lambda _: VMEM, outs),
        scratch_shapes=list(scratch),
        compiler_params=pltpu.CompilerParams(vmem_limit_bytes=mib * MIB),
        cost_estimate=pl.CostEstimate(flops=flops, bytes_accessed=n_bytes, transcendentals=0),
    )(*args)


def place():
    s, v = lax.axis_index("seq"), lax.axis_index("vocab")
    return s, lax.div(s, Y), lax.rem(s, Y), v, lax.div(v, C), lax.rem(v, C)


def swap_z(z, k, Z):
    return jnp.bitwise_xor(z, k) if Z & (Z - 1) == 0 else lax.rem(z + (Z - k), Z)


def slots_of(row):
    tok = row.shape[1]
    upto = lax.broadcasted_iota(jnp.int32, (tok, tok), 0) <= lax.broadcasted_iota(jnp.int32, (tok, tok), 1)
    row = row.astype(jnp.float32)
    count = jnp.dot(jnp.broadcast_to(row, (8, tok)), upto.astype(jnp.float32), preferred_element_type=jnp.float32)[0:1]
    slots = lax.broadcasted_iota(jnp.int32, (CAP, tok), 0).astype(jnp.float32)
    return ((count - 1.0) == slots) & (row == 1.0)


def exact_dot(a, b, dims):
    return lax.dot_general(a, b, dims, precision=lax.Precision.HIGHEST, preferred_element_type=jnp.float32)


def select_kernel(mask_ref, q_ref, q_out, blk_out):
    s, _, y, _, _, _ = place()
    tok = mask_ref.shape[1]
    block = lax.shift_right_logical(lax.broadcasted_iota(jnp.int32, (CAP, tok), 1), SHIFT).astype(jnp.float32)
    for which in range(2):
        pick = jnp.where(slots_of(mask_ref[pl.ds(s if which == 0 else s + 1 - 2 * y, 1), :]), 1.0, 0.0)
        blk_out[which] = jnp.broadcast_to(jnp.sum(pick * block, axis=1, keepdims=True), (CAP, LANES))
        if which == 0:
            pick = pick.astype(jnp.bfloat16)
            q_out[...] = jnp.dot(pick, q_ref[...], preferred_element_type=jnp.float32).astype(jnp.bfloat16)


def residual_kernel(Z, mask_ref, target_ref, res_ref, after_ref, res_out, target_out):
    s, z, y, _, _, c = place()
    pick = jnp.where(slots_of(mask_ref[pl.ds(s, 1), :]), 1.0, 0.0).astype(jnp.bfloat16)
    res_out[...] = jnp.dot(pick, res_ref[...], preferred_element_type=jnp.float32).astype(jnp.bfloat16)
    wide = target_out.shape[1]
    lane = lax.broadcasted_iota(jnp.int32, (8, wide), 1)
    found = jnp.zeros((8, wide), jnp.float32)
    for p, (k, other) in enumerate(row_order(Z)):
        src = swap_z(z, k, Z) * Y + (1 - y if other else y)
        hit = jnp.where(slots_of(mask_ref[pl.ds(src, 1), :]), 1.0, 0.0)
        half = jnp.where(c == 0, hit[:HALF], hit[HALF:])
        hit = jnp.concatenate([half, jnp.zeros((LANES - HALF, half.shape[1]), jnp.float32)], axis=0)
        row = jnp.broadcast_to(target_ref[pl.ds(src, 1), :].astype(jnp.float32), (8, target_ref.shape[1]))
        ids = exact_dot(row, hit, NT)
        ids = jnp.concatenate([ids] + [jnp.zeros((8, LANES), jnp.float32)] * (wide // LANES - 1), axis=1)
        ids = pltpu.roll(ids, p * HALF, 1) if p else ids
        found = jnp.where((lane >= p * HALF) & (lane < (p + 1) * HALF), ids, found)
    target_out[...] = found.astype(jnp.int32)


def stage_kernel(n, after, *refs):
    sems = refs[-1]
    copies = [pltpu.make_async_copy(refs[i], refs[n + i], sems.at[i]) for i in range(n)]
    for copy in copies:
        copy.start()
    for copy in copies:
        copy.wait()


def stage(after, *arrays):
    n = len(arrays)
    return call(
        functools.partial(stage_kernel, n),
        tuple(jax.ShapeDtypeStruct(a.shape, a.dtype) for a in arrays),
        (after, *arrays),
        1,
        scratch=[pltpu.SemaphoreType.DMA((n,))],
        specs=[ANY] * (n + 1),
        out_specs=(ANY,) * n,
    )


def split3(value):
    high = value.astype(jnp.bfloat16).astype(jnp.float32)
    rest = value - high
    mid = rest.astype(jnp.bfloat16).astype(jnp.float32)
    return high, mid, rest - mid


def attend_kernel(n_pieces, heads, kv_heads, S, blk_ref, q_own, q_other, kn_ref, vn_ref, *refs):
    s, z, y, _, _, _ = place()
    pieces, (own_out, own_lse, other_out) = refs[:n_pieces], refs[n_pieces:]
    group = heads // kv_heads
    tok = kn_ref.shape[0]
    per_dev = tok // BLOCK
    scale = HEAD_DIM ** (-0.5)
    lane = lax.broadcasted_iota(jnp.int32, (CAP, LANES), 1)
    key_block = lax.shift_right_logical(lax.broadcasted_iota(jnp.int32, (CAP, tok), 1), SHIFT)
    for which in range(2):
        q_ref = (q_own, q_other)[which]
        slot_block = blk_ref[which][:, :1].astype(jnp.int32)
        row_block = slot_block + (s if which == 0 else s + 1 - 2 * y) * per_dev
        bias = []
        for k in range(n_pieces):
            source = jnp.where(z >= k, s - k * Y, S)
            seen = (key_block + source * per_dev) < row_block
            bias.append(jnp.concatenate([jnp.where(seen, 0.0, very_low)] * group, axis=0))
        if which == 0:
            bias.append(jnp.concatenate([jnp.where(key_block == slot_block, 0.0, very_low)] * group, axis=0))
        lse_all = jnp.zeros((CAP, LANES), jnp.float32)
        for g in range(kv_heads):
            cols = slice(g * HEAD_DIM, (g + 1) * HEAD_DIM)
            q_g = jnp.concatenate(
                [q_ref[:, (g * group + h) * HEAD_DIM : (g * group + h + 1) * HEAD_DIM] for h in range(group)], axis=0
            )
            keys = [p[0][:, cols] for p in pieces]
            values = [p[1][:, cols] for p in pieces]
            if which == 0:
                keys.append(kn_ref[:, cols])
                values.append(vn_ref[:, cols])
            scores = [
                lax.dot_general(q_g, k, NT, preferred_element_type=jnp.float32) * scale + b for k, b in zip(keys, bias)
            ]
            top = jnp.max(functools.reduce(jnp.maximum, scores), axis=1, keepdims=True)
            weights = [jnp.exp(score - top) for score in scores]
            total = jnp.sum(functools.reduce(jnp.add, weights), axis=1, keepdims=True)
            mixed = functools.reduce(
                jnp.add,
                [jnp.dot(w.astype(jnp.bfloat16), v, preferred_element_type=jnp.float32) for w, v in zip(weights, values)],
            )
            mixed = mixed / total
            lse = top + jnp.log(total)
            for h in range(group):
                head = g * group + h
                rows = slice(h * CAP, (h + 1) * CAP)
                at = slice(head * HEAD_DIM, (head + 1) * HEAD_DIM)
                lse_all = jnp.where(lane == head, lse[rows], lse_all)
                if which == 0:
                    own_out[:, at] = mixed[rows]
                else:
                    other_out[:, at] = mixed[rows].astype(jnp.bfloat16)
        if which == 0:
            own_lse[...] = lse_all
        else:
            high, mid, low = split3(lse_all)
            packed = high + pltpu.roll(mid, 32, 1) + pltpu.roll(low, 64, 1)
            other_out[:, heads * HEAD_DIM :] = packed.astype(jnp.bfloat16)


def project_kernel(heads, own_ref, lse_ref, got_ref, w_ref, mine_out, theirs_out):
    _, _, _, _, _, c = place()
    packed = got_ref[:, heads * HEAD_DIM :].astype(jnp.float32)
    got_lse = packed + pltpu.roll(packed, LANES - 32, 1) + pltpu.roll(packed, LANES - 64, 1)
    own_lse = lse_ref[...]
    top = jnp.maximum(own_lse, got_lse)
    w_own, w_got = jnp.exp(own_lse - top), jnp.exp(got_lse - top)
    total = w_own + w_got
    w_own, w_got = w_own / total, w_got / total
    parts = []
    for h in range(heads):
        at = slice(h * HEAD_DIM, (h + 1) * HEAD_DIM)
        joined = own_ref[:, at] * w_own[:, h : h + 1] + got_ref[:, at].astype(jnp.float32) * w_got[:, h : h + 1]
        parts.append(joined.astype(jnp.bfloat16))
    attention = jnp.concatenate(parts, axis=1)
    first = c == 0
    width = w_ref.shape[1]
    step = min(1024, width)
    for j in range(0, width, step):
        out = jnp.dot(attention, w_ref[:, j : j + step], preferred_element_type=jnp.float32)
        upper, lower = out[:HALF], out[HALF:]
        mine_out[:, j : j + step] = jnp.where(first, upper, lower)
        theirs_out[:, j : j + step] = jnp.where(first, lower, upper).astype(jnp.bfloat16)


def norm_kernel(share, mine_ref, res_ref, gain_ref, *refs):
    _, _, _, _, x, c = place()
    *got, own_out, normed = refs
    res = res_ref[...].astype(jnp.float32)
    hidden = mine_ref[...]
    for ref in got:
        hidden = hidden + ref[...].astype(jnp.float32)
    hidden = jnp.where(c == 0, res[:HALF], res[HALF:]) + hidden
    squares = jnp.sum(hidden * hidden, axis=1, keepdims=True)
    normed[...] = hidden * lax.rsqrt(squares / D + norm_eps) * gain_ref[...]
    own_out[...] = normed[:, pl.ds(pl.multiple_of(x * share, LANES), share)].astype(jnp.bfloat16)


def row_groups(Z):
    return [g for g in (list(range(min(2, Z))), list(range(2, Z))) if g]


def row_order(Z):
    return [(k, other) for group in row_groups(Z) for other in (False, True) for k in group]


def logits_kernel(mixed, X, Z, V, target_ref, *refs):
    s, z, y, v, x, c = place()
    share = refs[0].shape[1]
    sizes = [len(g) for g in row_groups(Z)]
    n_rows = Y * Z * HALF
    n_refs = (3 if mixed else X) * len(sizes)
    pieces, (w_own, w_other, out_ref, *rows) = refs[:n_refs], refs[n_refs:]
    base = 0
    for i, size in enumerate(sizes):
        n = size * HALF
        if mixed:
            column, step1, step2 = pieces[3 * i : 3 * i + 3]
            near, far = rows
            near[base : base + n] = column[...]
            far[base + n : base + 2 * n] = step2[n:]

            @pl.when(c == 0)
            def _(base=base, n=n, step1=step1, step2=step2):
                near[base + n : base + 2 * n] = step2[:n]
                far[base : base + n] = step1[...]

            @pl.when(c != 0)
            def _(base=base, n=n, step1=step1, step2=step2):
                near[base + n : base + 2 * n] = step1[...]
                far[base : base + n] = step2[:n]
        else:
            for k in range(X):
                rows[k][base : base + Y * n] = pieces[X * i + k][...]
        base += Y * n
    logits = []
    for w in (w_own, w_other):
        total = None
        for k in range(X):
            at = pl.multiple_of(lax.rem(x + (X - k), X) * share, LANES)
            part = lax.dot_general(w[:, pl.ds(at, share)], rows[k][...], NT, preferred_element_type=jnp.float32)
            total = part if total is None else total + part
        logits.append(total)
    vocab_rows = w_own.shape[0]
    starts = [(s * V + v) * vocab_rows, (s * V + v + 1 - 2 * c) * vocab_rows]
    top = jnp.maximum(jnp.max(logits[0], axis=0, keepdims=True), jnp.max(logits[1], axis=0, keepdims=True))
    summed = 0.0
    picked = 0.0
    wanted = target_ref[0:1, :n_rows]
    for start, lg in zip(starts, logits):
        ids = lax.broadcasted_iota(jnp.int32, lg.shape, 0)
        summed = summed + jnp.sum(jnp.exp(lg - top), axis=0, keepdims=True)
        picked = picked + jnp.sum(jnp.where(ids == wanted - start, lg, 0.0), axis=0, keepdims=True)
    lse = top + jnp.log(summed)
    wide = target_ref.shape[1]
    pad = [jnp.zeros((1, wide - n_rows), jnp.float32)] if wide > n_rows else []
    lse = jnp.broadcast_to(jnp.concatenate([lse, *pad], axis=1), (8, wide))
    picked = jnp.broadcast_to(jnp.concatenate([picked, *pad], axis=1), (8, wide))
    lane = lax.broadcasted_iota(jnp.int32, (8, LANES), 1)
    for p, (k, other) in enumerate(row_order(Z)):
        a = pltpu.roll(lse, (wide - p * HALF) % wide, 1)[:, :LANES]
        b = pltpu.roll(picked, (wide - p * HALF + HALF) % wide, 1)[:, :LANES]
        row = jnp.where(lane < HALF, a, b)[0:1]
        first = (swap_z(z, k, Z) * Y + (1 - y if other else y)) * V
        for i in range(V):
            out_ref[first + i] = row


def loss_kernel(levels_ref, mask_ref, got_ref, out_ref):
    s, _, _, _, _, _ = place()
    got = got_ref[...]
    tok = mask_ref.shape[1]
    core = lax.rem(lax.broadcasted_iota(jnp.int32, got.shape, 0), C)
    lane = lax.broadcasted_iota(jnp.int32, (8, LANES), 1)
    nll = jnp.zeros((8, LANES), jnp.float32)
    for half in range(C):
        here = core == half
        best = jnp.max(jnp.where(here, got, -jnp.inf), axis=0, keepdims=True)
        total = jnp.sum(jnp.where(here, jnp.exp(got - best), 0.0), axis=0, keepdims=True)
        picked = jnp.broadcast_to(jnp.sum(jnp.where(here, got, 0.0), axis=0, keepdims=True), (8, LANES))
        value = best + jnp.log(total) - pltpu.roll(picked, LANES - HALF, 1)
        value = pltpu.roll(value, half * HALF, 1) if half else value
        nll = jnp.where((lane >= half * HALF) & (lane < (half + 1) * HALF), value, nll)
    chosen = jnp.where(slots_of(mask_ref[pl.ds(s, 1), :]), 1.0, 0.0)
    chosen = jnp.concatenate([chosen, jnp.zeros((LANES - CAP, tok), jnp.float32)], axis=0)
    token_nll = exact_dot(nll, chosen, (((1,), (0,)), ((), ())))[0:1]
    block = lax.shift_right_logical(lax.broadcasted_iota(jnp.int32, (1, tok), 1), SHIFT)
    weight = jnp.ones((1, tok), jnp.float32)
    for b in range(tok // BLOCK):
        weight = jnp.where(block == b, (levels_ref[s * (tok // BLOCK) + b] + 1).astype(jnp.float32), weight)
    out_ref[...] = token_nll / weight


def shards(
    q_noised,
    key_clean,
    value_clean,
    key_noised,
    value_noised,
    out_weight,
    residual,
    norm_gain,
    head_weight,
    targets,
    mask_flags,
    levels,
):
    tok_rows, q_width = q_noised.shape
    width = residual.shape[1]
    heads_local = q_width // HEAD_DIM
    kv_local = key_clean.shape[1] // HEAD_DIM
    vocab_rows = head_weight.shape[0]
    S = lax.axis_size("seq")
    V = lax.axis_size("vocab")
    X = V // C
    Z = S // Y
    share = width // X
    every = [(zi, yi, xi, ci) for zi in range(Z) for yi in range(Y) for xi in range(X) for ci in range(C)]

    def permute(block, to):
        def dev(zi, yi, xi, ci):
            return ((zi * Y + yi) * X + xi) * C + ci

        return lax.ppermute(block, ("seq", "vocab"), [(dev(*e), dev(*to(*e))) for e in every if to(*e)[0] < Z])

    def core_flip(block):
        return permute(block, lambda a, b, e, f: (a, b, e, 1 - f))

    def x_shift(block, k):
        return permute(block, lambda a, b, e, f: (a, b, (e + k) % X, f))

    def y_flip(block):
        return permute(block, lambda a, b, e, f: (a, 1 - b, e, f))

    def z_up(block, k):
        return permute(block, lambda a, b, e, f: (a + k, b, e, f))

    def z_swap(block, k):
        paired = Z & (Z - 1) == 0
        return permute(block, lambda a, b, e, f: (a ^ k if paired else (a + k) % Z, b, e, f))

    def mixed_flip(block, x_core):
        return permute(block, lambda a, b, e, f: (a, b, 1 - e, f) if f == x_core else (a, 1 - b, e, f))

    def struct(*shape, dtype=jnp.bfloat16):
        return jax.ShapeDtypeStruct(shape, dtype)

    all_mask = mask_flags.reshape(S, tok_rows)
    own_kv = jnp.stack([key_clean, value_clean])
    pieces = [own_kv] + [z_up(own_kv, k) for k in range(1, Z)]
    queries, slot_blocks = call(
        select_kernel, (struct(CAP, q_width), struct(2, CAP, LANES, dtype=jnp.float32)), (all_mask, q_noised), 8
    )
    other_queries = y_flip(queries)
    other_head = core_flip(head_weight)
    keys_here, values_here, staged_out = stage(queries, key_noised, value_noised, out_weight)
    own_sum, own_lse, other_sum = call(
        functools.partial(attend_kernel, Z, heads_local, kv_local, S),
        (
            struct(CAP, q_width, dtype=jnp.float32),
            struct(CAP, LANES, dtype=jnp.float32),
            struct(CAP, q_width + LANES),
        ),
        (slot_blocks, queries, other_queries, keys_here, values_here, *pieces),
        16,
    )
    got_sum = y_flip(other_sum)
    mine, theirs = call(
        functools.partial(project_kernel, heads_local),
        (struct(HALF, width, dtype=jnp.float32), struct(HALF, width)),
        (own_sum, own_lse, got_sum, staged_out),
        16,
    )

    mine = mine + core_flip(theirs).astype(jnp.float32)
    sent = mine.astype(jnp.bfloat16)
    n_rows = Y * Z * HALF
    wide = -(-n_rows // LANES) * LANES
    residual_sel, row_targets = call(
        functools.partial(residual_kernel, Z),
        (struct(CAP, width), struct(8, wide, dtype=jnp.int32)),
        (all_mask, targets.reshape(S, tok_rows), residual, theirs),
        8,
    )
    own = call(
        functools.partial(norm_kernel, share),
        struct(HALF, share),
        (mine, residual_sel, norm_gain.reshape(1, width), *[x_shift(sent, k) for k in range(1, X)]),
        8,
        scratch=[pltpu.VMEM((HALF, width), jnp.float32)],
    )

    slabs = [own]
    for k in range(1, Z):
        slabs.append(z_swap(own, k))
    mixed = X == Y
    rows = []
    for group in row_groups(Z):
        n = len(group) * HALF
        column = jnp.stack([slabs[k] for k in group])
        if mixed:
            step1 = mixed_flip(column, 0)
            both = jnp.stack([column, step1])
            step2 = mixed_flip(both, 1)
            rows += [column.reshape(n, share), step1.reshape(n, share), step2.reshape(Y * n, share)]
        else:
            pair = jnp.stack([column, y_flip(column)])
            rows += [pair.reshape(Y * n, share)] + [x_shift(pair, k).reshape(Y * n, share) for k in range(1, X)]
    staged = stage(own, head_weight, other_head)
    send = call(
        functools.partial(logits_kernel, mixed, X, Z, V),
        struct(S * V, 1, LANES, dtype=jnp.float32),
        (row_targets, *rows, *staged),
        24,
        4 * n_rows * width * vocab_rows,
        [pltpu.VMEM((n_rows, share), jnp.bfloat16)] * X,
    ).reshape(S * V, LANES)
    got = lax.all_to_all(send, ("seq", "vocab"), 0, 0, tiled=True)
    loss = call(
        loss_kernel, struct(1, tok_rows, dtype=jnp.float32), (levels, all_mask, got), 4, specs=[SMEM, VMEM, VMEM]
    )
    return loss.reshape(tok_rows)


def solution(mesh):
    in_specs = (
        P("seq", "vocab"),
        P("seq", "vocab"),
        P("seq", "vocab"),
        P("seq", "vocab"),
        P("seq", "vocab"),
        P("vocab", None),
        P("seq", None),
        P(),
        P(("seq", "vocab"), None),
        P(),
        P(),
        P(),
    )
    return jax.shard_map(shards, mesh=mesh, in_specs=in_specs, out_specs=P("seq"), check_vma=False)
```

time: 101 us -> 80.5 us (0.80)
  Pallas kernels: 24.9 us -> 11.2 us
  blocking collectives: 0 us -> 11.5 us
  local copies, waits for them, and re-layouts: 13.2 us -> 6.72 us
  starting transfers between devices: 28.6 us -> 23.5 us
  other arithmetic: 6.11 us -> 1.06 us
  waiting for transfers between devices: 27.4 us -> 26 us
    pallas_call x6 -> x9, Pallas kernels: 24.9 us -> 11.2 us  [call(): pl.pallas_call(kernel, out_shape=outs, in_specs=specs or [VMEM] * len(arg...]
    all_to_all x0 -> x1, blocking collectives: none -> 11.5 us  [shards(): got = lax.all_to_all(send, ('seq', 'vocab'), 0, 0, tiled=True)]
    all_to_all x1 -> x0, waiting for transfers between devices: 6.92 us -> none  [shards(): lax.all_to_all(send, ('seq', 'vocab'), 0, 0, tiled=True)]
    all_to_all x1 -> x0, starting transfers between devices: 6.36 us -> none  [shards(): lax.all_to_all(send, ('seq', 'vocab'), 0, 0, tiled=True)]
    ppermute x15, waiting for transfers between devices: 20.5 us -> 26 us  [permute(): lax.ppermute(block, ('seq', 'vocab'), [(dev(*e), dev(*to(*e))) for e in e...]
    unnamed x24, local copies, waits for them, and re-layouts: 10.9 us -> 6.72 us
    eq x3 -> x0, other arithmetic: 1.46 us -> none  [the longest x1 0.76 us: shards(): my_mask[None, :] == 1]
    another operation x7 -> x4, other arithmetic: 1.36 us -> 0.13 us  [shards(): both = jnp.stack([column, step1])]
  transfers between devices with their start and end apart: 16 -> 15, of which waited for: 7 -> 8; matrix products, arithmetic and copies ran while one was open for 7% -> 1% of each run, Pallas kernels for 20% -> 8%
where the time goes in v4:
time: 80.5 us; the launch traced here: 80.1 us
  waiting for transfers between devices  26 us (32%)
  starting transfers between devices  23.5 us (29%)
  blocking collectives  11.5 us (14%)
  Pallas kernels  11.2 us (14%)
  local copies, waits for them, and re-layouts  6.72 us (8%)
  other arithmetic  1.06 us (1%)
    ppermute x15, waiting for transfers between devices, permute(): lax.ppermute(block, ('seq', 'vocab'), [(dev(*e), dev(*to(*e))) for e in e...  26 us
    ppermute x15, starting transfers between devices, permute(): lax.ppermute(block, ('seq', 'vocab'), [(dev(*e), dev(*to(*e))) for e in e...  23.5 us
    all_to_all x1, blocking collectives, shards(): got = lax.all_to_all(send, ('seq', 'vocab'), 0, 0, tiled=True)  11.5 us
    pallas_call x9, Pallas kernels, call(): pl.pallas_call(kernel, out_shape=outs, in_specs=specs or [VMEM] * len(arg...  11.2 us
    unnamed x24, local copies, waits for them, and re-layouts  6.72 us
  transfers between devices with their start and end apart: 15, of which 8 were waited for; matrix products, arithmetic and copies ran while one was open for 1% of the time, Pallas kernels for 8%

profile of v4, /device:TPU:0, one launch (start us, length us, event | category | flops | bytes accessed | tf_op | source)
XLA Modules:
  0.0 80.1 jit_solution(4531295159413577242)
XLA Ops:
  0.5 0.9 %pad_maximum_fusion.4.refs_0_ = bf16[2,128,256]{2,1,0:T(8,128)(2,1)S(1)} fusion(bf16[1,128,256]{2,1,0:T(8,128)(2,1)} %bitcast.43, bf16[1,128,256]{2,1,0:T(8,128)(2,1)} %bitcast.44), kind=kLoop, calls=%fused_computation.5 | loop fusion | flops 65536 | bytes 262144 | tf_op jit(solution)/shard_map/stack | solution.py:375
  1.4 4.5 %collective-permute-start.1 = (bf16[2,128,256]{2,1,0:T(8,128)(2,1)S(1)}, bf16[2,128,256]{2,1,0:T(8,128)(2,1)S(1)}, u32[]{:S(2)}, u32[]{:S(2)}) collective-permute-start(bf16[2,128,256]{2,1,0:T(8,128)(2,1)S(1)} %pad_maximum_fusion.4.refs_0_), channel_id=1, source_target_pairs={{0,8},{1,9},{2,10},{3,11},{4,12},{5,13},{6,14},{7,15},{8,16},{9,17... | collective-permute-start | bytes 393224 | tf_op jit(solution)/shard_map/ppermute | solution.py:350
  5.9 4.5 %collective-permute-start.2 = (bf16[2,128,256]{2,1,0:T(8,128)(2,1)S(1)}, bf16[2,128,256]{2,1,0:T(8,128)(2,1)S(1)}, u32[]{:S(2)}, u32[]{:S(2)}) collective-permute-start(bf16[2,128,256]{2,1,0:T(8,128)(2,1)S(1)} %pad_maximum_fusion.4.refs_0_), channel_id=1, source_target_pairs={{0,16},{1,17},{2,18},{3,19},{4,20},{5,21},{6,22},{7,23},{8,24},{9,... | collective-permute-start | bytes 393224 | tf_op jit(solution)/shard_map/ppermute | solution.py:350
  10.4 1.3 %collective-permute-start.3 = (bf16[2,128,256]{2,1,0:T(8,128)(2,1)S(1)}, bf16[2,128,256]{2,1,0:T(8,128)(2,1)S(1)}, u32[]{:S(2)}, u32[]{:S(2)}) collective-permute-start(bf16[2,128,256]{2,1,0:T(8,128)(2,1)S(1)} %pad_maximum_fusion.4.refs_0_), channel_id=1, source_target_pairs={{0,24},{1,25},{2,26},{3,27},{4,28},{5,29},{6,30},{7,31}} | collective-permute-start | bytes 393224 | tf_op jit(solution)/shard_map/ppermute | solution.py:350
  11.7 0.9 %copy-done.2 = bf16[128,1024]{1,0:T(8,128)(2,1)S(1)} copy-done((bf16[128,1024]{1,0:T(8,128)(2,1)S(1)}, bf16[128,1024]{1,0:T(8,128)(2,1)}, u32[]{:S(2)}) %copy-start.2) | copy-done | bytes 262168
  13.7 1.5 %collective-permute-start = (bf16[48,1024]{1,0:T(8,128)(2,1)S(1)}, bf16[48,1024]{1,0:T(8,128)(2,1)S(1)}, u32[]{:S(2)}, u32[]{:S(2)}) collective-permute-start(bf16[48,1024]{1,0:T(8,128)(2,1)S(1)} %get-tuple-element.20.after.q_own), channel_id=1, source_target_pairs={{0,4},{1,5},{2,6},{3,7},{4,0},{5,1},{6,2},{7,3},{8,12},{9,13},{10,... | collective-permute-start | bytes 294920 | tf_op jit(solution)/shard_map/ppermute | solution.py:350
  15.2 3.4 %copy-done = bf16[1024,4096]{1,0:T(8,128)(2,1)S(1)} copy-done((bf16[1024,4096]{1,0:T(8,128)(2,1)S(1)}, bf16[1024,4096]{1,0:T(8,128)(2,1)}, u32[]{:S(2)}) %copy-start) | copy-done | bytes 8388632
  18.6 0.8 %copy-done.3 = bf16[128,256]{1,0:T(8,128)(2,1)S(1)} copy-done((bf16[128,256]{1,0:T(8,128)(2,1)S(1)}, bf16[128,256]{1,0:T(8,128)(2,1)}, u32[]{:S(2)}) %copy-start.3) | copy-done | bytes 65560
  19.4 0.8 %copy-done.4 = bf16[128,256]{1,0:T(8,128)(2,1)S(1)} copy-done((bf16[128,256]{1,0:T(8,128)(2,1)S(1)}, bf16[128,256]{1,0:T(8,128)(2,1)}, u32[]{:S(2)}) %copy-start.4) | copy-done | bytes 65560
  20.3 0.7 shard_map.119
  21.0 1.4 %shard_map.120 = (f32[48,1024]{1,0:T(8,128)S(1)}, f32[48,128]{1,0:T(8,128)S(1)}, bf16[48,1152]{1,0:T(8,128)(2,1)S(1)}) custom-call(f32[2,48,128]{2,1,0:T(8,128)S(1)} %get-tuple-element.19.blk_ref, bf16[48,1024]{1,0:T(8,128)(2,1)S(1)} %get-tuple-element.20.after.q_own, bf16[48,1024]{1,0:T(8,128)(2,1)S(1)} %collective-permute-done.q_other, ...), custom_call_target="tpu_custom_call" | custom-call | bytes 901120 | tf_op jit(solution)/shard_map/pallas_call | solution.py:33
  23.1 4.2 %collective-permute-done.4.got_ref = bf16[48,1152]{1,0:T(8,128)(2,1)S(1)} collective-permute-done((bf16[48,1152]{1,0:T(8,128)(2,1)S(1)}, bf16[48,1152]{1,0:T(8,128)(2,1)S(1)}, u32[]{:S(2)}, u32[]{:S(2)}) %collective-permute-start.4) | collective-permute-done | bytes 110624 | tf_op jit(solution)/shard_map/ppermute | solution.py:350
  27.3 1.7 %shard_map.121 = (f32[24,4096]{1,0:T(8,128)S(1)}, bf16[24,4096]{1,0:T(8,128)(2,1)S(1)}) custom-call(f32[48,1024]{1,0:T(8,128)S(1)} %get-tuple-element.23.own_ref, f32[48,128]{1,0:T(8,128)S(1)} %get-tuple-element.24.lse_ref, bf16[48,1152]{1,0:T(8,128)(2,1)S(1)} %collective-permute-done.4.got_ref, bf16[1024,4096]{1,0:T(8,128)(2,1)S(1)} %get-tuple-element.26.w_ref), custom_call_target="tpu_custom_call" | custom-call | bytes 8720384 | tf_op jit(solution)/shard_map/pallas_call | solution.py:33
  29.1 1.4 %collective-permute-done.5 = bf16[24,4096]{1,0:T(8,128)(2,1)S(1)} collective-permute-done((bf16[24,4096]{1,0:T(8,128)(2,1)S(1)}, bf16[24,4096]{1,0:T(8,128)(2,1)S(1)}, u32[]{:S(2)}, u32[]{:S(2)}) %collective-permute-start.5) | collective-permute-done | bytes 196640 | tf_op jit(solution)/shard_map/ppermute | solution.py:350
  30.6 1.6 %collective-permute-start.6 = (bf16[24,4096]{1,0:T(8,128)(2,1)S(1)}, bf16[24,4096]{1,0:T(8,128)(2,1)S(1)}, u32[]{:S(2)}, u32[]{:S(2)}) collective-permute-start(bf16[24,4096]{1,0:T(8,128)(2,1)S(1)} %get-tuple-element.33), channel_id=1, source_target_pairs={{0,2},{1,3},{2,0},{3,1},{4,6},{5,7},{6,4},{7,5},{8,10},{9,11},{10,... | collective-permute-start | bytes 589832 | tf_op jit(solution)/shard_map/ppermute | solution.py:350
  32.1 1.2 %shard_map.122 = (bf16[48,4096]{1,0:T(8,128)(2,1)S(1)}, s32[8,256]{1,0:T(8,128)S(1)}) custom-call(s32[8,128]{1,0:T(8,128)S(1)} %bitcast.36, s32[8,128]{1,0:T(8,128)S(1)} %bitcast.39, bf16[128,4096]{1,0:T(8,128)(2,1)S(1)} %copy-done.1, bf16[24,4096]{1,0:T(8,128)(2,1)S(1)} %get-tuple-element.27.after_ref), custom_call_target="tpu_custom_call" | custom-call | bytes 1253376 | tf_op jit(solution)/shard_map/pallas_call | solution.py:33
  33.3 4.3 %collective-permute-done.6.refs_0_ = bf16[24,4096]{1,0:T(8,128)(2,1)S(1)} collective-permute-done((bf16[24,4096]{1,0:T(8,128)(2,1)S(1)}, bf16[24,4096]{1,0:T(8,128)(2,1)S(1)}, u32[]{:S(2)}, u32[]{:S(2)}) %collective-permute-start.6) | collective-permute-done | bytes 196640 | tf_op jit(solution)/shard_map/ppermute | solution.py:350
  38.0 1.3 %collective-permute-start.11 = (bf16[24,2048]{1,0:T(8,128)(2,1)S(1)}, bf16[24,2048]{1,0:T(8,128)(2,1)S(1)}, u32[]{:S(2)}, u32[]{:S(2)}) collective-permute-start(bf16[24,2048]{1,0:T(8,128)(2,1)S(1)} %shard_map.123.after), channel_id=1, source_target_pairs={{0,24},{1,25},{2,26},{3,27},{4,28},{5,29},{6,30},{7,31},{8,16},{9,... | collective-permute-start | bytes 294920 | tf_op jit(solution)/shard_map/ppermute | solution.py:350
  39.2 2.2 %collective-permute-start.7 = (bf16[24,2048]{1,0:T(8,128)(2,1)S(1)}, bf16[24,2048]{1,0:T(8,128)(2,1)S(1)}, u32[]{:S(2)}, u32[]{:S(2)}) collective-permute-start(bf16[24,2048]{1,0:T(8,128)(2,1)S(1)} %shard_map.123.after), channel_id=1, source_target_pairs={{0,8},{1,9},{2,10},{3,11},{4,12},{5,13},{6,14},{7,15},{8,0},{9,1},... | collective-permute-start | bytes 294920 | tf_op jit(solution)/shard_map/ppermute | solution.py:350
  41.4 4.7 %collective-permute-done.10 = bf16[24,2048]{1,0:T(8,128)(2,1)S(1)} collective-permute-done((bf16[24,2048]{1,0:T(8,128)(2,1)S(1)}, bf16[24,2048]{1,0:T(8,128)(2,1)S(1)}, u32[]{:S(2)}, u32[]{:S(2)}) %collective-permute-start.10) | collective-permute-done | bytes 98336 | tf_op jit(solution)/shard_map/ppermute | solution.py:350
  46.2 1.6 %collective-permute-start.12 = (bf16[2,24,2048]{2,1,0:T(8,128)(2,1)S(1)}, bf16[2,24,2048]{2,1,0:T(8,128)(2,1)S(1)}, u32[]{:S(2)}, u32[]{:S(2)}) collective-permute-start(bf16[2,24,2048]{2,1,0:T(8,128)(2,1)S(1)} %get-tuple-element.36), channel_id=1, source_target_pairs={{0,2},{1,5},{2,0},{3,7},{4,6},{5,1},{6,4},{7,3},{8,10},{9,13},{10,... | collective-permute-start | bytes 589832 | tf_op jit(solution)/shard_map/ppermute | solution.py:350
  47.8 1.0 %collective-permute-start.8 = (bf16[2,24,2048]{2,1,0:T(8,128)(2,1)S(1)}, bf16[2,24,2048]{2,1,0:T(8,128)(2,1)S(1)}, u32[]{:S(2)}, u32[]{:S(2)}) collective-permute-start(bf16[2,24,2048]{2,1,0:T(8,128)(2,1)S(1)} %get-tuple-element.38), channel_id=1, source_target_pairs={{0,2},{1,5},{2,0},{3,7},{4,6},{5,1},{6,4},{7,3},{8,10},{9,13},{10,... | collective-permute-start | bytes 589832 | tf_op jit(solution)/shard_map/ppermute | solution.py:350
  48.8 3.2 %collective-permute-done.12 = bf16[2,24,2048]{2,1,0:T(8,128)(2,1)S(1)} collective-permute-done((bf16[2,24,2048]{2,1,0:T(8,128)(2,1)S(1)}, bf16[2,24,2048]{2,1,0:T(8,128)(2,1)S(1)}, u32[]{:S(2)}, u32[]{:S(2)}) %collective-permute-start.12) | collective-permute-done | bytes 196640 | tf_op jit(solution)/shard_map/ppermute | solution.py:350
  52.0 1.2 %collective-permute-start.13 = (bf16[2,2,24,2048]{3,2,1,0:T(8,128)(2,1)S(1)}, bf16[2,2,24,2048]{3,2,1,0:T(8,128)(2,1)S(1)}, u32[]{:S(2)}, u32[]{:S(2)}) collective-permute-start(bf16[2,2,24,2048]{3,2,1,0:T(8,128)(2,1)S(1)} %pad_maximum_fusion.1), channel_id=1, source_target_pairs={{0,4},{1,3},{2,6},{3,1},{4,0},{5,7},{6,2},{7,5},{8,12},{9,11},{10,... | collective-permute-start | bytes 1179656 | tf_op jit(solution)/shard_map/ppermute | solution.py:350
  53.2 1.3 %collective-permute-done.8 = bf16[2,24,2048]{2,1,0:T(8,128)(2,1)S(1)} collective-permute-done((bf16[2,24,2048]{2,1,0:T(8,128)(2,1)S(1)}, bf16[2,24,2048]{2,1,0:T(8,128)(2,1)S(1)}, u32[]{:S(2)}, u32[]{:S(2)}) %collective-permute-start.8) | collective-permute-done | bytes 196640 | tf_op jit(solution)/shard_map/ppermute | solution.py:350
  54.5 1.7 %collective-permute-start.9 = (bf16[2,2,24,2048]{3,2,1,0:T(8,128)(2,1)S(1)}, bf16[2,2,24,2048]{3,2,1,0:T(8,128)(2,1)S(1)}, u32[]{:S(2)}, u32[]{:S(2)}) collective-permute-start(bf16[2,2,24,2048]{3,2,1,0:T(8,128)(2,1)S(1)} %pad_maximum_fusion), channel_id=1, source_target_pairs={{0,4},{1,3},{2,6},{3,1},{4,0},{5,7},{6,2},{7,5},{8,12},{9,11},{10,... | collective-permute-start | bytes 1179656 | tf_op jit(solution)/shard_map/ppermute | solution.py:350
  56.2 1.0 %shard_map.124 = (bf16[592,4096]{1,0:T(8,128)(2,1)S(1)}, bf16[592,4096]{1,0:T(8,128)(2,1)S(1)}) custom-call(bf16[24,2048]{1,0:T(8,128)(2,1)S(1)} %shard_map.123.after, bf16[592,4096]{1,0:T(8,128)(2,1)S(1)} %bitcast.24, bf16[592,4096]{1,0:T(8,128)(2,1)S(1)} %collective-permute-done.14.refs_1_), custom_call_target="tpu_custom_call" | custom-call | bytes 9797632 | tf_op jit(solution)/shard_map/pallas_call | solution.py:33
  57.2 2.6 %collective-permute-done.13 = bf16[2,2,24,2048]{3,2,1,0:T(8,128)(2,1)S(1)} collective-permute-done((bf16[2,2,24,2048]{3,2,1,0:T(8,128)(2,1)S(1)}, bf16[2,2,24,2048]{3,2,1,0:T(8,128)(2,1)S(1)}, u32[]{:S(2)}, u32[]{:S(2)}) %collective-permute-start.13) | collective-permute-done | bytes 393248 | tf_op jit(solution)/shard_map/ppermute | solution.py:350
  59.8 4.2 %collective-permute-done.9 = bf16[2,2,24,2048]{3,2,1,0:T(8,128)(2,1)S(1)} collective-permute-done((bf16[2,2,24,2048]{3,2,1,0:T(8,128)(2,1)S(1)}, bf16[2,2,24,2048]{3,2,1,0:T(8,128)(2,1)S(1)}, u32[]{:S(2)}, u32[]{:S(2)}) %collective-permute-start.9) | collective-permute-done | bytes 393248 | tf_op jit(solution)/shard_map/ppermute | solution.py:350
  64.0 3.2 %shard_map.125 = f32[32,1,128]{2,1,0:T(1,128)S(1)} custom-call(s32[8,256]{1,0:T(8,128)S(1)} %get-tuple-element.28.target_ref, bf16[48,2048]{1,0:T(8,128)(2,1)S(1)} %bitcast.29, bf16[48,2048]{1,0:T(8,128)(2,1)S(1)} %bitcast.31, bf16[96,2048]{1,0:T(8,128)(2,1)S(1)} %bitcast.33, bf16[48,2048]{1,0:T(8,128)(2,1)S(1)} %bitcast.26, bf16[48,2048]{1,0:T(8,128)(2,1)S(1)} %bitcast.28, ...), custom_call_target="tpu_custom_call" | custom-call | flops 1862270976 | bytes 11280384 | tf_op jit(solution)/shard_map/pallas_call | solution.py:33
  67.2 11.5 %all_to_all.8 = f32[32,1,128]{2,1,0:T(1,128)S(1)} all-to-all(f32[32,1,128]{2,1,0:T(1,128)S(1)} %shard_map.125), channel_id=1, replica_groups=mesh['seq'=8,'vocab'=4] {'seq','vocab'}, dimensions={0} | all-to-all | bytes 32768 | tf_op jit(solution)/shard_map/all_to_all | solution.py:444
  78.7 1.3 %shard_map.126 = f32[1,128]{1,0:T(1,128)} custom-call(s32[32]{0:T(128)S(1)} %copy-done.9, s32[8,128]{1,0:T(8,128)S(1)} %bitcast.37, f32[32,128]{1,0:T(8,128)S(1)} %bitcast.34), custom_call_target="tpu_custom_call" | custom-call | bytes 20608 | tf_op jit(solution)/shard_map/pallas_call | solution.py:33
  (39 shorter events, 2.8 us)
Async XLA Ops:
  0.0 56.2 %collective-permute-start.14 = (bf16[592,4096]{1,0:T(8,128)(2,1)}, bf16[592,4096]{1,0:T(8,128)(2,1)S(1)}, u32[]{:S(2)}, u32[]{:S(2)}) collective-permute-start(bf16[592,4096]{1,0:T(8,128)(2,1)} %refs_0_.3), channel_id=1, source_target_pairs={{0,1},{1,0},{2,3},{3,2},{4,5},{5,4},{6,7},{7,6},{8,9},{9,8},{10,11... | collective-permute-start | bytes 14549000 | tf_op jit(solution)/shard_map/ppermute | solution.py:350
  1.4 19.6 %collective-permute-start.1 = (bf16[2,128,256]{2,1,0:T(8,128)(2,1)S(1)}, bf16[2,128,256]{2,1,0:T(8,128)(2,1)S(1)}, u32[]{:S(2)}, u32[]{:S(2)}) collective-permute-start(bf16[2,128,256]{2,1,0:T(8,128)(2,1)S(1)} %pad_maximum_fusion.4.refs_0_), channel_id=1, source_target_pairs={{0,8},{1,9},{2,10},{3,11},{4,12},{5,13},{6,14},{7,15},{8,16},{9,17... | collective-permute-start | bytes 393224 | tf_op jit(solution)/shard_map/ppermute | solution.py:350
  5.9 15.2 %collective-permute-start.2 = (bf16[2,128,256]{2,1,0:T(8,128)(2,1)S(1)}, bf16[2,128,256]{2,1,0:T(8,128)(2,1)S(1)}, u32[]{:S(2)}, u32[]{:S(2)}) collective-permute-start(bf16[2,128,256]{2,1,0:T(8,128)(2,1)S(1)} %pad_maximum_fusion.4.refs_0_), channel_id=1, source_target_pairs={{0,16},{1,17},{2,18},{3,19},{4,20},{5,21},{6,22},{7,23},{8,24},{9,... | collective-permute-start | bytes 393224 | tf_op jit(solution)/shard_map/ppermute | solution.py:350
  10.4 10.7 %collective-permute-start.3 = (bf16[2,128,256]{2,1,0:T(8,128)(2,1)S(1)}, bf16[2,128,256]{2,1,0:T(8,128)(2,1)S(1)}, u32[]{:S(2)}, u32[]{:S(2)}) collective-permute-start(bf16[2,128,256]{2,1,0:T(8,128)(2,1)S(1)} %pad_maximum_fusion.4.refs_0_), channel_id=1, source_target_pairs={{0,24},{1,25},{2,26},{3,27},{4,28},{5,29},{6,30},{7,31}} | collective-permute-start | bytes 393224 | tf_op jit(solution)/shard_map/ppermute | solution.py:350
  11.7 1.0 %copy-start.2 = (bf16[128,1024]{1,0:T(8,128)(2,1)S(1)}, bf16[128,1024]{1,0:T(8,128)(2,1)}, u32[]{:S(2)}) copy-start(bf16[128,1024]{1,0:T(8,128)(2,1)} %q_ref.1) | copy-start | bytes 786436
  12.6 0.7 copy-start.5
  13.7 7.3 %collective-permute-start = (bf16[48,1024]{1,0:T(8,128)(2,1)S(1)}, bf16[48,1024]{1,0:T(8,128)(2,1)S(1)}, u32[]{:S(2)}, u32[]{:S(2)}) collective-permute-start(bf16[48,1024]{1,0:T(8,128)(2,1)S(1)} %get-tuple-element.20.after.q_own), channel_id=1, source_target_pairs={{0,4},{1,5},{2,6},{3,7},{4,0},{5,1},{6,2},{7,3},{8,12},{9,13},{10,... | collective-permute-start | bytes 294920 | tf_op jit(solution)/shard_map/ppermute | solution.py:350
  15.2 3.4 %copy-start = (bf16[1024,4096]{1,0:T(8,128)(2,1)S(1)}, bf16[1024,4096]{1,0:T(8,128)(2,1)}, u32[]{:S(2)}) copy-start(bf16[1024,4096]{1,0:T(8,128)(2,1)} %refs_2_.1) | copy-start | bytes 25165828
  18.6 0.8 %copy-start.3 = (bf16[128,256]{1,0:T(8,128)(2,1)S(1)}, bf16[128,256]{1,0:T(8,128)(2,1)}, u32[]{:S(2)}) copy-start(bf16[128,256]{1,0:T(8,128)(2,1)} %refs_0_.2) | copy-start | bytes 196612
  19.4 0.8 %copy-start.4 = (bf16[128,256]{1,0:T(8,128)(2,1)S(1)}, bf16[128,256]{1,0:T(8,128)(2,1)}, u32[]{:S(2)}) copy-start(bf16[128,256]{1,0:T(8,128)(2,1)} %refs_1_.1) | copy-start | bytes 196612
  22.5 4.8 %collective-permute-start.4 = (bf16[48,1152]{1,0:T(8,128)(2,1)S(1)}, bf16[48,1152]{1,0:T(8,128)(2,1)S(1)}, u32[]{:S(2)}, u32[]{:S(2)}) collective-permute-start(bf16[48,1152]{1,0:T(8,128)(2,1)S(1)} %get-tuple-element.25), channel_id=1, source_target_pairs={{0,4},{1,5},{2,6},{3,7},{4,0},{5,1},{6,2},{7,3},{8,12},{9,13},{10,... | collective-permute-start | bytes 331784 | tf_op jit(solution)/shard_map/ppermute | solution.py:350
  27.3 28.9 %slice-start = ((s8[4849664]{0:T(1024)(128)(4,1)}), s8[4194304]{0:T(1024)(128)(4,1)S(1)}, s32[]{:S(2)}) async-start(s8[4849664]{0:T(1024)(128)(4,1)} %bitcast.23), calls=%async_computation.1 | async-start | bytes 8388608
  27.3 4.8 %copy-start.1 = (bf16[128,4096]{1,0:T(8,128)(2,1)S(1)}, bf16[128,4096]{1,0:T(8,128)(2,1)}, u32[]{:S(2)}) copy-start(bf16[128,4096]{1,0:T(8,128)(2,1)} %res_ref.1) | copy-start | bytes 3145732
  27.3 4.8 %copy-start.6 = (s32[1024]{0:T(1024)S(1)}, s32[1024]{0:T(1024)}, u32[]{:S(2)}) copy-start(s32[1024]{0:T(1024)} %param.22) | copy-start | bytes 12292
  27.3 4.8 %copy-start.8 = (s32[1024]{0:T(1024)S(1)}, s32[1024]{0:T(1024)}, u32[]{:S(2)}) copy-start(s32[1024]{0:T(1024)} %param.21) | copy-start | bytes 12292
  27.3 10.3 %copy-start.7 = (f32[4096]{0:T(1024)S(1)}, f32[4096]{0:T(1024)}, u32[]{:S(2)}) copy-start(f32[4096]{0:T(1024)} %param.19) | copy-start | bytes 49156
  27.3 28.9 %slice-start.1 = ((s8[4849664]{0:T(1024)(128)(4,1)}), s8[655360]{0:T(1024)(128)(4,1)S(1)}, s32[]{:S(2)}) async-start(s8[4849664]{0:T(1024)(128)(4,1)} %bitcast.23), calls=%async_computation.2 | async-start | bytes 1310720
  29.0 1.5 %collective-permute-start.5 = (bf16[24,4096]{1,0:T(8,128)(2,1)S(1)}, bf16[24,4096]{1,0:T(8,128)(2,1)S(1)}, u32[]{:S(2)}, u32[]{:S(2)}) collective-permute-start(bf16[24,4096]{1,0:T(8,128)(2,1)S(1)} %get-tuple-element.27.after_ref), channel_id=1, source_target_pairs={{0,1},{1,0},{2,3},{3,2},{4,5},{5,4},{6,7},{7,6},{8,9},{9,8},{10,11... | collective-permute-start | bytes 589832 | tf_op jit(solution)/shard_map/ppermute | solution.py:350
  30.6 7.0 %collective-permute-start.6 = (bf16[24,4096]{1,0:T(8,128)(2,1)S(1)}, bf16[24,4096]{1,0:T(8,128)(2,1)S(1)}, u32[]{:S(2)}, u32[]{:S(2)}) collective-permute-start(bf16[24,4096]{1,0:T(8,128)(2,1)S(1)} %get-tuple-element.33), channel_id=1, source_target_pairs={{0,2},{1,3},{2,0},{3,1},{4,6},{5,7},{6,4},{7,5},{8,10},{9,11},{10,... | collective-permute-start | bytes 589832 | tf_op jit(solution)/shard_map/ppermute | solution.py:350
  37.9 8.3 %collective-permute-start.10 = (bf16[24,2048]{1,0:T(8,128)(2,1)S(1)}, bf16[24,2048]{1,0:T(8,128)(2,1)S(1)}, u32[]{:S(2)}, u32[]{:S(2)}) collective-permute-start(bf16[24,2048]{1,0:T(8,128)(2,1)S(1)} %shard_map.123.after), channel_id=1, source_target_pairs={{0,16},{1,17},{2,18},{3,19},{4,20},{5,21},{6,22},{7,23},{8,24},{9,... | collective-permute-start | bytes 294920 | tf_op jit(solution)/shard_map/ppermute | solution.py:350
  38.0 8.2 %collective-permute-start.11 = (bf16[24,2048]{1,0:T(8,128)(2,1)S(1)}, bf16[24,2048]{1,0:T(8,128)(2,1)S(1)}, u32[]{:S(2)}, u32[]{:S(2)}) collective-permute-start(bf16[24,2048]{1,0:T(8,128)(2,1)S(1)} %shard_map.123.after), channel_id=1, source_target_pairs={{0,24},{1,25},{2,26},{3,27},{4,28},{5,29},{6,30},{7,31},{8,16},{9,... | collective-permute-start | bytes 294920 | tf_op jit(solution)/shard_map/ppermute | solution.py:350
  39.2 8.5 %collective-permute-start.7 = (bf16[24,2048]{1,0:T(8,128)(2,1)S(1)}, bf16[24,2048]{1,0:T(8,128)(2,1)S(1)}, u32[]{:S(2)}, u32[]{:S(2)}) collective-permute-start(bf16[24,2048]{1,0:T(8,128)(2,1)S(1)} %shard_map.123.after), channel_id=1, source_target_pairs={{0,8},{1,9},{2,10},{3,11},{4,12},{5,13},{6,14},{7,15},{8,0},{9,1},... | collective-permute-start | bytes 294920 | tf_op jit(solution)/shard_map/ppermute | solution.py:350
  46.2 5.7 %collective-permute-start.12 = (bf16[2,24,2048]{2,1,0:T(8,128)(2,1)S(1)}, bf16[2,24,2048]{2,1,0:T(8,128)(2,1)S(1)}, u32[]{:S(2)}, u32[]{:S(2)}) collective-permute-start(bf16[2,24,2048]{2,1,0:T(8,128)(2,1)S(1)} %get-tuple-element.36), channel_id=1, source_target_pairs={{0,2},{1,5},{2,0},{3,7},{4,6},{5,1},{6,4},{7,3},{8,10},{9,13},{10,... | collective-permute-start | bytes 589832 | tf_op jit(solution)/shard_map/ppermute | solution.py:350
  47.8 6.7 %collective-permute-start.8 = (bf16[2,24,2048]{2,1,0:T(8,128)(2,1)S(1)}, bf16[2,24,2048]{2,1,0:T(8,128)(2,1)S(1)}, u32[]{:S(2)}, u32[]{:S(2)}) collective-permute-start(bf16[2,24,2048]{2,1,0:T(8,128)(2,1)S(1)} %get-tuple-element.38), channel_id=1, source_target_pairs={{0,2},{1,5},{2,0},{3,7},{4,6},{5,1},{6,4},{7,3},{8,10},{9,13},{10,... | collective-permute-start | bytes 589832 | tf_op jit(solution)/shard_map/ppermute | solution.py:350
  52.0 7.8 %collective-permute-start.13 = (bf16[2,2,24,2048]{3,2,1,0:T(8,128)(2,1)S(1)}, bf16[2,2,24,2048]{3,2,1,0:T(8,128)(2,1)S(1)}, u32[]{:S(2)}, u32[]{:S(2)}) collective-permute-start(bf16[2,2,24,2048]{3,2,1,0:T(8,128)(2,1)S(1)} %pad_maximum_fusion.1), channel_id=1, source_target_pairs={{0,4},{1,3},{2,6},{3,1},{4,0},{5,7},{6,2},{7,5},{8,12},{9,11},{10,... | collective-permute-start | bytes 1179656 | tf_op jit(solution)/shard_map/ppermute | solution.py:350
  54.5 9.5 %collective-permute-start.9 = (bf16[2,2,24,2048]{3,2,1,0:T(8,128)(2,1)S(1)}, bf16[2,2,24,2048]{3,2,1,0:T(8,128)(2,1)S(1)}, u32[]{:S(2)}, u32[]{:S(2)}) collective-permute-start(bf16[2,2,24,2048]{3,2,1,0:T(8,128)(2,1)S(1)} %pad_maximum_fusion), channel_id=1, source_target_pairs={{0,4},{1,3},{2,6},{3,1},{4,0},{5,7},{6,2},{7,5},{8,12},{9,11},{10,... | collective-permute-start | bytes 1179656 | tf_op jit(solution)/shard_map/ppermute | solution.py:350
  64.0 14.7 %copy-start.9 = (s32[32]{0:T(128)S(1)}, s32[32]{0:T(128)}, u32[]{:S(2)}) copy-start(s32[32]{0:T(128)} %levels_ref.1) | copy-start | bytes 388

commit v5 on v4

--- a/solution.py
+++ b/solution.py
@@ -75,9 +75,17 @@
             q_out[...] = jnp.dot(pick, q_ref[...], preferred_element_type=jnp.float32).astype(jnp.bfloat16)
 
 
-def residual_kernel(Z, mask_ref, target_ref, res_ref, after_ref, res_out, target_out):
+def residual_kernel(Z, levels_ref, mask_ref, target_ref, res_ref, after_ref, res_out, target_out, chosen_out, weight_out):
     s, z, y, _, _, c = place()
-    pick = jnp.where(slots_of(mask_ref[pl.ds(s, 1), :]), 1.0, 0.0).astype(jnp.bfloat16)
+    pick = jnp.where(slots_of(mask_ref[pl.ds(s, 1), :]), 1.0, 0.0)
+    tok = pick.shape[1]
+    chosen_out[...] = jnp.concatenate([pick, jnp.zeros((LANES - CAP, tok), jnp.float32)], axis=0)
+    block = lax.shift_right_logical(lax.broadcasted_iota(jnp.int32, (8, tok), 1), SHIFT)
+    weight = jnp.ones((8, tok), jnp.float32)
+    for b in range(tok // BLOCK):
+        weight = jnp.where(block == b, (levels_ref[s * (tok // BLOCK) + b] + 1).astype(jnp.float32), weight)
+    weight_out[...] = weight
+    pick = pick.astype(jnp.bfloat16)
     res_out[...] = jnp.dot(pick, res_ref[...], preferred_element_type=jnp.float32).astype(jnp.bfloat16)
     wide = target_out.shape[1]
     lane = lax.broadcasted_iota(jnp.int32, (8, wide), 1)
@@ -124,9 +132,15 @@
     return high, mid, rest - mid
 
 
-def attend_kernel(n_pieces, heads, kv_heads, S, blk_ref, q_own, q_other, kn_ref, vn_ref, *refs):
+def attend_kernel(Z, heads, kv_heads, S, blk_ref, q_own, q_other, kn_ref, vn_ref, *refs):
     s, z, y, _, _, _ = place()
-    pieces, (own_out, own_lse, other_out) = refs[:n_pieces], refs[n_pieces:]
+    *pieces, own_out, own_lse, other_out = refs
+    passed = pieces.pop() if Z == 4 else None
+
+    def piece(k, part, cols):
+        block = pieces[k][part][:, cols]
+        return block if passed is None or k != 2 else jnp.where(z == Z - 1, passed[part][:, cols], block)
+
     group = heads // kv_heads
     tok = kn_ref.shape[0]
     per_dev = tok // BLOCK
@@ -138,7 +152,7 @@
         slot_block = blk_ref[which][:, :1].astype(jnp.int32)
         row_block = slot_block + (s if which == 0 else s + 1 - 2 * y) * per_dev
         bias = []
-        for k in range(n_pieces):
+        for k in range(Z):
             source = jnp.where(z >= k, s - k * Y, S)
             seen = (key_block + source * per_dev) < row_block
             bias.append(jnp.concatenate([jnp.where(seen, 0.0, very_low)] * group, axis=0))
@@ -150,8 +164,8 @@
             q_g = jnp.concatenate(
                 [q_ref[:, (g * group + h) * HEAD_DIM : (g * group + h + 1) * HEAD_DIM] for h in range(group)], axis=0
             )
-            keys = [p[0][:, cols] for p in pieces]
-            values = [p[1][:, cols] for p in pieces]
+            keys = [piece(k, 0, cols) for k in range(Z)]
+            values = [piece(k, 1, cols) for k in range(Z)]
             if which == 0:
                 keys.append(kn_ref[:, cols])
                 values.append(vn_ref[:, cols])
@@ -211,7 +225,7 @@
 
 def norm_kernel(share, mine_ref, res_ref, gain_ref, *refs):
     _, _, _, _, x, c = place()
-    *got, own_out, normed = refs
+    *got, full_out, own_out, normed = refs
     res = res_ref[...].astype(jnp.float32)
     hidden = mine_ref[...]
     for ref in got:
@@ -219,46 +233,44 @@
     hidden = jnp.where(c == 0, res[:HALF], res[HALF:]) + hidden
     squares = jnp.sum(hidden * hidden, axis=1, keepdims=True)
     normed[...] = hidden * lax.rsqrt(squares / D + norm_eps) * gain_ref[...]
+    full_out[...] = normed[...].astype(jnp.bfloat16)
     own_out[...] = normed[:, pl.ds(pl.multiple_of(x * share, LANES), share)].astype(jnp.bfloat16)
 
 
-def row_groups(Z):
-    return [g for g in (list(range(min(2, Z))), list(range(2, Z))) if g]
-
-
 def row_order(Z):
-    return [(k, other) for group in row_groups(Z) for other in (False, True) for k in group]
+    return [(0, False), (0, True)] + [(k, other) for other in (False, True) for k in range(1, Z)]
 
 
 def logits_kernel(mixed, X, Z, V, target_ref, *refs):
     s, z, y, v, x, c = place()
-    share = refs[0].shape[1]
-    sizes = [len(g) for g in row_groups(Z)]
+    share = refs[0].shape[1] // X
     n_rows = Y * Z * HALF
-    n_refs = (3 if mixed else X) * len(sizes)
-    pieces, (w_own, w_other, out_ref, *rows) = refs[:n_refs], refs[n_refs:]
-    base = 0
-    for i, size in enumerate(sizes):
-        n = size * HALF
-        if mixed:
-            column, step1, step2 = pieces[3 * i : 3 * i + 3]
-            near, far = rows
-            near[base : base + n] = column[...]
-            far[base + n : base + 2 * n] = step2[n:]
-
-            @pl.when(c == 0)
-            def _(base=base, n=n, step1=step1, step2=step2):
-                near[base + n : base + 2 * n] = step2[:n]
-                far[base : base + n] = step1[...]
-
-            @pl.when(c != 0)
-            def _(base=base, n=n, step1=step1, step2=step2):
-                near[base + n : base + 2 * n] = step1[...]
-                far[base : base + n] = step2[:n]
-        else:
-            for k in range(X):
-                rows[k][base : base + Y * n] = pieces[X * i + k][...]
-        base += Y * n
+    n_refs = 2 + (3 if mixed else X)
+    (own, across, *pieces), (w_own, w_other, out_ref, *rows) = refs[:n_refs], refs[n_refs:]
+    n = (Z - 1) * HALF
+    base = 2 * HALF
+    for k in range(X):
+        at = pl.multiple_of(lax.rem(x + (X - k), X) * share, LANES)
+        rows[k][:HALF] = own[:, pl.ds(at, share)]
+        rows[k][HALF:base] = across[:, pl.ds(at, share)]
+    if mixed:
+        column, step1, step2 = pieces
+        near, far = rows
+        near[base : base + n] = column[...]
+        far[base + n :] = step2[n:]
+
+        @pl.when(c == 0)
+        def _():
+            near[base + n :] = step2[:n]
+            far[base : base + n] = step1[...]
+
+        @pl.when(c != 0)
+        def _():
+            near[base + n :] = step1[...]
+            far[base : base + n] = step2[:n]
+    else:
+        for k in range(X):
+            rows[k][base:] = pieces[k][...]
     logits = []
     for w in (w_own, w_other):
         total = None
@@ -292,10 +304,8 @@
             out_ref[first + i] = row
 
 
-def loss_kernel(levels_ref, mask_ref, got_ref, out_ref):
-    s, _, _, _, _, _ = place()
+def loss_kernel(chosen_ref, weight_ref, got_ref, out_ref):
     got = got_ref[...]
-    tok = mask_ref.shape[1]
     core = lax.rem(lax.broadcasted_iota(jnp.int32, got.shape, 0), C)
     lane = lax.broadcasted_iota(jnp.int32, (8, LANES), 1)
     nll = jnp.zeros((8, LANES), jnp.float32)
@@ -307,14 +317,8 @@
         value = best + jnp.log(total) - pltpu.roll(picked, LANES - HALF, 1)
         value = pltpu.roll(value, half * HALF, 1) if half else value
         nll = jnp.where((lane >= half * HALF) & (lane < (half + 1) * HALF), value, nll)
-    chosen = jnp.where(slots_of(mask_ref[pl.ds(s, 1), :]), 1.0, 0.0)
-    chosen = jnp.concatenate([chosen, jnp.zeros((LANES - CAP, tok), jnp.float32)], axis=0)
-    token_nll = exact_dot(nll, chosen, (((1,), (0,)), ((), ())))[0:1]
-    block = lax.shift_right_logical(lax.broadcasted_iota(jnp.int32, (1, tok), 1), SHIFT)
-    weight = jnp.ones((1, tok), jnp.float32)
-    for b in range(tok // BLOCK):
-        weight = jnp.where(block == b, (levels_ref[s * (tok // BLOCK) + b] + 1).astype(jnp.float32), weight)
-    out_ref[...] = token_nll / weight
+    token_nll = exact_dot(nll, chosen_ref[...], (((1,), (0,)), ((), ())))
+    out_ref[...] = (token_nll / weight_ref[...])[0:1]
 
 
 def shards(
@@ -361,6 +365,9 @@
     def z_up(block, k):
         return permute(block, lambda a, b, e, f: (a + k, b, e, f))
 
+    def along_z(block, pairs):
+        return permute(block, lambda a, b, e, f: (dict(pairs).get(a, Z), b, e, f))
+
     def z_swap(block, k):
         paired = Z & (Z - 1) == 0
         return permute(block, lambda a, b, e, f: (a ^ k if paired else (a + k) % Z, b, e, f))
@@ -373,13 +380,20 @@
 
     all_mask = mask_flags.reshape(S, tok_rows)
     own_kv = jnp.stack([key_clean, value_clean])
-    pieces = [own_kv] + [z_up(own_kv, k) for k in range(1, Z)]
+    next_kv = z_up(own_kv, 1)
+    if Z == 4:
+        far_kv = along_z(own_kv, ((0, 3),))
+        second_kv = along_z(own_kv, ((0, 2),))
+        passed_kv = along_z(next_kv, ((2, 3),))
+        pieces = [own_kv, next_kv, second_kv, far_kv, passed_kv]
+    else:
+        pieces = [own_kv, next_kv] + [z_up(own_kv, k) for k in range(2, Z)]
     queries, slot_blocks = call(
         select_kernel, (struct(CAP, q_width), struct(2, CAP, LANES, dtype=jnp.float32)), (all_mask, q_noised), 8
     )
     other_queries = y_flip(queries)
     other_head = core_flip(head_weight)
-    keys_here, values_here, staged_out = stage(queries, key_noised, value_noised, out_weight)
+    keys_here, values_here = stage(queries, key_noised, value_noised)
     own_sum, own_lse, other_sum = call(
         functools.partial(attend_kernel, Z, heads_local, kv_local, S),
         (
@@ -391,6 +405,7 @@
         16,
     )
     got_sum = y_flip(other_sum)
+    (staged_out,) = stage(other_sum, out_weight)
     mine, theirs = call(
         functools.partial(project_kernel, heads_local),
         (struct(HALF, width, dtype=jnp.float32), struct(HALF, width)),
@@ -402,49 +417,51 @@
     sent = mine.astype(jnp.bfloat16)
     n_rows = Y * Z * HALF
     wide = -(-n_rows // LANES) * LANES
-    residual_sel, row_targets = call(
+    residual_sel, row_targets, chosen, weight = call(
         functools.partial(residual_kernel, Z),
-        (struct(CAP, width), struct(8, wide, dtype=jnp.int32)),
-        (all_mask, targets.reshape(S, tok_rows), residual, theirs),
+        (
+            struct(CAP, width),
+            struct(8, wide, dtype=jnp.int32),
+            struct(LANES, tok_rows, dtype=jnp.float32),
+            struct(8, tok_rows, dtype=jnp.float32),
+        ),
+        (levels, all_mask, targets.reshape(S, tok_rows), residual, theirs),
         8,
-    )
-    own = call(
+        specs=[SMEM] + [VMEM] * 4,
+    )
+    own_full, own = call(
         functools.partial(norm_kernel, share),
-        struct(HALF, share),
+        (struct(HALF, width), struct(HALF, share)),
         (mine, residual_sel, norm_gain.reshape(1, width), *[x_shift(sent, k) for k in range(1, X)]),
         8,
         scratch=[pltpu.VMEM((HALF, width), jnp.float32)],
     )
 
-    slabs = [own]
+    slabs = []
     for k in range(1, Z):
         slabs.append(z_swap(own, k))
+    across = y_flip(own_full)
     mixed = X == Y
-    rows = []
-    for group in row_groups(Z):
-        n = len(group) * HALF
-        column = jnp.stack([slabs[k] for k in group])
-        if mixed:
-            step1 = mixed_flip(column, 0)
-            both = jnp.stack([column, step1])
-            step2 = mixed_flip(both, 1)
-            rows += [column.reshape(n, share), step1.reshape(n, share), step2.reshape(Y * n, share)]
-        else:
-            pair = jnp.stack([column, y_flip(column)])
-            rows += [pair.reshape(Y * n, share)] + [x_shift(pair, k).reshape(Y * n, share) for k in range(1, X)]
+    n = (Z - 1) * HALF
+    column = jnp.stack(slabs)
+    if mixed:
+        step1 = mixed_flip(column, 0)
+        step2 = mixed_flip(jnp.stack([column, step1]), 1)
+        rows = [column.reshape(n, share), step1.reshape(n, share), step2.reshape(Y * n, share)]
+    else:
+        pair = jnp.stack([column, y_flip(column)])
+        rows = [pair.reshape(Y * n, share)] + [x_shift(pair, k).reshape(Y * n, share) for k in range(1, X)]
     staged = stage(own, head_weight, other_head)
     send = call(
         functools.partial(logits_kernel, mixed, X, Z, V),
         struct(S * V, 1, LANES, dtype=jnp.float32),
-        (row_targets, *rows, *staged),
+        (row_targets, own_full, across, *rows, *staged),
         24,
         4 * n_rows * width * vocab_rows,
         [pltpu.VMEM((n_rows, share), jnp.bfloat16)] * X,
     ).reshape(S * V, LANES)
     got = lax.all_to_all(send, ("seq", "vocab"), 0, 0, tiled=True)
-    loss = call(
-        loss_kernel, struct(1, tok_rows, dtype=jnp.float32), (levels, all_mask, got), 4, specs=[SMEM, VMEM, VMEM]
-    )
+    loss = call(loss_kernel, struct(1, tok_rows, dtype=jnp.float32), (chosen, weight, got), 4)
     return loss.reshape(tok_rows)
 
 

time: 80.5 us -> 84.3 us (1.047)
  waiting for transfers between devices: 26 us -> 28.6 us
  starting transfers between devices: 23.5 us -> 25.2 us
    ppermute x15, waiting for transfers between devices: 26 us -> 28.6 us  [permute(): lax.ppermute(block, ('seq', 'vocab'), [(dev(*e), dev(*to(*e))) for e in e...]
    ppermute x15, starting transfers between devices: 23.5 us -> 25.2 us  [permute(): lax.ppermute(block, ('seq', 'vocab'), [(dev(*e), dev(*to(*e))) for e in e...]
    pallas_call x9 -> x10, Pallas kernels: 11.2 us -> 11.2 us  [call(): pl.pallas_call(kernel, out_shape=outs, in_specs=specs or [VMEM] * len(arg...]
  transfers between devices with their start and end apart: 15 -> 15, of which waited for: 8 -> 7; matrix products, arithmetic and copies ran while one was open for 1% -> 1% of each run, Pallas kernels for 8% -> 9%
where the time goes in v5:
time: 84.3 us; the launch traced here: 83.9 us
  waiting for transfers between devices  28.6 us (34%)
  starting transfers between devices  25.2 us (30%)
  Pallas kernels  11.2 us (13%)
  blocking collectives  10.8 us (13%)
  local copies, waits for them, and re-layouts  6.73 us (8%)
  other arithmetic  1.03 us (1%)
    ppermute x15, waiting for transfers between devices, permute(): lax.ppermute(block, ('seq', 'vocab'), [(dev(*e), dev(*to(*e))) for e in e...  28.6 us
    ppermute x15, starting transfers between devices, permute(): lax.ppermute(block, ('seq', 'vocab'), [(dev(*e), dev(*to(*e))) for e in e...  25.2 us
    pallas_call x10, Pallas kernels, call(): pl.pallas_call(kernel, out_shape=outs, in_specs=specs or [VMEM] * len(arg...  11.2 us
    all_to_all x1, blocking collectives, shards(): got = lax.all_to_all(send, ('seq', 'vocab'), 0, 0, tiled=True)  10.8 us
    unnamed x24, local copies, waits for them, and re-layouts  6.73 us
  transfers between devices with their start and end apart: 15, of which 7 were waited for; matrix products, arithmetic and copies ran while one was open for 1% of the time, Pallas kernels for 9%

profile of v5, /device:TPU:0, one launch (start us, length us, event | category | flops | bytes accessed | tf_op | source)
XLA Modules:
  0.0 83.9 jit_solution(102137910216434652)
XLA Ops:
  0.5 0.9 %pad_maximum_fusion.2.refs_0_ = bf16[2,128,256]{2,1,0:T(8,128)(2,1)S(1)} fusion(bf16[1,128,256]{2,1,0:T(8,128)(2,1)} %bitcast.30, bf16[1,128,256]{2,1,0:T(8,128)(2,1)} %bitcast.31), kind=kLoop, calls=%fused_computation.3 | loop fusion | flops 65536 | bytes 262144 | tf_op jit(solution)/shard_map/stack | solution.py:382
  1.4 4.5 %collective-permute-start.1 = (bf16[2,128,256]{2,1,0:T(8,128)(2,1)S(1)}, bf16[2,128,256]{2,1,0:T(8,128)(2,1)S(1)}, u32[]{:S(2)}, u32[]{:S(2)}) collective-permute-start(bf16[2,128,256]{2,1,0:T(8,128)(2,1)S(1)} %pad_maximum_fusion.2.refs_0_), channel_id=1, source_target_pairs={{0,8},{1,9},{2,10},{3,11},{4,12},{5,13},{6,14},{7,15},{8,16},{9,17... | collective-permute-start | bytes 393224 | tf_op jit(solution)/shard_map/ppermute | solution.py:354
  5.9 4.5 %collective-permute-start.2 = (bf16[2,128,256]{2,1,0:T(8,128)(2,1)S(1)}, bf16[2,128,256]{2,1,0:T(8,128)(2,1)S(1)}, u32[]{:S(2)}, u32[]{:S(2)}) collective-permute-start(bf16[2,128,256]{2,1,0:T(8,128)(2,1)S(1)} %pad_maximum_fusion.2.refs_0_), channel_id=1, source_target_pairs={{0,16},{1,17},{2,18},{3,19},{4,20},{5,21},{6,22},{7,23}} | collective-permute-start | bytes 393224 | tf_op jit(solution)/shard_map/ppermute | solution.py:354
  10.4 1.3 %collective-permute-start.3 = (bf16[2,128,256]{2,1,0:T(8,128)(2,1)S(1)}, bf16[2,128,256]{2,1,0:T(8,128)(2,1)S(1)}, u32[]{:S(2)}, u32[]{:S(2)}) collective-permute-start(bf16[2,128,256]{2,1,0:T(8,128)(2,1)S(1)} %pad_maximum_fusion.2.refs_0_), channel_id=1, source_target_pairs={{0,24},{1,25},{2,26},{3,27},{4,28},{5,29},{6,30},{7,31}} | collective-permute-start | bytes 393224 | tf_op jit(solution)/shard_map/ppermute | solution.py:354
  11.7 0.7 collective-permute-start.4
  12.4 0.9 %copy-done.2 = bf16[128,1024]{1,0:T(8,128)(2,1)S(1)} copy-done((bf16[128,1024]{1,0:T(8,128)(2,1)S(1)}, bf16[128,1024]{1,0:T(8,128)(2,1)}, u32[]{:S(2)}) %copy-start.2) | copy-done | bytes 262168
  13.3 0.7 copy-done.6
  14.4 1.5 %collective-permute-start = (bf16[48,1024]{1,0:T(8,128)(2,1)S(1)}, bf16[48,1024]{1,0:T(8,128)(2,1)S(1)}, u32[]{:S(2)}, u32[]{:S(2)}) collective-permute-start(bf16[48,1024]{1,0:T(8,128)(2,1)S(1)} %get-tuple-element.23.after.q_own), channel_id=1, source_target_pairs={{0,4},{1,5},{2,6},{3,7},{4,0},{5,1},{6,2},{7,3},{8,12},{9,13},{10,... | collective-permute-start | bytes 294920 | tf_op jit(solution)/shard_map/ppermute | solution.py:354
  15.9 0.8 copy-done.3
  16.7 0.8 copy-done.4
  17.7 1.3 %collective-permute-done.q_other = bf16[48,1024]{1,0:T(8,128)(2,1)S(1)} collective-permute-done((bf16[48,1024]{1,0:T(8,128)(2,1)S(1)}, bf16[48,1024]{1,0:T(8,128)(2,1)S(1)}, u32[]{:S(2)}, u32[]{:S(2)}) %collective-permute-start) | collective-permute-done | bytes 98336 | tf_op jit(solution)/shard_map/ppermute | solution.py:354
  19.0 1.4 %shard_map.120 = (f32[48,1024]{1,0:T(8,128)S(1)}, f32[48,128]{1,0:T(8,128)S(1)}, bf16[48,1152]{1,0:T(8,128)(2,1)S(1)}) custom-call(f32[2,48,128]{2,1,0:T(8,128)S(1)} %get-tuple-element.22.blk_ref, bf16[48,1024]{1,0:T(8,128)(2,1)S(1)} %get-tuple-element.23.after.q_own, bf16[48,1024]{1,0:T(8,128)(2,1)S(1)} %collective-permute-done.q_other, ...), custom_call_target="tpu_custom_call" | custom-call | bytes 1032192 | tf_op jit(solution)/shard_map/pallas_call | solution.py:33
  20.5 1.6 %collective-permute-start.5 = (bf16[48,1152]{1,0:T(8,128)(2,1)S(1)}, bf16[48,1152]{1,0:T(8,128)(2,1)S(1)}, u32[]{:S(2)}, u32[]{:S(2)}) collective-permute-start(bf16[48,1152]{1,0:T(8,128)(2,1)S(1)} %get-tuple-element.28.after), channel_id=1, source_target_pairs={{0,4},{1,5},{2,6},{3,7},{4,0},{5,1},{6,2},{7,3},{8,12},{9,13},{10,... | collective-permute-start | bytes 331784 | tf_op jit(solution)/shard_map/ppermute | solution.py:354
  22.1 3.4 %copy-done = bf16[1024,4096]{1,0:T(8,128)(2,1)S(1)} copy-done((bf16[1024,4096]{1,0:T(8,128)(2,1)S(1)}, bf16[1024,4096]{1,0:T(8,128)(2,1)}, u32[]{:S(2)}) %copy-start) | copy-done | bytes 8388632
  25.4 0.6 shard_map.121.w_ref
  26.1 1.7 %shard_map.122 = (f32[24,4096]{1,0:T(8,128)S(1)}, bf16[24,4096]{1,0:T(8,128)(2,1)S(1)}) custom-call(f32[48,1024]{1,0:T(8,128)S(1)} %get-tuple-element.26.own_ref, f32[48,128]{1,0:T(8,128)S(1)} %get-tuple-element.27.lse_ref, bf16[48,1152]{1,0:T(8,128)(2,1)S(1)} %collective-permute-done.5.got_ref, bf16[1024,4096]{1,0:T(8,128)(2,1)S(1)} %shard_map.121.w_ref), custom_call_target="tpu_custom_call" | custom-call | bytes 8720384 | tf_op jit(solution)/shard_map/pallas_call | solution.py:33
  27.9 1.4 %collective-permute-done.6 = bf16[24,4096]{1,0:T(8,128)(2,1)S(1)} collective-permute-done((bf16[24,4096]{1,0:T(8,128)(2,1)S(1)}, bf16[24,4096]{1,0:T(8,128)(2,1)S(1)}, u32[]{:S(2)}, u32[]{:S(2)}) %collective-permute-start.6) | collective-permute-done | bytes 196640 | tf_op jit(solution)/shard_map/ppermute | solution.py:354
  29.3 1.6 %collective-permute-start.7 = (bf16[24,4096]{1,0:T(8,128)(2,1)S(1)}, bf16[24,4096]{1,0:T(8,128)(2,1)S(1)}, u32[]{:S(2)}, u32[]{:S(2)}) collective-permute-start(bf16[24,4096]{1,0:T(8,128)(2,1)S(1)} %get-tuple-element.39), channel_id=1, source_target_pairs={{0,2},{1,3},{2,0},{3,1},{4,6},{5,7},{6,4},{7,5},{8,10},{9,11},{10,... | collective-permute-start | bytes 589832 | tf_op jit(solution)/shard_map/ppermute | solution.py:354
  30.9 1.7 %shard_map.123 = (bf16[48,4096]{1,0:T(8,128)(2,1)S(1)}, s32[8,256]{1,0:T(8,128)S(1)}, f32[128,128]{1,0:T(8,128)S(1)}, f32[8,128]{1,0:T(8,128)S(1)}) custom-call(s32[32]{0:T(128)S(1)} %copy-done.9, s32[8,128]{1,0:T(8,128)S(1)} %bitcast.25, s32[8,128]{1,0:T(8,128)S(1)} %bitcast.26, bf16[128,4096]{1,0:T(8,128)(2,1)S(1)} %copy-done.1, ...), custom_call_target="tpu_custom_call" | custom-call | bytes 1253504 | tf_op jit(solution)/shard_map/pallas_call | solution.py:33
  32.6 3.7 %collective-permute-done.7.refs_0_ = bf16[24,4096]{1,0:T(8,128)(2,1)S(1)} collective-permute-done((bf16[24,4096]{1,0:T(8,128)(2,1)S(1)}, bf16[24,4096]{1,0:T(8,128)(2,1)S(1)}, u32[]{:S(2)}, u32[]{:S(2)}) %collective-permute-start.7) | collective-permute-done | bytes 196640 | tf_op jit(solution)/shard_map/ppermute | solution.py:354
  36.7 4.6 %collective-permute-start.10 = (bf16[24,2048]{1,0:T(8,128)(2,1)S(1)}, bf16[24,2048]{1,0:T(8,128)(2,1)S(1)}, u32[]{:S(2)}, u32[]{:S(2)}) collective-permute-start(bf16[24,2048]{1,0:T(8,128)(2,1)S(1)} %get-tuple-element.36.after), channel_id=1, source_target_pairs={{0,16},{1,17},{2,18},{3,19},{4,20},{5,21},{6,22},{7,23},{8,24},{9,... | collective-permute-start | bytes 294920 | tf_op jit(solution)/shard_map/ppermute | solution.py:354
  41.3 0.7 collective-permute-start.11
  42.4 6.6 %collective-permute-done.10 = bf16[24,2048]{1,0:T(8,128)(2,1)S(1)} collective-permute-done((bf16[24,2048]{1,0:T(8,128)(2,1)S(1)}, bf16[24,2048]{1,0:T(8,128)(2,1)S(1)}, u32[]{:S(2)}, u32[]{:S(2)}) %collective-permute-start.10) | collective-permute-done | bytes 98336 | tf_op jit(solution)/shard_map/ppermute | solution.py:354
  49.0 1.6 %collective-permute-start.12 = (bf16[3,24,2048]{2,1,0:T(8,128)(2,1)S(1)}, bf16[3,24,2048]{2,1,0:T(8,128)(2,1)S(1)}, u32[]{:S(2)}, u32[]{:S(2)}) collective-permute-start(bf16[3,24,2048]{2,1,0:T(8,128)(2,1)S(1)} %get-tuple-element.42), channel_id=1, source_target_pairs={{0,2},{1,5},{2,0},{3,7},{4,6},{5,1},{6,4},{7,3},{8,10},{9,13},{10,... | collective-permute-start | bytes 884744 | tf_op jit(solution)/shard_map/ppermute | solution.py:354
  50.6 6.3 %collective-permute-done.12 = bf16[3,24,2048]{2,1,0:T(8,128)(2,1)S(1)} collective-permute-done((bf16[3,24,2048]{2,1,0:T(8,128)(2,1)S(1)}, bf16[3,24,2048]{2,1,0:T(8,128)(2,1)S(1)}, u32[]{:S(2)}, u32[]{:S(2)}) %collective-permute-start.12) | collective-permute-done | bytes 294944 | tf_op jit(solution)/shard_map/ppermute | solution.py:354
  57.0 0.8 collective-permute-start.13
  57.8 1.3 %collective-permute-start.8 = (bf16[24,4096]{1,0:T(8,128)(2,1)S(1)}, bf16[24,4096]{1,0:T(8,128)(2,1)S(1)}, u32[]{:S(2)}, u32[]{:S(2)}) collective-permute-start(bf16[24,4096]{1,0:T(8,128)(2,1)S(1)} %get-tuple-element.35.refs_0_), channel_id=1, source_target_pairs={{0,4},{1,5},{2,6},{3,7},{4,0},{5,1},{6,2},{7,3},{8,12},{9,13},{10,... | collective-permute-start | bytes 589832 | tf_op jit(solution)/shard_map/ppermute | solution.py:354
  59.1 1.0 %shard_map.125 = (bf16[592,4096]{1,0:T(8,128)(2,1)S(1)}, bf16[592,4096]{1,0:T(8,128)(2,1)S(1)}) custom-call(bf16[24,2048]{1,0:T(8,128)(2,1)S(1)} %get-tuple-element.36.after, bf16[592,4096]{1,0:T(8,128)(2,1)S(1)} %bitcast.17, bf16[592,4096]{1,0:T(8,128)(2,1)S(1)} %collective-permute-done.14.refs_1_), custom_call_target="tpu_custom_call" | custom-call | bytes 9797632 | tf_op jit(solution)/shard_map/pallas_call | solution.py:33
  60.1 8.9 %collective-permute-done.8.refs_1_ = bf16[24,4096]{1,0:T(8,128)(2,1)S(1)} collective-permute-done((bf16[24,4096]{1,0:T(8,128)(2,1)S(1)}, bf16[24,4096]{1,0:T(8,128)(2,1)S(1)}, u32[]{:S(2)}, u32[]{:S(2)}) %collective-permute-start.8) | collective-permute-done | bytes 196640 | tf_op jit(solution)/shard_map/ppermute | solution.py:354
  69.0 3.2 %shard_map.126 = f32[32,1,128]{2,1,0:T(1,128)S(1)} custom-call(s32[8,256]{1,0:T(8,128)S(1)} %get-tuple-element.32.target_ref, bf16[24,4096]{1,0:T(8,128)(2,1)S(1)} %get-tuple-element.35.refs_0_, bf16[24,4096]{1,0:T(8,128)(2,1)S(1)} %collective-permute-done.8.refs_1_, bf16[72,2048]{1,0:T(8,128)(2,1)S(1)} %bitcast.18, bf16[72,2048]{1,0:T(8,128)(2,1)S(1)} %bitcast.20, ...), custom_call_target="tpu_custom_call" | custom-call | flops 1862270976 | bytes 11280384 | tf_op jit(solution)/shard_map/pallas_call | solution.py:33
  72.2 10.8 %all_to_all.8 = f32[32,1,128]{2,1,0:T(1,128)S(1)} all-to-all(f32[32,1,128]{2,1,0:T(1,128)S(1)} %shard_map.126), channel_id=1, replica_groups=mesh['seq'=8,'vocab'=4] {'seq','vocab'}, dimensions={0} | all-to-all | bytes 32768 | tf_op jit(solution)/shard_map/all_to_all | solution.py:463
  83.0 0.8 shard_map.127
  (38 shorter events, 2.0 us)
Async XLA Ops:
  0.0 59.1 %collective-permute-start.14 = (bf16[592,4096]{1,0:T(8,128)(2,1)}, bf16[592,4096]{1,0:T(8,128)(2,1)S(1)}, u32[]{:S(2)}, u32[]{:S(2)}) collective-permute-start(bf16[592,4096]{1,0:T(8,128)(2,1)} %refs_0_.5), channel_id=1, source_target_pairs={{0,1},{1,0},{2,3},{3,2},{4,5},{5,4},{6,7},{7,6},{8,9},{9,8},{10,11... | collective-permute-start | bytes 14549000 | tf_op jit(solution)/shard_map/ppermute | solution.py:354
  1.4 10.3 %collective-permute-start.1 = (bf16[2,128,256]{2,1,0:T(8,128)(2,1)S(1)}, bf16[2,128,256]{2,1,0:T(8,128)(2,1)S(1)}, u32[]{:S(2)}, u32[]{:S(2)}) collective-permute-start(bf16[2,128,256]{2,1,0:T(8,128)(2,1)S(1)} %pad_maximum_fusion.2.refs_0_), channel_id=1, source_target_pairs={{0,8},{1,9},{2,10},{3,11},{4,12},{5,13},{6,14},{7,15},{8,16},{9,17... | collective-permute-start | bytes 393224 | tf_op jit(solution)/shard_map/ppermute | solution.py:354
  5.9 13.2 %collective-permute-start.2 = (bf16[2,128,256]{2,1,0:T(8,128)(2,1)S(1)}, bf16[2,128,256]{2,1,0:T(8,128)(2,1)S(1)}, u32[]{:S(2)}, u32[]{:S(2)}) collective-permute-start(bf16[2,128,256]{2,1,0:T(8,128)(2,1)S(1)} %pad_maximum_fusion.2.refs_0_), channel_id=1, source_target_pairs={{0,16},{1,17},{2,18},{3,19},{4,20},{5,21},{6,22},{7,23}} | collective-permute-start | bytes 393224 | tf_op jit(solution)/shard_map/ppermute | solution.py:354
  10.4 8.7 %collective-permute-start.3 = (bf16[2,128,256]{2,1,0:T(8,128)(2,1)S(1)}, bf16[2,128,256]{2,1,0:T(8,128)(2,1)S(1)}, u32[]{:S(2)}, u32[]{:S(2)}) collective-permute-start(bf16[2,128,256]{2,1,0:T(8,128)(2,1)S(1)} %pad_maximum_fusion.2.refs_0_), channel_id=1, source_target_pairs={{0,24},{1,25},{2,26},{3,27},{4,28},{5,29},{6,30},{7,31}} | collective-permute-start | bytes 393224 | tf_op jit(solution)/shard_map/ppermute | solution.py:354
  11.7 7.4 %collective-permute-start.4 = (bf16[2,128,256]{2,1,0:T(8,128)(2,1)S(1)}, bf16[2,128,256]{2,1,0:T(8,128)(2,1)S(1)}, u32[]{:S(2)}, u32[]{:S(2)}) collective-permute-start(bf16[2,128,256]{2,1,0:T(8,128)(2,1)S(1)} %collective-permute-done.1.refs_1_), channel_id=1, source_target_pairs={{16,24},{17,25},{18,26},{19,27},{20,28},{21,29},{22,30},{23,31}} | collective-permute-start | bytes 393224 | tf_op jit(solution)/shard_map/ppermute | solution.py:354
  12.4 1.0 %copy-start.2 = (bf16[128,1024]{1,0:T(8,128)(2,1)S(1)}, bf16[128,1024]{1,0:T(8,128)(2,1)}, u32[]{:S(2)}) copy-start(bf16[128,1024]{1,0:T(8,128)(2,1)} %q_ref.1) | copy-start | bytes 786436
  13.3 0.7 copy-start.6
  14.4 4.7 %collective-permute-start = (bf16[48,1024]{1,0:T(8,128)(2,1)S(1)}, bf16[48,1024]{1,0:T(8,128)(2,1)S(1)}, u32[]{:S(2)}, u32[]{:S(2)}) collective-permute-start(bf16[48,1024]{1,0:T(8,128)(2,1)S(1)} %get-tuple-element.23.after.q_own), channel_id=1, source_target_pairs={{0,4},{1,5},{2,6},{3,7},{4,0},{5,1},{6,2},{7,3},{8,12},{9,13},{10,... | collective-permute-start | bytes 294920 | tf_op jit(solution)/shard_map/ppermute | solution.py:354
  15.9 0.8 %copy-start.3 = (bf16[128,256]{1,0:T(8,128)(2,1)S(1)}, bf16[128,256]{1,0:T(8,128)(2,1)}, u32[]{:S(2)}) copy-start(bf16[128,256]{1,0:T(8,128)(2,1)} %refs_0_.3) | copy-start | bytes 196612
  16.7 0.8 %copy-start.4 = (bf16[128,256]{1,0:T(8,128)(2,1)S(1)}, bf16[128,256]{1,0:T(8,128)(2,1)}, u32[]{:S(2)}) copy-start(bf16[128,256]{1,0:T(8,128)(2,1)} %refs_1_.1) | copy-start | bytes 196612
  20.5 5.5 %collective-permute-start.5 = (bf16[48,1152]{1,0:T(8,128)(2,1)S(1)}, bf16[48,1152]{1,0:T(8,128)(2,1)S(1)}, u32[]{:S(2)}, u32[]{:S(2)}) collective-permute-start(bf16[48,1152]{1,0:T(8,128)(2,1)S(1)} %get-tuple-element.28.after), channel_id=1, source_target_pairs={{0,4},{1,5},{2,6},{3,7},{4,0},{5,1},{6,2},{7,3},{8,12},{9,13},{10,... | collective-permute-start | bytes 331784 | tf_op jit(solution)/shard_map/ppermute | solution.py:354
  22.1 3.4 %copy-start = (bf16[1024,4096]{1,0:T(8,128)(2,1)S(1)}, bf16[1024,4096]{1,0:T(8,128)(2,1)}, u32[]{:S(2)}) copy-start(bf16[1024,4096]{1,0:T(8,128)(2,1)} %refs_0_.4) | copy-start | bytes 25165828
  26.0 33.0 %slice-start = ((s8[4849664]{0:T(1024)(128)(4,1)}), s8[4194304]{0:T(1024)(128)(4,1)S(1)}, s32[]{:S(2)}) async-start(s8[4849664]{0:T(1024)(128)(4,1)} %bitcast.16), calls=%async_computation.1 | async-start | bytes 8388608
  26.0 4.9 %copy-start.1 = (bf16[128,4096]{1,0:T(8,128)(2,1)S(1)}, bf16[128,4096]{1,0:T(8,128)(2,1)}, u32[]{:S(2)}) copy-start(bf16[128,4096]{1,0:T(8,128)(2,1)} %res_ref.1) | copy-start | bytes 3145732
  26.0 4.9 %copy-start.7 = (s32[1024]{0:T(1024)S(1)}, s32[1024]{0:T(1024)}, u32[]{:S(2)}) copy-start(s32[1024]{0:T(1024)} %param.22) | copy-start | bytes 12292
  26.1 4.9 %copy-start.8 = (s32[1024]{0:T(1024)S(1)}, s32[1024]{0:T(1024)}, u32[]{:S(2)}) copy-start(s32[1024]{0:T(1024)} %param.21) | copy-start | bytes 12292
  26.1 4.8 %copy-start.9 = (s32[32]{0:T(128)S(1)}, s32[32]{0:T(128)}, u32[]{:S(2)}) copy-start(s32[32]{0:T(128)} %levels_ref.1) | copy-start | bytes 388
  26.1 10.3 %copy-start.5 = (f32[4096]{0:T(1024)S(1)}, f32[4096]{0:T(1024)}, u32[]{:S(2)}) copy-start(f32[4096]{0:T(1024)} %param.19) | copy-start | bytes 49156
  26.1 33.0 %slice-start.1 = ((s8[4849664]{0:T(1024)(128)(4,1)}), s8[655360]{0:T(1024)(128)(4,1)S(1)}, s32[]{:S(2)}) async-start(s8[4849664]{0:T(1024)(128)(4,1)} %bitcast.16), calls=%async_computation.2 | async-start | bytes 1310720
  27.8 1.5 %collective-permute-start.6 = (bf16[24,4096]{1,0:T(8,128)(2,1)S(1)}, bf16[24,4096]{1,0:T(8,128)(2,1)S(1)}, u32[]{:S(2)}, u32[]{:S(2)}) collective-permute-start(bf16[24,4096]{1,0:T(8,128)(2,1)S(1)} %get-tuple-element.29.after_ref), channel_id=1, source_target_pairs={{0,1},{1,0},{2,3},{3,2},{4,5},{5,4},{6,7},{7,6},{8,9},{9,8},{10,11... | collective-permute-start | bytes 589832 | tf_op jit(solution)/shard_map/ppermute | solution.py:354
  29.3 7.0 %collective-permute-start.7 = (bf16[24,4096]{1,0:T(8,128)(2,1)S(1)}, bf16[24,4096]{1,0:T(8,128)(2,1)S(1)}, u32[]{:S(2)}, u32[]{:S(2)}) collective-permute-start(bf16[24,4096]{1,0:T(8,128)(2,1)S(1)} %get-tuple-element.39), channel_id=1, source_target_pairs={{0,2},{1,3},{2,0},{3,1},{4,6},{5,7},{6,4},{7,5},{8,10},{9,11},{10,... | collective-permute-start | bytes 589832 | tf_op jit(solution)/shard_map/ppermute | solution.py:354
  36.6 5.7 %collective-permute-start.9 = (bf16[24,2048]{1,0:T(8,128)(2,1)S(1)}, bf16[24,2048]{1,0:T(8,128)(2,1)S(1)}, u32[]{:S(2)}, u32[]{:S(2)}) collective-permute-start(bf16[24,2048]{1,0:T(8,128)(2,1)S(1)} %get-tuple-element.36.after), channel_id=1, source_target_pairs={{0,8},{1,9},{2,10},{3,11},{4,12},{5,13},{6,14},{7,15},{8,0},{9,1},... | collective-permute-start | bytes 294920 | tf_op jit(solution)/shard_map/ppermute | solution.py:354
  36.7 12.2 %collective-permute-start.10 = (bf16[24,2048]{1,0:T(8,128)(2,1)S(1)}, bf16[24,2048]{1,0:T(8,128)(2,1)S(1)}, u32[]{:S(2)}, u32[]{:S(2)}) collective-permute-start(bf16[24,2048]{1,0:T(8,128)(2,1)S(1)} %get-tuple-element.36.after), channel_id=1, source_target_pairs={{0,16},{1,17},{2,18},{3,19},{4,20},{5,21},{6,22},{7,23},{8,24},{9,... | collective-permute-start | bytes 294920 | tf_op jit(solution)/shard_map/ppermute | solution.py:354
  41.3 7.7 %collective-permute-start.11 = (bf16[24,2048]{1,0:T(8,128)(2,1)S(1)}, bf16[24,2048]{1,0:T(8,128)(2,1)S(1)}, u32[]{:S(2)}, u32[]{:S(2)}) collective-permute-start(bf16[24,2048]{1,0:T(8,128)(2,1)S(1)} %get-tuple-element.36.after), channel_id=1, source_target_pairs={{0,24},{1,25},{2,26},{3,27},{4,28},{5,29},{6,30},{7,31},{8,16},{9,... | collective-permute-start | bytes 294920 | tf_op jit(solution)/shard_map/ppermute | solution.py:354
  49.0 7.9 %collective-permute-start.12 = (bf16[3,24,2048]{2,1,0:T(8,128)(2,1)S(1)}, bf16[3,24,2048]{2,1,0:T(8,128)(2,1)S(1)}, u32[]{:S(2)}, u32[]{:S(2)}) collective-permute-start(bf16[3,24,2048]{2,1,0:T(8,128)(2,1)S(1)} %get-tuple-element.42), channel_id=1, source_target_pairs={{0,2},{1,5},{2,0},{3,7},{4,6},{5,1},{6,4},{7,3},{8,10},{9,13},{10,... | collective-permute-start | bytes 884744 | tf_op jit(solution)/shard_map/ppermute | solution.py:354
  57.0 12.1 %collective-permute-start.13 = (bf16[2,3,24,2048]{3,2,1,0:T(8,128)(2,1)S(1)}, bf16[2,3,24,2048]{3,2,1,0:T(8,128)(2,1)S(1)}, u32[]{:S(2)}, u32[]{:S(2)}) collective-permute-start(bf16[2,3,24,2048]{3,2,1,0:T(8,128)(2,1)S(1)} %pad_maximum_fusion), channel_id=1, source_target_pairs={{0,4},{1,3},{2,6},{3,1},{4,0},{5,7},{6,2},{7,5},{8,12},{9,11},{10,... | collective-permute-start | bytes 1769480 | tf_op jit(solution)/shard_map/ppermute | solution.py:354
  57.8 11.2 %collective-permute-start.8 = (bf16[24,4096]{1,0:T(8,128)(2,1)S(1)}, bf16[24,4096]{1,0:T(8,128)(2,1)S(1)}, u32[]{:S(2)}, u32[]{:S(2)}) collective-permute-start(bf16[24,4096]{1,0:T(8,128)(2,1)S(1)} %get-tuple-element.35.refs_0_), channel_id=1, source_target_pairs={{0,4},{1,5},{2,6},{3,7},{4,0},{5,1},{6,2},{7,3},{8,12},{9,13},{10,... | collective-permute-start | bytes 589832 | tf_op jit(solution)/shard_map/ppermute | solution.py:354

commit v6 on v5

--- a/solution.py
+++ b/solution.py
@@ -20,6 +20,9 @@
 
 very_low = -1e30
 norm_eps = 1e-06
+
+GROUPS = [[1], [3], [2]]
+STRAIGHT = [[2]]
 
 VMEM = pl.BlockSpec(memory_space=pltpu.VMEM)
 SMEM = pl.BlockSpec(memory_space=pltpu.SMEM)
@@ -237,40 +240,56 @@
     own_out[...] = normed[:, pl.ds(pl.multiple_of(x * share, LANES), share)].astype(jnp.bfloat16)
 
 
+def groups_of(Z):
+    return GROUPS if Z == 4 else [range(1, Z)]
+
+
+def pieces_of(group, mixed, X):
+    return X if not mixed else 4 if group in STRAIGHT else 3
+
+
 def row_order(Z):
-    return [(0, False), (0, True)] + [(k, other) for other in (False, True) for k in range(1, Z)]
+    return [(0, False), (0, True)] + [(k, other) for group in groups_of(Z) for other in (False, True) for k in group]
 
 
 def logits_kernel(mixed, X, Z, V, target_ref, *refs):
     s, z, y, v, x, c = place()
     share = refs[0].shape[1] // X
     n_rows = Y * Z * HALF
-    n_refs = 2 + (3 if mixed else X)
+    sizes = [len(g) for g in groups_of(Z)]
+    counts = [pieces_of(g, mixed, X) for g in groups_of(Z)]
+    n_refs = 2 + sum(counts)
     (own, across, *pieces), (w_own, w_other, out_ref, *rows) = refs[:n_refs], refs[n_refs:]
-    n = (Z - 1) * HALF
     base = 2 * HALF
     for k in range(X):
         at = pl.multiple_of(lax.rem(x + (X - k), X) * share, LANES)
         rows[k][:HALF] = own[:, pl.ds(at, share)]
         rows[k][HALF:base] = across[:, pl.ds(at, share)]
-    if mixed:
-        column, step1, step2 = pieces
-        near, far = rows
-        near[base : base + n] = column[...]
-        far[base + n :] = step2[n:]
-
-        @pl.when(c == 0)
-        def _():
-            near[base + n :] = step2[:n]
-            far[base : base + n] = step1[...]
-
-        @pl.when(c != 0)
-        def _():
-            near[base + n :] = step1[...]
-            far[base : base + n] = step2[:n]
-    else:
-        for k in range(X):
-            rows[k][base:] = pieces[k][...]
+    for i, size in enumerate(sizes):
+        n = size * HALF
+        mine = pieces[sum(counts[:i]) : sum(counts[: i + 1])]
+        if mixed and counts[i] == 4:
+            for ref, (at, block) in zip(mine, ((0, rows[0]), (0, rows[1]), (n, rows[0]), (n, rows[1]))):
+                block[base + at : base + at + n] = ref[...]
+        elif mixed:
+            column, step1, step2 = mine
+            near, far = rows
+            near[base : base + n] = column[...]
+            far[base + n : base + 2 * n] = step2[n:]
+
+            @pl.when(c == 0)
+            def _(base=base, n=n, step1=step1, step2=step2):
+                near[base + n : base + 2 * n] = step2[:n]
+                far[base : base + n] = step1[...]
+
+            @pl.when(c != 0)
+            def _(base=base, n=n, step1=step1, step2=step2):
+                near[base + n : base + 2 * n] = step1[...]
+                far[base : base + n] = step2[:n]
+        else:
+            for k in range(X):
+                rows[k][base : base + Y * n] = mine[k][...]
+        base += Y * n
     logits = []
     for w in (w_own, w_other):
         total = None
@@ -437,20 +456,28 @@
         scratch=[pltpu.VMEM((HALF, width), jnp.float32)],
     )
 
-    slabs = []
+    slabs = {}
     for k in range(1, Z):
-        slabs.append(z_swap(own, k))
+        slabs[k] = z_swap(own, k)
     across = y_flip(own_full)
     mixed = X == Y
-    n = (Z - 1) * HALF
-    column = jnp.stack(slabs)
-    if mixed:
-        step1 = mixed_flip(column, 0)
-        step2 = mixed_flip(jnp.stack([column, step1]), 1)
-        rows = [column.reshape(n, share), step1.reshape(n, share), step2.reshape(Y * n, share)]
-    else:
-        pair = jnp.stack([column, y_flip(column)])
-        rows = [pair.reshape(Y * n, share)] + [x_shift(pair, k).reshape(Y * n, share) for k in range(1, X)]
+    rows = []
+    for group in groups_of(Z):
+        n = len(group) * HALF
+        column = jnp.stack([slabs[k] for k in group])
+        if mixed and group in STRAIGHT:
+            over_x = x_shift(column, 1)
+            over_y = y_flip(column)
+            over_xy = permute(column, lambda a, b, e, f: (a, 1 - b, 1 - e, f))
+            rows += [a.reshape(n, share) for a in (column, over_x, over_y, over_xy)]
+        elif mixed:
+            step1 = mixed_flip(column, 0)
+            both = jnp.stack([column, step1])
+            step2 = mixed_flip(both, 1)
+            rows += [column.reshape(n, share), step1.reshape(n, share), step2.reshape(Y * n, share)]
+        else:
+            pair = jnp.stack([column, y_flip(column)])
+            rows += [pair.reshape(Y * n, share)] + [x_shift(pair, k).reshape(Y * n, share) for k in range(1, X)]
     staged = stage(own, head_weight, other_head)
     send = call(
         functools.partial(logits_kernel, mixed, X, Z, V),

time: 84.3 us -> 78.2 us (0.928)
  waiting for transfers between devices: 28.6 us -> 16.3 us
  starting transfers between devices: 25.2 us -> 30.8 us
    ppermute x15 -> x20, waiting for transfers between devices: 28.6 us -> 16.3 us  [permute(): lax.ppermute(block, ('seq', 'vocab'), [(dev(*e), dev(*to(*e))) for e in e...]
    ppermute x15 -> x20, starting transfers between devices: 25.2 us -> 30.8 us  [permute(): lax.ppermute(block, ('seq', 'vocab'), [(dev(*e), dev(*to(*e))) for e in e...]
  transfers between devices with their start and end apart: 15 -> 20, of which waited for: 7 -> 8; matrix products, arithmetic and copies ran while one was open for 1% -> 1% of each run, Pallas kernels for 9% -> 9%
where the time goes in v6:
time: 78.2 us; the launch traced here: 77.8 us
  starting transfers between devices  30.8 us (39%)
  waiting for transfers between devices  16.3 us (21%)
  blocking collectives  11.6 us (15%)
  Pallas kernels  11.2 us (14%)
  local copies, waits for them, and re-layouts  6.73 us (9%)
  other arithmetic  0.97 us (1%)
    ppermute x20, starting transfers between devices, permute(): lax.ppermute(block, ('seq', 'vocab'), [(dev(*e), dev(*to(*e))) for e in e...  30.8 us
    ppermute x20, waiting for transfers between devices, permute(): lax.ppermute(block, ('seq', 'vocab'), [(dev(*e), dev(*to(*e))) for e in e...  16.3 us
    all_to_all x1, blocking collectives, shards(): got = lax.all_to_all(send, ('seq', 'vocab'), 0, 0, tiled=True)  11.6 us
    pallas_call x10, Pallas kernels, call(): pl.pallas_call(kernel, out_shape=outs, in_specs=specs or [VMEM] * len(arg...  11.2 us
    unnamed x24, local copies, waits for them, and re-layouts  6.73 us
  transfers between devices with their start and end apart: 20, of which 8 were waited for; matrix products, arithmetic and copies ran while one was open for 1% of the time, Pallas kernels for 9%

profile of v6, /device:TPU:0, one launch (start us, length us, event | category | flops | bytes accessed | tf_op | source)
XLA Modules:
  0.0 77.8 jit_solution(7982983986222287169)
XLA Ops:
  0.5 0.9 %pad_maximum_fusion.2.refs_0_ = bf16[2,128,256]{2,1,0:T(8,128)(2,1)S(1)} fusion(bf16[1,128,256]{2,1,0:T(8,128)(2,1)} %bitcast.44, bf16[1,128,256]{2,1,0:T(8,128)(2,1)} %bitcast.45), kind=kLoop, calls=%fused_computation.3 | loop fusion | flops 65536 | bytes 262144 | tf_op jit(solution)/shard_map/stack | solution.py:401
  1.4 4.5 %collective-permute-start.1 = (bf16[2,128,256]{2,1,0:T(8,128)(2,1)S(1)}, bf16[2,128,256]{2,1,0:T(8,128)(2,1)S(1)}, u32[]{:S(2)}, u32[]{:S(2)}) collective-permute-start(bf16[2,128,256]{2,1,0:T(8,128)(2,1)S(1)} %pad_maximum_fusion.2.refs_0_), channel_id=1, source_target_pairs={{0,8},{1,9},{2,10},{3,11},{4,12},{5,13},{6,14},{7,15},{8,16},{9,17... | collective-permute-start | bytes 393224 | tf_op jit(solution)/shard_map/ppermute | solution.py:373
  5.9 4.5 %collective-permute-start.2 = (bf16[2,128,256]{2,1,0:T(8,128)(2,1)S(1)}, bf16[2,128,256]{2,1,0:T(8,128)(2,1)S(1)}, u32[]{:S(2)}, u32[]{:S(2)}) collective-permute-start(bf16[2,128,256]{2,1,0:T(8,128)(2,1)S(1)} %pad_maximum_fusion.2.refs_0_), channel_id=1, source_target_pairs={{0,16},{1,17},{2,18},{3,19},{4,20},{5,21},{6,22},{7,23}} | collective-permute-start | bytes 393224 | tf_op jit(solution)/shard_map/ppermute | solution.py:373
  10.4 1.3 %collective-permute-start.3 = (bf16[2,128,256]{2,1,0:T(8,128)(2,1)S(1)}, bf16[2,128,256]{2,1,0:T(8,128)(2,1)S(1)}, u32[]{:S(2)}, u32[]{:S(2)}) collective-permute-start(bf16[2,128,256]{2,1,0:T(8,128)(2,1)S(1)} %pad_maximum_fusion.2.refs_0_), channel_id=1, source_target_pairs={{0,24},{1,25},{2,26},{3,27},{4,28},{5,29},{6,30},{7,31}} | collective-permute-start | bytes 393224 | tf_op jit(solution)/shard_map/ppermute | solution.py:373
  12.4 0.9 %copy-done.2 = bf16[128,1024]{1,0:T(8,128)(2,1)S(1)} copy-done((bf16[128,1024]{1,0:T(8,128)(2,1)S(1)}, bf16[128,1024]{1,0:T(8,128)(2,1)}, u32[]{:S(2)}) %copy-start.2) | copy-done | bytes 262168
  14.4 1.5 %collective-permute-start = (bf16[48,1024]{1,0:T(8,128)(2,1)S(1)}, bf16[48,1024]{1,0:T(8,128)(2,1)S(1)}, u32[]{:S(2)}, u32[]{:S(2)}) collective-permute-start(bf16[48,1024]{1,0:T(8,128)(2,1)S(1)} %get-tuple-element.23.after.q_own), channel_id=1, source_target_pairs={{0,4},{1,5},{2,6},{3,7},{4,0},{5,1},{6,2},{7,3},{8,12},{9,13},{10,... | collective-permute-start | bytes 294920 | tf_op jit(solution)/shard_map/ppermute | solution.py:373
  15.9 0.8 %copy-done.3 = bf16[128,256]{1,0:T(8,128)(2,1)S(1)} copy-done((bf16[128,256]{1,0:T(8,128)(2,1)S(1)}, bf16[128,256]{1,0:T(8,128)(2,1)}, u32[]{:S(2)}) %copy-start.3) | copy-done | bytes 65560
  16.7 0.8 %copy-done.4 = bf16[128,256]{1,0:T(8,128)(2,1)S(1)} copy-done((bf16[128,256]{1,0:T(8,128)(2,1)S(1)}, bf16[128,256]{1,0:T(8,128)(2,1)}, u32[]{:S(2)}) %copy-start.4) | copy-done | bytes 65560
  17.7 1.3 %collective-permute-done.q_other = bf16[48,1024]{1,0:T(8,128)(2,1)S(1)} collective-permute-done((bf16[48,1024]{1,0:T(8,128)(2,1)S(1)}, bf16[48,1024]{1,0:T(8,128)(2,1)S(1)}, u32[]{:S(2)}, u32[]{:S(2)}) %collective-permute-start) | collective-permute-done | bytes 98336 | tf_op jit(solution)/shard_map/ppermute | solution.py:373
  19.0 1.4 %shard_map.120 = (f32[48,1024]{1,0:T(8,128)S(1)}, f32[48,128]{1,0:T(8,128)S(1)}, bf16[48,1152]{1,0:T(8,128)(2,1)S(1)}) custom-call(f32[2,48,128]{2,1,0:T(8,128)S(1)} %get-tuple-element.22.blk_ref, bf16[48,1024]{1,0:T(8,128)(2,1)S(1)} %get-tuple-element.23.after.q_own, bf16[48,1024]{1,0:T(8,128)(2,1)S(1)} %collective-permute-done.q_other, ...), custom_call_target="tpu_custom_call" | custom-call | bytes 1032192 | tf_op jit(solution)/shard_map/pallas_call | solution.py:36
  20.5 1.6 %collective-permute-start.5 = (bf16[48,1152]{1,0:T(8,128)(2,1)S(1)}, bf16[48,1152]{1,0:T(8,128)(2,1)S(1)}, u32[]{:S(2)}, u32[]{:S(2)}) collective-permute-start(bf16[48,1152]{1,0:T(8,128)(2,1)S(1)} %get-tuple-element.28.after), channel_id=1, source_target_pairs={{0,4},{1,5},{2,6},{3,7},{4,0},{5,1},{6,2},{7,3},{8,12},{9,13},{10,... | collective-permute-start | bytes 331784 | tf_op jit(solution)/shard_map/ppermute | solution.py:373
  22.1 3.4 %copy-done = bf16[1024,4096]{1,0:T(8,128)(2,1)S(1)} copy-done((bf16[1024,4096]{1,0:T(8,128)(2,1)S(1)}, bf16[1024,4096]{1,0:T(8,128)(2,1)}, u32[]{:S(2)}) %copy-start) | copy-done | bytes 8388632
  26.1 1.7 %shard_map.122 = (f32[24,4096]{1,0:T(8,128)S(1)}, bf16[24,4096]{1,0:T(8,128)(2,1)S(1)}) custom-call(f32[48,1024]{1,0:T(8,128)S(1)} %get-tuple-element.26.own_ref, f32[48,128]{1,0:T(8,128)S(1)} %get-tuple-element.27.lse_ref, bf16[48,1152]{1,0:T(8,128)(2,1)S(1)} %collective-permute-done.5.got_ref, bf16[1024,4096]{1,0:T(8,128)(2,1)S(1)} %shard_map.121.w_ref), custom_call_target="tpu_custom_call" | custom-call | bytes 8720384 | tf_op jit(solution)/shard_map/pallas_call | solution.py:36
  27.9 1.4 %collective-permute-done.6 = bf16[24,4096]{1,0:T(8,128)(2,1)S(1)} collective-permute-done((bf16[24,4096]{1,0:T(8,128)(2,1)S(1)}, bf16[24,4096]{1,0:T(8,128)(2,1)S(1)}, u32[]{:S(2)}, u32[]{:S(2)}) %collective-permute-start.6) | collective-permute-done | bytes 196640 | tf_op jit(solution)/shard_map/ppermute | solution.py:373
  29.3 1.6 %collective-permute-start.7 = (bf16[24,4096]{1,0:T(8,128)(2,1)S(1)}, bf16[24,4096]{1,0:T(8,128)(2,1)S(1)}, u32[]{:S(2)}, u32[]{:S(2)}) collective-permute-start(bf16[24,4096]{1,0:T(8,128)(2,1)S(1)} %get-tuple-element.39), channel_id=1, source_target_pairs={{0,2},{1,3},{2,0},{3,1},{4,6},{5,7},{6,4},{7,5},{8,10},{9,11},{10,... | collective-permute-start | bytes 589832 | tf_op jit(solution)/shard_map/ppermute | solution.py:373
  30.9 1.7 %shard_map.123 = (bf16[48,4096]{1,0:T(8,128)(2,1)S(1)}, s32[8,256]{1,0:T(8,128)S(1)}, f32[128,128]{1,0:T(8,128)S(1)}, f32[8,128]{1,0:T(8,128)S(1)}) custom-call(s32[32]{0:T(128)S(1)} %copy-done.9, s32[8,128]{1,0:T(8,128)S(1)} %bitcast.42, s32[8,128]{1,0:T(8,128)S(1)} %bitcast.43, bf16[128,4096]{1,0:T(8,128)(2,1)S(1)} %copy-done.1, ...), custom_call_target="tpu_custom_call" | custom-call | bytes 1253504 | tf_op jit(solution)/shard_map/pallas_call | solution.py:36
  32.6 3.7 %collective-permute-done.7.refs_0_ = bf16[24,4096]{1,0:T(8,128)(2,1)S(1)} collective-permute-done((bf16[24,4096]{1,0:T(8,128)(2,1)S(1)}, bf16[24,4096]{1,0:T(8,128)(2,1)S(1)}, u32[]{:S(2)}, u32[]{:S(2)}) %collective-permute-start.7) | collective-permute-done | bytes 196640 | tf_op jit(solution)/shard_map/ppermute | solution.py:373
  36.6 4.1 %collective-permute-start.12 = (bf16[24,2048]{1,0:T(8,128)(2,1)S(1)}, bf16[24,2048]{1,0:T(8,128)(2,1)S(1)}, u32[]{:S(2)}, u32[]{:S(2)}) collective-permute-start(bf16[24,2048]{1,0:T(8,128)(2,1)S(1)} %get-tuple-element.36.after), channel_id=1, source_target_pairs={{0,24},{1,25},{2,26},{3,27},{4,28},{5,29},{6,30},{7,31},{8,16},{9,... | collective-permute-start | bytes 294920 | tf_op jit(solution)/shard_map/ppermute | solution.py:373
  41.1 3.1 %collective-permute-done.12.refs_5_ = bf16[24,2048]{1,0:T(8,128)(2,1)S(1)} collective-permute-done((bf16[24,2048]{1,0:T(8,128)(2,1)S(1)}, bf16[24,2048]{1,0:T(8,128)(2,1)S(1)}, u32[]{:S(2)}, u32[]{:S(2)}) %collective-permute-start.12) | collective-permute-done | bytes 98336 | tf_op jit(solution)/shard_map/ppermute | solution.py:373
  44.2 1.5 %collective-permute-start.13 = (bf16[1,24,2048]{2,1,0:T(8,128)(2,1)S(1)}, bf16[1,24,2048]{2,1,0:T(8,128)(2,1)S(1)}, u32[]{:S(2)}, u32[]{:S(2)}) collective-permute-start(bf16[1,24,2048]{2,1,0:T(8,128)(2,1)S(1)} %bitcast.23), channel_id=1, source_target_pairs={{0,2},{1,5},{2,0},{3,7},{4,6},{5,1},{6,4},{7,3},{8,10},{9,13},{10,... | collective-permute-start | bytes 294920 | tf_op jit(solution)/shard_map/ppermute | solution.py:373
  45.7 1.9 %collective-permute-start.15 = (bf16[24,2048]{1,0:T(8,128)(2,1)S(1)}, bf16[24,2048]{1,0:T(8,128)(2,1)S(1)}, u32[]{:S(2)}, u32[]{:S(2)}) collective-permute-start(bf16[24,2048]{1,0:T(8,128)(2,1)S(1)} %get-tuple-element.36.after), channel_id=1, source_target_pairs={{0,16},{1,17},{2,18},{3,19},{4,20},{5,21},{6,22},{7,23},{8,24},{9,... | collective-permute-start | bytes 294920 | tf_op jit(solution)/shard_map/ppermute | solution.py:373
  47.5 0.7 collective-permute-start.8
  49.2 1.0 %collective-permute-start.14 = (bf16[2,1,24,2048]{3,2,1,0:T(8,128)(2,1)S(1)}, bf16[2,1,24,2048]{3,2,1,0:T(8,128)(2,1)S(1)}, u32[]{:S(2)}, u32[]{:S(2)}) collective-permute-start(bf16[2,1,24,2048]{3,2,1,0:T(8,128)(2,1)S(1)} %pad_maximum_fusion.1), channel_id=1, source_target_pairs={{0,4},{1,3},{2,6},{3,1},{4,0},{5,7},{6,2},{7,5},{8,12},{9,11},{10,... | collective-permute-start | bytes 589832 | tf_op jit(solution)/shard_map/ppermute | solution.py:373
  50.2 3.0 %collective-permute-done.10 = bf16[1,24,2048]{2,1,0:T(8,128)(2,1)S(1)} collective-permute-done((bf16[1,24,2048]{2,1,0:T(8,128)(2,1)S(1)}, bf16[1,24,2048]{2,1,0:T(8,128)(2,1)S(1)}, u32[]{:S(2)}, u32[]{:S(2)}) %collective-permute-start.10) | collective-permute-done | bytes 98336 | tf_op jit(solution)/shard_map/ppermute | solution.py:373
  53.2 1.0 %collective-permute-start.11 = (bf16[2,1,24,2048]{3,2,1,0:T(8,128)(2,1)S(1)}, bf16[2,1,24,2048]{3,2,1,0:T(8,128)(2,1)S(1)}, u32[]{:S(2)}, u32[]{:S(2)}) collective-permute-start(bf16[2,1,24,2048]{3,2,1,0:T(8,128)(2,1)S(1)} %pad_maximum_fusion), channel_id=1, source_target_pairs={{0,4},{1,3},{2,6},{3,1},{4,0},{5,7},{6,2},{7,5},{8,12},{9,11},{10,... | collective-permute-start | bytes 589832 | tf_op jit(solution)/shard_map/ppermute | solution.py:373
  54.8 0.8 collective-permute-start.17
  55.6 2.2 %collective-permute-start.18 = (bf16[1,24,2048]{2,1,0:T(8,128)(2,1)S(1)}, bf16[1,24,2048]{2,1,0:T(8,128)(2,1)S(1)}, u32[]{:S(2)}, u32[]{:S(2)}) collective-permute-start(bf16[1,24,2048]{2,1,0:T(8,128)(2,1)S(1)} %bitcast.35), channel_id=1, source_target_pairs={{0,6},{1,7},{2,4},{3,5},{4,2},{5,3},{6,0},{7,1},{8,14},{9,15},{10,... | collective-permute-start | bytes 294920 | tf_op jit(solution)/shard_map/ppermute | solution.py:373
  57.8 1.0 %shard_map.125 = (bf16[592,4096]{1,0:T(8,128)(2,1)S(1)}, bf16[592,4096]{1,0:T(8,128)(2,1)S(1)}) custom-call(bf16[24,2048]{1,0:T(8,128)(2,1)S(1)} %get-tuple-element.36.after, bf16[592,4096]{1,0:T(8,128)(2,1)S(1)} %bitcast.22, bf16[592,4096]{1,0:T(8,128)(2,1)S(1)} %collective-permute-done.19.refs_1_), custom_call_target="tpu_custom_call" | custom-call | bytes 9797632 | tf_op jit(solution)/shard_map/pallas_call | solution.py:36
  58.9 3.2 %collective-permute-done.17 = bf16[1,24,2048]{2,1,0:T(8,128)(2,1)S(1)} collective-permute-done((bf16[1,24,2048]{2,1,0:T(8,128)(2,1)S(1)}, bf16[1,24,2048]{2,1,0:T(8,128)(2,1)S(1)}, u32[]{:S(2)}, u32[]{:S(2)}) %collective-permute-start.17) | collective-permute-done | bytes 98336 | tf_op jit(solution)/shard_map/ppermute | solution.py:373
  62.1 3.2 %shard_map.126 = f32[32,1,128]{2,1,0:T(1,128)S(1)} custom-call(s32[8,256]{1,0:T(8,128)S(1)} %get-tuple-element.32.target_ref, bf16[24,4096]{1,0:T(8,128)(2,1)S(1)} %get-tuple-element.35.refs_0_, bf16[24,4096]{1,0:T(8,128)(2,1)S(1)} %collective-permute-done.8.refs_1_, bf16[24,2048]{1,0:T(8,128)(2,1)S(1)} %collective-permute-done.9.refs_2_, ...), custom_call_target="tpu_custom_call" | custom-call | flops 1862270976 | bytes 11280384 | tf_op jit(solution)/shard_map/pallas_call | solution.py:36
  65.3 11.6 %all_to_all.8 = f32[32,1,128]{2,1,0:T(1,128)S(1)} all-to-all(f32[32,1,128]{2,1,0:T(1,128)S(1)} %shard_map.126), channel_id=1, replica_groups=mesh['seq'=8,'vocab'=4] {'seq','vocab'}, dimensions={0} | all-to-all | bytes 32768 | tf_op jit(solution)/shard_map/all_to_all | solution.py:490
  76.9 0.8 %shard_map.127 = f32[1,128]{1,0:T(1,128)} custom-call(f32[128,128]{1,0:T(8,128)S(1)} %get-tuple-element.30.chosen_ref, f32[8,128]{1,0:T(8,128)S(1)} %get-tuple-element.31.weight_ref, f32[32,128]{1,0:T(8,128)S(1)} %bitcast.39), custom_call_target="tpu_custom_call" | custom-call | bytes 86016 | tf_op jit(solution)/shard_map/pallas_call | solution.py:36
  (48 shorter events, 5.4 us)
Async XLA Ops:
  0.0 55.6 %collective-permute-start.19 = (bf16[592,4096]{1,0:T(8,128)(2,1)}, bf16[592,4096]{1,0:T(8,128)(2,1)S(1)}, u32[]{:S(2)}, u32[]{:S(2)}) collective-permute-start(bf16[592,4096]{1,0:T(8,128)(2,1)} %refs_0_.5), channel_id=1, source_target_pairs={{0,1},{1,0},{2,3},{3,2},{4,5},{5,4},{6,7},{7,6},{8,9},{9,8},{10,11... | collective-permute-start | bytes 14549000 | tf_op jit(solution)/shard_map/ppermute | solution.py:373
  1.4 10.3 %collective-permute-start.1 = (bf16[2,128,256]{2,1,0:T(8,128)(2,1)S(1)}, bf16[2,128,256]{2,1,0:T(8,128)(2,1)S(1)}, u32[]{:S(2)}, u32[]{:S(2)}) collective-permute-start(bf16[2,128,256]{2,1,0:T(8,128)(2,1)S(1)} %pad_maximum_fusion.2.refs_0_), channel_id=1, source_target_pairs={{0,8},{1,9},{2,10},{3,11},{4,12},{5,13},{6,14},{7,15},{8,16},{9,17... | collective-permute-start | bytes 393224 | tf_op jit(solution)/shard_map/ppermute | solution.py:373
  5.9 13.2 %collective-permute-start.2 = (bf16[2,128,256]{2,1,0:T(8,128)(2,1)S(1)}, bf16[2,128,256]{2,1,0:T(8,128)(2,1)S(1)}, u32[]{:S(2)}, u32[]{:S(2)}) collective-permute-start(bf16[2,128,256]{2,1,0:T(8,128)(2,1)S(1)} %pad_maximum_fusion.2.refs_0_), channel_id=1, source_target_pairs={{0,16},{1,17},{2,18},{3,19},{4,20},{5,21},{6,22},{7,23}} | collective-permute-start | bytes 393224 | tf_op jit(solution)/shard_map/ppermute | solution.py:373
  10.4 8.7 %collective-permute-start.3 = (bf16[2,128,256]{2,1,0:T(8,128)(2,1)S(1)}, bf16[2,128,256]{2,1,0:T(8,128)(2,1)S(1)}, u32[]{:S(2)}, u32[]{:S(2)}) collective-permute-start(bf16[2,128,256]{2,1,0:T(8,128)(2,1)S(1)} %pad_maximum_fusion.2.refs_0_), channel_id=1, source_target_pairs={{0,24},{1,25},{2,26},{3,27},{4,28},{5,29},{6,30},{7,31}} | collective-permute-start | bytes 393224 | tf_op jit(solution)/shard_map/ppermute | solution.py:373
  11.7 7.4 %collective-permute-start.4 = (bf16[2,128,256]{2,1,0:T(8,128)(2,1)S(1)}, bf16[2,128,256]{2,1,0:T(8,128)(2,1)S(1)}, u32[]{:S(2)}, u32[]{:S(2)}) collective-permute-start(bf16[2,128,256]{2,1,0:T(8,128)(2,1)S(1)} %collective-permute-done.1.refs_1_), channel_id=1, source_target_pairs={{16,24},{17,25},{18,26},{19,27},{20,28},{21,29},{22,30},{23,31}} | collective-permute-start | bytes 393224 | tf_op jit(solution)/shard_map/ppermute | solution.py:373
  12.4 1.0 %copy-start.2 = (bf16[128,1024]{1,0:T(8,128)(2,1)S(1)}, bf16[128,1024]{1,0:T(8,128)(2,1)}, u32[]{:S(2)}) copy-start(bf16[128,1024]{1,0:T(8,128)(2,1)} %q_ref.1) | copy-start | bytes 786436
  13.3 0.7 copy-start.6
  14.4 4.7 %collective-permute-start = (bf16[48,1024]{1,0:T(8,128)(2,1)S(1)}, bf16[48,1024]{1,0:T(8,128)(2,1)S(1)}, u32[]{:S(2)}, u32[]{:S(2)}) collective-permute-start(bf16[48,1024]{1,0:T(8,128)(2,1)S(1)} %get-tuple-element.23.after.q_own), channel_id=1, source_target_pairs={{0,4},{1,5},{2,6},{3,7},{4,0},{5,1},{6,2},{7,3},{8,12},{9,13},{10,... | collective-permute-start | bytes 294920 | tf_op jit(solution)/shard_map/ppermute | solution.py:373
  15.9 0.8 %copy-start.3 = (bf16[128,256]{1,0:T(8,128)(2,1)S(1)}, bf16[128,256]{1,0:T(8,128)(2,1)}, u32[]{:S(2)}) copy-start(bf16[128,256]{1,0:T(8,128)(2,1)} %refs_0_.3) | copy-start | bytes 196612
  16.7 0.8 %copy-start.4 = (bf16[128,256]{1,0:T(8,128)(2,1)S(1)}, bf16[128,256]{1,0:T(8,128)(2,1)}, u32[]{:S(2)}) copy-start(bf16[128,256]{1,0:T(8,128)(2,1)} %refs_1_.1) | copy-start | bytes 196612
  20.5 5.5 %collective-permute-start.5 = (bf16[48,1152]{1,0:T(8,128)(2,1)S(1)}, bf16[48,1152]{1,0:T(8,128)(2,1)S(1)}, u32[]{:S(2)}, u32[]{:S(2)}) collective-permute-start(bf16[48,1152]{1,0:T(8,128)(2,1)S(1)} %get-tuple-element.28.after), channel_id=1, source_target_pairs={{0,4},{1,5},{2,6},{3,7},{4,0},{5,1},{6,2},{7,3},{8,12},{9,13},{10,... | collective-permute-start | bytes 331784 | tf_op jit(solution)/shard_map/ppermute | solution.py:373
  22.1 3.4 %copy-start = (bf16[1024,4096]{1,0:T(8,128)(2,1)S(1)}, bf16[1024,4096]{1,0:T(8,128)(2,1)}, u32[]{:S(2)}) copy-start(bf16[1024,4096]{1,0:T(8,128)(2,1)} %refs_0_.4) | copy-start | bytes 25165828
  26.0 31.7 %slice-start = ((s8[4849664]{0:T(1024)(128)(4,1)}), s8[4194304]{0:T(1024)(128)(4,1)S(1)}, s32[]{:S(2)}) async-start(s8[4849664]{0:T(1024)(128)(4,1)} %bitcast.21), calls=%async_computation.1 | async-start | bytes 8388608
  26.0 4.9 %copy-start.1 = (bf16[128,4096]{1,0:T(8,128)(2,1)S(1)}, bf16[128,4096]{1,0:T(8,128)(2,1)}, u32[]{:S(2)}) copy-start(bf16[128,4096]{1,0:T(8,128)(2,1)} %res_ref.1) | copy-start | bytes 3145732
  26.0 4.9 %copy-start.7 = (s32[1024]{0:T(1024)S(1)}, s32[1024]{0:T(1024)}, u32[]{:S(2)}) copy-start(s32[1024]{0:T(1024)} %param.22) | copy-start | bytes 12292
  26.1 4.9 %copy-start.8 = (s32[1024]{0:T(1024)S(1)}, s32[1024]{0:T(1024)}, u32[]{:S(2)}) copy-start(s32[1024]{0:T(1024)} %param.21) | copy-start | bytes 12292
  26.1 4.8 %copy-start.9 = (s32[32]{0:T(128)S(1)}, s32[32]{0:T(128)}, u32[]{:S(2)}) copy-start(s32[32]{0:T(128)} %levels_ref.1) | copy-start | bytes 388
  26.1 10.3 %copy-start.5 = (f32[4096]{0:T(1024)S(1)}, f32[4096]{0:T(1024)}, u32[]{:S(2)}) copy-start(f32[4096]{0:T(1024)} %param.19) | copy-start | bytes 49156
  26.1 31.7 %slice-start.1 = ((s8[4849664]{0:T(1024)(128)(4,1)}), s8[655360]{0:T(1024)(128)(4,1)S(1)}, s32[]{:S(2)}) async-start(s8[4849664]{0:T(1024)(128)(4,1)} %bitcast.21), calls=%async_computation.2 | async-start | bytes 1310720
  27.8 1.5 %collective-permute-start.6 = (bf16[24,4096]{1,0:T(8,128)(2,1)S(1)}, bf16[24,4096]{1,0:T(8,128)(2,1)S(1)}, u32[]{:S(2)}, u32[]{:S(2)}) collective-permute-start(bf16[24,4096]{1,0:T(8,128)(2,1)S(1)} %get-tuple-element.29.after_ref), channel_id=1, source_target_pairs={{0,1},{1,0},{2,3},{3,2},{4,5},{5,4},{6,7},{7,6},{8,9},{9,8},{10,11... | collective-permute-start | bytes 589832 | tf_op jit(solution)/shard_map/ppermute | solution.py:373
  29.3 7.0 %collective-permute-start.7 = (bf16[24,4096]{1,0:T(8,128)(2,1)S(1)}, bf16[24,4096]{1,0:T(8,128)(2,1)S(1)}, u32[]{:S(2)}, u32[]{:S(2)}) collective-permute-start(bf16[24,4096]{1,0:T(8,128)(2,1)S(1)} %get-tuple-element.39), channel_id=1, source_target_pairs={{0,2},{1,3},{2,0},{3,1},{4,6},{5,7},{6,4},{7,5},{8,10},{9,11},{10,... | collective-permute-start | bytes 589832 | tf_op jit(solution)/shard_map/ppermute | solution.py:373
  36.6 7.5 %collective-permute-start.12 = (bf16[24,2048]{1,0:T(8,128)(2,1)S(1)}, bf16[24,2048]{1,0:T(8,128)(2,1)S(1)}, u32[]{:S(2)}, u32[]{:S(2)}) collective-permute-start(bf16[24,2048]{1,0:T(8,128)(2,1)S(1)} %get-tuple-element.36.after), channel_id=1, source_target_pairs={{0,24},{1,25},{2,26},{3,27},{4,28},{5,29},{6,30},{7,31},{8,16},{9,... | collective-permute-start | bytes 294920 | tf_op jit(solution)/shard_map/ppermute | solution.py:373
  40.7 7.5 %collective-permute-start.9 = (bf16[24,2048]{1,0:T(8,128)(2,1)S(1)}, bf16[24,2048]{1,0:T(8,128)(2,1)S(1)}, u32[]{:S(2)}, u32[]{:S(2)}) collective-permute-start(bf16[24,2048]{1,0:T(8,128)(2,1)S(1)} %get-tuple-element.36.after), channel_id=1, source_target_pairs={{0,8},{1,9},{2,10},{3,11},{4,12},{5,13},{6,14},{7,15},{8,0},{9,1},... | collective-permute-start | bytes 294920 | tf_op jit(solution)/shard_map/ppermute | solution.py:373
  44.2 5.0 %collective-permute-start.13 = (bf16[1,24,2048]{2,1,0:T(8,128)(2,1)S(1)}, bf16[1,24,2048]{2,1,0:T(8,128)(2,1)S(1)}, u32[]{:S(2)}, u32[]{:S(2)}) collective-permute-start(bf16[1,24,2048]{2,1,0:T(8,128)(2,1)S(1)} %bitcast.23), channel_id=1, source_target_pairs={{0,2},{1,5},{2,0},{3,7},{4,6},{5,1},{6,4},{7,3},{8,10},{9,13},{10,... | collective-permute-start | bytes 294920 | tf_op jit(solution)/shard_map/ppermute | solution.py:373
  45.7 8.6 %collective-permute-start.15 = (bf16[24,2048]{1,0:T(8,128)(2,1)S(1)}, bf16[24,2048]{1,0:T(8,128)(2,1)S(1)}, u32[]{:S(2)}, u32[]{:S(2)}) collective-permute-start(bf16[24,2048]{1,0:T(8,128)(2,1)S(1)} %get-tuple-element.36.after), channel_id=1, source_target_pairs={{0,16},{1,17},{2,18},{3,19},{4,20},{5,21},{6,22},{7,23},{8,24},{9,... | collective-permute-start | bytes 294920 | tf_op jit(solution)/shard_map/ppermute | solution.py:373
  47.5 7.3 %collective-permute-start.8 = (bf16[24,4096]{1,0:T(8,128)(2,1)S(1)}, bf16[24,4096]{1,0:T(8,128)(2,1)S(1)}, u32[]{:S(2)}, u32[]{:S(2)}) collective-permute-start(bf16[24,4096]{1,0:T(8,128)(2,1)S(1)} %get-tuple-element.35.refs_0_), channel_id=1, source_target_pairs={{0,4},{1,5},{2,6},{3,7},{4,0},{5,1},{6,2},{7,3},{8,12},{9,13},{10,... | collective-permute-start | bytes 589832 | tf_op jit(solution)/shard_map/ppermute | solution.py:373
  48.3 4.9 %collective-permute-start.10 = (bf16[1,24,2048]{2,1,0:T(8,128)(2,1)S(1)}, bf16[1,24,2048]{2,1,0:T(8,128)(2,1)S(1)}, u32[]{:S(2)}, u32[]{:S(2)}) collective-permute-start(bf16[1,24,2048]{2,1,0:T(8,128)(2,1)S(1)} %bitcast.25), channel_id=1, source_target_pairs={{0,2},{1,5},{2,0},{3,7},{4,6},{5,1},{6,4},{7,3},{8,10},{9,13},{10,... | collective-permute-start | bytes 294920 | tf_op jit(solution)/shard_map/ppermute | solution.py:373
  49.2 12.9 %collective-permute-start.14 = (bf16[2,1,24,2048]{3,2,1,0:T(8,128)(2,1)S(1)}, bf16[2,1,24,2048]{3,2,1,0:T(8,128)(2,1)S(1)}, u32[]{:S(2)}, u32[]{:S(2)}) collective-permute-start(bf16[2,1,24,2048]{3,2,1,0:T(8,128)(2,1)S(1)} %pad_maximum_fusion.1), channel_id=1, source_target_pairs={{0,4},{1,3},{2,6},{3,1},{4,0},{5,7},{6,2},{7,5},{8,12},{9,11},{10,... | collective-permute-start | bytes 589832 | tf_op jit(solution)/shard_map/ppermute | solution.py:373
  53.2 8.9 %collective-permute-start.11 = (bf16[2,1,24,2048]{3,2,1,0:T(8,128)(2,1)S(1)}, bf16[2,1,24,2048]{3,2,1,0:T(8,128)(2,1)S(1)}, u32[]{:S(2)}, u32[]{:S(2)}) collective-permute-start(bf16[2,1,24,2048]{3,2,1,0:T(8,128)(2,1)S(1)} %pad_maximum_fusion), channel_id=1, source_target_pairs={{0,4},{1,3},{2,6},{3,1},{4,0},{5,7},{6,2},{7,5},{8,12},{9,11},{10,... | collective-permute-start | bytes 589832 | tf_op jit(solution)/shard_map/ppermute | solution.py:373
  54.3 4.6 %collective-permute-start.16 = (bf16[1,24,2048]{2,1,0:T(8,128)(2,1)S(1)}, bf16[1,24,2048]{2,1,0:T(8,128)(2,1)S(1)}, u32[]{:S(2)}, u32[]{:S(2)}) collective-permute-start(bf16[1,24,2048]{2,1,0:T(8,128)(2,1)S(1)} %bitcast.33), channel_id=1, source_target_pairs={{0,2},{1,3},{2,0},{3,1},{4,6},{5,7},{6,4},{7,5},{8,10},{9,11},{10,... | collective-permute-start | bytes 294920 | tf_op jit(solution)/shard_map/ppermute | solution.py:373
  54.8 7.3 %collective-permute-start.17 = (bf16[1,24,2048]{2,1,0:T(8,128)(2,1)S(1)}, bf16[1,24,2048]{2,1,0:T(8,128)(2,1)S(1)}, u32[]{:S(2)}, u32[]{:S(2)}) collective-permute-start(bf16[1,24,2048]{2,1,0:T(8,128)(2,1)S(1)} %bitcast.34), channel_id=1, source_target_pairs={{0,4},{1,5},{2,6},{3,7},{4,0},{5,1},{6,2},{7,3},{8,12},{9,13},{10,... | collective-permute-start | bytes 294920 | tf_op jit(solution)/shard_map/ppermute | solution.py:373
  55.6 6.5 %collective-permute-start.18 = (bf16[1,24,2048]{2,1,0:T(8,128)(2,1)S(1)}, bf16[1,24,2048]{2,1,0:T(8,128)(2,1)S(1)}, u32[]{:S(2)}, u32[]{:S(2)}) collective-permute-start(bf16[1,24,2048]{2,1,0:T(8,128)(2,1)S(1)} %bitcast.35), channel_id=1, source_target_pairs={{0,6},{1,7},{2,4},{3,5},{4,2},{5,3},{6,0},{7,1},{8,14},{9,15},{10,... | collective-permute-start | bytes 294920 | tf_op jit(solution)/shard_map/ppermute | solution.py:373

commit v7 on v6

--- a/solution.py
+++ b/solution.py
@@ -22,7 +22,6 @@
 norm_eps = 1e-06
 
 GROUPS = [[1], [3], [2]]
-STRAIGHT = [[2]]
 
 VMEM = pl.BlockSpec(memory_space=pltpu.VMEM)
 SMEM = pl.BlockSpec(memory_space=pltpu.SMEM)
@@ -244,10 +243,6 @@
     return GROUPS if Z == 4 else [range(1, Z)]
 
 
-def pieces_of(group, mixed, X):
-    return X if not mixed else 4 if group in STRAIGHT else 3
-
-
 def row_order(Z):
     return [(0, False), (0, True)] + [(k, other) for group in groups_of(Z) for other in (False, True) for k in group]
 
@@ -257,8 +252,7 @@
     share = refs[0].shape[1] // X
     n_rows = Y * Z * HALF
     sizes = [len(g) for g in groups_of(Z)]
-    counts = [pieces_of(g, mixed, X) for g in groups_of(Z)]
-    n_refs = 2 + sum(counts)
+    n_refs = 2 + (3 if mixed else X) * len(sizes)
     (own, across, *pieces), (w_own, w_other, out_ref, *rows) = refs[:n_refs], refs[n_refs:]
     base = 2 * HALF
     for k in range(X):
@@ -267,28 +261,24 @@
         rows[k][HALF:base] = across[:, pl.ds(at, share)]
     for i, size in enumerate(sizes):
         n = size * HALF
-        mine = pieces[sum(counts[:i]) : sum(counts[: i + 1])]
-        if mixed and counts[i] == 4:
-            for ref, (at, block) in zip(mine, ((0, rows[0]), (0, rows[1]), (n, rows[0]), (n, rows[1]))):
-                block[base + at : base + at + n] = ref[...]
-        elif mixed:
-            column, step1, step2 = mine
+        if mixed:
+            column, step1, step2 = pieces[3 * i : 3 * i + 3]
             near, far = rows
             near[base : base + n] = column[...]
             far[base + n : base + 2 * n] = step2[n:]
 
-            @pl.when(c == 0)
+            @pl.when(c != 0)
             def _(base=base, n=n, step1=step1, step2=step2):
                 near[base + n : base + 2 * n] = step2[:n]
                 far[base : base + n] = step1[...]
 
-            @pl.when(c != 0)
+            @pl.when(c == 0)
             def _(base=base, n=n, step1=step1, step2=step2):
                 near[base + n : base + 2 * n] = step1[...]
                 far[base : base + n] = step2[:n]
         else:
             for k in range(X):
-                rows[k][base : base + Y * n] = mine[k][...]
+                rows[k][base : base + Y * n] = pieces[X * i + k][...]
         base += Y * n
     logits = []
     for w in (w_own, w_other):
@@ -465,15 +455,10 @@
     for group in groups_of(Z):
         n = len(group) * HALF
         column = jnp.stack([slabs[k] for k in group])
-        if mixed and group in STRAIGHT:
-            over_x = x_shift(column, 1)
-            over_y = y_flip(column)
-            over_xy = permute(column, lambda a, b, e, f: (a, 1 - b, 1 - e, f))
-            rows += [a.reshape(n, share) for a in (column, over_x, over_y, over_xy)]
-        elif mixed:
-            step1 = mixed_flip(column, 0)
+        if mixed:
+            step1 = mixed_flip(column, 1)
             both = jnp.stack([column, step1])
-            step2 = mixed_flip(both, 1)
+            step2 = mixed_flip(both, 0)
             rows += [column.reshape(n, share), step1.reshape(n, share), step2.reshape(Y * n, share)]
         else:
             pair = jnp.stack([column, y_flip(column)])

time: 78.2 us -> 83.4 us (1.066)
  waiting for transfers between devices: 16.3 us -> 25.4 us
  starting transfers between devices: 30.8 us -> 26.8 us
    ppermute x20 -> x19, waiting for transfers between devices: 16.3 us -> 25.4 us  [permute(): lax.ppermute(block, ('seq', 'vocab'), [(dev(*e), dev(*to(*e))) for e in e...]
    ppermute x20 -> x19, starting transfers between devices: 30.8 us -> 26.8 us  [permute(): lax.ppermute(block, ('seq', 'vocab'), [(dev(*e), dev(*to(*e))) for e in e...]
  transfers between devices with their start and end apart: 20 -> 19, of which waited for: 8 -> 9; matrix products, arithmetic and copies ran while one was open for 1% -> 1% of each run, Pallas kernels for 9% -> 9%
where the time goes in v7:
time: 83.4 us; the launch traced here: 83 us
  starting transfers between devices  26.8 us (32%)
  waiting for transfers between devices  25.4 us (30%)
  blocking collectives  11.7 us (14%)
  Pallas kernels  11.2 us (13%)
  local copies, waits for them, and re-layouts  6.73 us (8%)
  other arithmetic  0.99 us (1%)
    ppermute x19, starting transfers between devices, permute(): lax.ppermute(block, ('seq', 'vocab'), [(dev(*e), dev(*to(*e))) for e in e...  26.8 us
    ppermute x19, waiting for transfers between devices, permute(): lax.ppermute(block, ('seq', 'vocab'), [(dev(*e), dev(*to(*e))) for e in e...  25.4 us
    all_to_all x1, blocking collectives, shards(): got = lax.all_to_all(send, ('seq', 'vocab'), 0, 0, tiled=True)  11.7 us
    pallas_call x10, Pallas kernels, call(): pl.pallas_call(kernel, out_shape=outs, in_specs=specs or [VMEM] * len(arg...  11.2 us
    unnamed x24, local copies, waits for them, and re-layouts  6.73 us
  transfers between devices with their start and end apart: 19, of which 9 were waited for; matrix products, arithmetic and copies ran while one was open for 1% of the time, Pallas kernels for 9%

profile of v7, /device:TPU:0, one launch (start us, length us, event | category | flops | bytes accessed | tf_op | source)
XLA Modules:
  0.0 83.0 jit_solution(6947194955903740861)
XLA Ops:
  0.5 0.9 %pad_maximum_fusion.3.refs_0_ = bf16[2,128,256]{2,1,0:T(8,128)(2,1)S(1)} fusion(bf16[1,128,256]{2,1,0:T(8,128)(2,1)} %bitcast.44, bf16[1,128,256]{2,1,0:T(8,128)(2,1)} %bitcast.45), kind=kLoop, calls=%fused_computation.4 | loop fusion | flops 65536 | bytes 262144 | tf_op jit(solution)/shard_map/stack | solution.py:391
  1.4 4.5 %collective-permute-start.1 = (bf16[2,128,256]{2,1,0:T(8,128)(2,1)S(1)}, bf16[2,128,256]{2,1,0:T(8,128)(2,1)S(1)}, u32[]{:S(2)}, u32[]{:S(2)}) collective-permute-start(bf16[2,128,256]{2,1,0:T(8,128)(2,1)S(1)} %pad_maximum_fusion.3.refs_0_), channel_id=1, source_target_pairs={{0,8},{1,9},{2,10},{3,11},{4,12},{5,13},{6,14},{7,15},{8,16},{9,17... | collective-permute-start | bytes 393224 | tf_op jit(solution)/shard_map/ppermute | solution.py:363
  5.9 4.5 %collective-permute-start.2 = (bf16[2,128,256]{2,1,0:T(8,128)(2,1)S(1)}, bf16[2,128,256]{2,1,0:T(8,128)(2,1)S(1)}, u32[]{:S(2)}, u32[]{:S(2)}) collective-permute-start(bf16[2,128,256]{2,1,0:T(8,128)(2,1)S(1)} %pad_maximum_fusion.3.refs_0_), channel_id=1, source_target_pairs={{0,16},{1,17},{2,18},{3,19},{4,20},{5,21},{6,22},{7,23}} | collective-permute-start | bytes 393224 | tf_op jit(solution)/shard_map/ppermute | solution.py:363
  10.4 1.3 %collective-permute-start.3 = (bf16[2,128,256]{2,1,0:T(8,128)(2,1)S(1)}, bf16[2,128,256]{2,1,0:T(8,128)(2,1)S(1)}, u32[]{:S(2)}, u32[]{:S(2)}) collective-permute-start(bf16[2,128,256]{2,1,0:T(8,128)(2,1)S(1)} %pad_maximum_fusion.3.refs_0_), channel_id=1, source_target_pairs={{0,24},{1,25},{2,26},{3,27},{4,28},{5,29},{6,30},{7,31}} | collective-permute-start | bytes 393224 | tf_op jit(solution)/shard_map/ppermute | solution.py:363
  12.4 0.9 %copy-done.2 = bf16[128,1024]{1,0:T(8,128)(2,1)S(1)} copy-done((bf16[128,1024]{1,0:T(8,128)(2,1)S(1)}, bf16[128,1024]{1,0:T(8,128)(2,1)}, u32[]{:S(2)}) %copy-start.2) | copy-done | bytes 262168
  14.4 1.5 %collective-permute-start = (bf16[48,1024]{1,0:T(8,128)(2,1)S(1)}, bf16[48,1024]{1,0:T(8,128)(2,1)S(1)}, u32[]{:S(2)}, u32[]{:S(2)}) collective-permute-start(bf16[48,1024]{1,0:T(8,128)(2,1)S(1)} %get-tuple-element.23.after.q_own), channel_id=1, source_target_pairs={{0,4},{1,5},{2,6},{3,7},{4,0},{5,1},{6,2},{7,3},{8,12},{9,13},{10,... | collective-permute-start | bytes 294920 | tf_op jit(solution)/shard_map/ppermute | solution.py:363
  15.9 0.8 %copy-done.3 = bf16[128,256]{1,0:T(8,128)(2,1)S(1)} copy-done((bf16[128,256]{1,0:T(8,128)(2,1)S(1)}, bf16[128,256]{1,0:T(8,128)(2,1)}, u32[]{:S(2)}) %copy-start.3) | copy-done | bytes 65560
  16.7 0.8 %copy-done.4 = bf16[128,256]{1,0:T(8,128)(2,1)S(1)} copy-done((bf16[128,256]{1,0:T(8,128)(2,1)S(1)}, bf16[128,256]{1,0:T(8,128)(2,1)}, u32[]{:S(2)}) %copy-start.4) | copy-done | bytes 65560
  17.7 1.3 %collective-permute-done.q_other = bf16[48,1024]{1,0:T(8,128)(2,1)S(1)} collective-permute-done((bf16[48,1024]{1,0:T(8,128)(2,1)S(1)}, bf16[48,1024]{1,0:T(8,128)(2,1)S(1)}, u32[]{:S(2)}, u32[]{:S(2)}) %collective-permute-start) | collective-permute-done | bytes 98336 | tf_op jit(solution)/shard_map/ppermute | solution.py:363
  19.0 1.4 %shard_map.120 = (f32[48,1024]{1,0:T(8,128)S(1)}, f32[48,128]{1,0:T(8,128)S(1)}, bf16[48,1152]{1,0:T(8,128)(2,1)S(1)}) custom-call(f32[2,48,128]{2,1,0:T(8,128)S(1)} %get-tuple-element.22.blk_ref, bf16[48,1024]{1,0:T(8,128)(2,1)S(1)} %get-tuple-element.23.after.q_own, bf16[48,1024]{1,0:T(8,128)(2,1)S(1)} %collective-permute-done.q_other, ...), custom_call_target="tpu_custom_call" | custom-call | bytes 1032192 | tf_op jit(solution)/shard_map/pallas_call | solution.py:35
  20.5 1.6 %collective-permute-start.5 = (bf16[48,1152]{1,0:T(8,128)(2,1)S(1)}, bf16[48,1152]{1,0:T(8,128)(2,1)S(1)}, u32[]{:S(2)}, u32[]{:S(2)}) collective-permute-start(bf16[48,1152]{1,0:T(8,128)(2,1)S(1)} %get-tuple-element.28.after), channel_id=1, source_target_pairs={{0,4},{1,5},{2,6},{3,7},{4,0},{5,1},{6,2},{7,3},{8,12},{9,13},{10,... | collective-permute-start | bytes 331784 | tf_op jit(solution)/shard_map/ppermute | solution.py:363
  22.1 3.4 %copy-done = bf16[1024,4096]{1,0:T(8,128)(2,1)S(1)} copy-done((bf16[1024,4096]{1,0:T(8,128)(2,1)S(1)}, bf16[1024,4096]{1,0:T(8,128)(2,1)}, u32[]{:S(2)}) %copy-start) | copy-done | bytes 8388632
  26.1 1.7 %shard_map.122 = (f32[24,4096]{1,0:T(8,128)S(1)}, bf16[24,4096]{1,0:T(8,128)(2,1)S(1)}) custom-call(f32[48,1024]{1,0:T(8,128)S(1)} %get-tuple-element.26.own_ref, f32[48,128]{1,0:T(8,128)S(1)} %get-tuple-element.27.lse_ref, bf16[48,1152]{1,0:T(8,128)(2,1)S(1)} %collective-permute-done.5.got_ref, bf16[1024,4096]{1,0:T(8,128)(2,1)S(1)} %shard_map.121.w_ref), custom_call_target="tpu_custom_call" | custom-call | bytes 8720384 | tf_op jit(solution)/shard_map/pallas_call | solution.py:35
  27.9 1.4 %collective-permute-done.6 = bf16[24,4096]{1,0:T(8,128)(2,1)S(1)} collective-permute-done((bf16[24,4096]{1,0:T(8,128)(2,1)S(1)}, bf16[24,4096]{1,0:T(8,128)(2,1)S(1)}, u32[]{:S(2)}, u32[]{:S(2)}) %collective-permute-start.6) | collective-permute-done | bytes 196640 | tf_op jit(solution)/shard_map/ppermute | solution.py:363
  29.3 1.6 %collective-permute-start.7 = (bf16[24,4096]{1,0:T(8,128)(2,1)S(1)}, bf16[24,4096]{1,0:T(8,128)(2,1)S(1)}, u32[]{:S(2)}, u32[]{:S(2)}) collective-permute-start(bf16[24,4096]{1,0:T(8,128)(2,1)S(1)} %get-tuple-element.39), channel_id=1, source_target_pairs={{0,2},{1,3},{2,0},{3,1},{4,6},{5,7},{6,4},{7,5},{8,10},{9,11},{10,... | collective-permute-start | bytes 589832 | tf_op jit(solution)/shard_map/ppermute | solution.py:363
  30.9 1.7 %shard_map.123 = (bf16[48,4096]{1,0:T(8,128)(2,1)S(1)}, s32[8,256]{1,0:T(8,128)S(1)}, f32[128,128]{1,0:T(8,128)S(1)}, f32[8,128]{1,0:T(8,128)S(1)}) custom-call(s32[32]{0:T(128)S(1)} %copy-done.9, s32[8,128]{1,0:T(8,128)S(1)} %bitcast.42, s32[8,128]{1,0:T(8,128)S(1)} %bitcast.43, bf16[128,4096]{1,0:T(8,128)(2,1)S(1)} %copy-done.1, ...), custom_call_target="tpu_custom_call" | custom-call | bytes 1253504 | tf_op jit(solution)/shard_map/pallas_call | solution.py:35
  32.6 3.7 %collective-permute-done.7.refs_0_ = bf16[24,4096]{1,0:T(8,128)(2,1)S(1)} collective-permute-done((bf16[24,4096]{1,0:T(8,128)(2,1)S(1)}, bf16[24,4096]{1,0:T(8,128)(2,1)S(1)}, u32[]{:S(2)}, u32[]{:S(2)}) %collective-permute-start.7) | collective-permute-done | bytes 196640 | tf_op jit(solution)/shard_map/ppermute | solution.py:363
  36.6 3.9 %collective-permute-start.15 = (bf16[24,2048]{1,0:T(8,128)(2,1)S(1)}, bf16[24,2048]{1,0:T(8,128)(2,1)S(1)}, u32[]{:S(2)}, u32[]{:S(2)}) collective-permute-start(bf16[24,2048]{1,0:T(8,128)(2,1)S(1)} %get-tuple-element.36.after), channel_id=1, source_target_pairs={{0,16},{1,17},{2,18},{3,19},{4,20},{5,21},{6,22},{7,23},{8,24},{9,... | collective-permute-start | bytes 294920 | tf_op jit(solution)/shard_map/ppermute | solution.py:363
  41.3 6.1 %collective-permute-done.15.refs_8_ = bf16[24,2048]{1,0:T(8,128)(2,1)S(1)} collective-permute-done((bf16[24,2048]{1,0:T(8,128)(2,1)S(1)}, bf16[24,2048]{1,0:T(8,128)(2,1)S(1)}, u32[]{:S(2)}, u32[]{:S(2)}) %collective-permute-start.15) | collective-permute-done | bytes 98336 | tf_op jit(solution)/shard_map/ppermute | solution.py:363
  47.4 0.7 collective-permute-start.16
  48.2 1.3 %collective-permute-start.8 = (bf16[24,4096]{1,0:T(8,128)(2,1)S(1)}, bf16[24,4096]{1,0:T(8,128)(2,1)S(1)}, u32[]{:S(2)}, u32[]{:S(2)}) collective-permute-start(bf16[24,4096]{1,0:T(8,128)(2,1)S(1)} %get-tuple-element.35.refs_0_), channel_id=1, source_target_pairs={{0,4},{1,5},{2,6},{3,7},{4,0},{5,1},{6,2},{7,3},{8,12},{9,13},{10,... | collective-permute-start | bytes 589832 | tf_op jit(solution)/shard_map/ppermute | solution.py:363
  49.4 0.7 collective-permute-start.13
  50.2 1.3 %collective-permute-start.10 = (bf16[1,24,2048]{2,1,0:T(8,128)(2,1)S(1)}, bf16[1,24,2048]{2,1,0:T(8,128)(2,1)S(1)}, u32[]{:S(2)}, u32[]{:S(2)}) collective-permute-start(bf16[1,24,2048]{2,1,0:T(8,128)(2,1)S(1)} %bitcast.28), channel_id=1, source_target_pairs={{0,4},{1,3},{2,6},{3,1},{4,0},{5,7},{6,2},{7,5},{8,12},{9,11},{10,... | collective-permute-start | bytes 294920 | tf_op jit(solution)/shard_map/ppermute | solution.py:363
  51.5 1.6 %collective-permute-done.16 = bf16[1,24,2048]{2,1,0:T(8,128)(2,1)S(1)} collective-permute-done((bf16[1,24,2048]{2,1,0:T(8,128)(2,1)S(1)}, bf16[1,24,2048]{2,1,0:T(8,128)(2,1)S(1)}, u32[]{:S(2)}, u32[]{:S(2)}) %collective-permute-start.16) | collective-permute-done | bytes 98336 | tf_op jit(solution)/shard_map/ppermute | solution.py:363
  53.7 5.7 %collective-permute-done.13 = bf16[1,24,2048]{2,1,0:T(8,128)(2,1)S(1)} collective-permute-done((bf16[1,24,2048]{2,1,0:T(8,128)(2,1)S(1)}, bf16[1,24,2048]{2,1,0:T(8,128)(2,1)S(1)}, u32[]{:S(2)}, u32[]{:S(2)}) %collective-permute-start.13) | collective-permute-done | bytes 98336 | tf_op jit(solution)/shard_map/ppermute | solution.py:363
  60.0 1.5 %collective-permute-done.10 = bf16[1,24,2048]{2,1,0:T(8,128)(2,1)S(1)} collective-permute-done((bf16[1,24,2048]{2,1,0:T(8,128)(2,1)S(1)}, bf16[1,24,2048]{2,1,0:T(8,128)(2,1)S(1)}, u32[]{:S(2)}, u32[]{:S(2)}) %collective-permute-start.10) | collective-permute-done | bytes 98336 | tf_op jit(solution)/shard_map/ppermute | solution.py:363
  62.2 1.0 %shard_map.125 = (bf16[592,4096]{1,0:T(8,128)(2,1)S(1)}, bf16[592,4096]{1,0:T(8,128)(2,1)S(1)}) custom-call(bf16[24,2048]{1,0:T(8,128)(2,1)S(1)} %get-tuple-element.36.after, bf16[592,4096]{1,0:T(8,128)(2,1)S(1)} %bitcast.23, bf16[592,4096]{1,0:T(8,128)(2,1)S(1)} %collective-permute-done.18.refs_1_), custom_call_target="tpu_custom_call" | custom-call | bytes 9797632 | tf_op jit(solution)/shard_map/pallas_call | solution.py:35
  63.2 1.9 %collective-permute-done.14 = bf16[2,1,24,2048]{3,2,1,0:T(8,128)(2,1)S(1)} collective-permute-done((bf16[2,1,24,2048]{3,2,1,0:T(8,128)(2,1)S(1)}, bf16[2,1,24,2048]{3,2,1,0:T(8,128)(2,1)S(1)}, u32[]{:S(2)}, u32[]{:S(2)}) %collective-permute-start.14) | collective-permute-done | bytes 196640 | tf_op jit(solution)/shard_map/ppermute | solution.py:363
  65.2 2.1 %collective-permute-done.11 = bf16[2,1,24,2048]{3,2,1,0:T(8,128)(2,1)S(1)} collective-permute-done((bf16[2,1,24,2048]{3,2,1,0:T(8,128)(2,1)S(1)}, bf16[2,1,24,2048]{3,2,1,0:T(8,128)(2,1)S(1)}, u32[]{:S(2)}, u32[]{:S(2)}) %collective-permute-start.11) | collective-permute-done | bytes 196640 | tf_op jit(solution)/shard_map/ppermute | solution.py:363
  67.3 3.2 %shard_map.126 = f32[32,1,128]{2,1,0:T(1,128)S(1)} custom-call(s32[8,256]{1,0:T(8,128)S(1)} %get-tuple-element.32.target_ref, bf16[24,4096]{1,0:T(8,128)(2,1)S(1)} %get-tuple-element.35.refs_0_, bf16[24,4096]{1,0:T(8,128)(2,1)S(1)} %collective-permute-done.8.refs_1_, bf16[24,2048]{1,0:T(8,128)(2,1)S(1)} %collective-permute-done.9.refs_2_, ...), custom_call_target="tpu_custom_call" | custom-call | flops 1862270976 | bytes 11280384 | tf_op jit(solution)/shard_map/pallas_call | solution.py:35
  70.4 11.7 %all_to_all.8 = f32[32,1,128]{2,1,0:T(1,128)S(1)} all-to-all(f32[32,1,128]{2,1,0:T(1,128)S(1)} %shard_map.126), channel_id=1, replica_groups=mesh['seq'=8,'vocab'=4] {'seq','vocab'}, dimensions={0} | all-to-all | bytes 32768 | tf_op jit(solution)/shard_map/all_to_all | solution.py:475
  82.1 0.8 shard_map.127
  (47 shorter events, 6.1 us)
Async XLA Ops:
  0.0 62.2 %collective-permute-start.18 = (bf16[592,4096]{1,0:T(8,128)(2,1)}, bf16[592,4096]{1,0:T(8,128)(2,1)S(1)}, u32[]{:S(2)}, u32[]{:S(2)}) collective-permute-start(bf16[592,4096]{1,0:T(8,128)(2,1)} %refs_0_.5), channel_id=1, source_target_pairs={{0,1},{1,0},{2,3},{3,2},{4,5},{5,4},{6,7},{7,6},{8,9},{9,8},{10,11... | collective-permute-start | bytes 14549000 | tf_op jit(solution)/shard_map/ppermute | solution.py:363
  1.4 10.3 %collective-permute-start.1 = (bf16[2,128,256]{2,1,0:T(8,128)(2,1)S(1)}, bf16[2,128,256]{2,1,0:T(8,128)(2,1)S(1)}, u32[]{:S(2)}, u32[]{:S(2)}) collective-permute-start(bf16[2,128,256]{2,1,0:T(8,128)(2,1)S(1)} %pad_maximum_fusion.3.refs_0_), channel_id=1, source_target_pairs={{0,8},{1,9},{2,10},{3,11},{4,12},{5,13},{6,14},{7,15},{8,16},{9,17... | collective-permute-start | bytes 393224 | tf_op jit(solution)/shard_map/ppermute | solution.py:363
  5.9 13.2 %collective-permute-start.2 = (bf16[2,128,256]{2,1,0:T(8,128)(2,1)S(1)}, bf16[2,128,256]{2,1,0:T(8,128)(2,1)S(1)}, u32[]{:S(2)}, u32[]{:S(2)}) collective-permute-start(bf16[2,128,256]{2,1,0:T(8,128)(2,1)S(1)} %pad_maximum_fusion.3.refs_0_), channel_id=1, source_target_pairs={{0,16},{1,17},{2,18},{3,19},{4,20},{5,21},{6,22},{7,23}} | collective-permute-start | bytes 393224 | tf_op jit(solution)/shard_map/ppermute | solution.py:363
  10.4 8.7 %collective-permute-start.3 = (bf16[2,128,256]{2,1,0:T(8,128)(2,1)S(1)}, bf16[2,128,256]{2,1,0:T(8,128)(2,1)S(1)}, u32[]{:S(2)}, u32[]{:S(2)}) collective-permute-start(bf16[2,128,256]{2,1,0:T(8,128)(2,1)S(1)} %pad_maximum_fusion.3.refs_0_), channel_id=1, source_target_pairs={{0,24},{1,25},{2,26},{3,27},{4,28},{5,29},{6,30},{7,31}} | collective-permute-start | bytes 393224 | tf_op jit(solution)/shard_map/ppermute | solution.py:363
  11.7 7.4 %collective-permute-start.4 = (bf16[2,128,256]{2,1,0:T(8,128)(2,1)S(1)}, bf16[2,128,256]{2,1,0:T(8,128)(2,1)S(1)}, u32[]{:S(2)}, u32[]{:S(2)}) collective-permute-start(bf16[2,128,256]{2,1,0:T(8,128)(2,1)S(1)} %collective-permute-done.1.refs_1_), channel_id=1, source_target_pairs={{16,24},{17,25},{18,26},{19,27},{20,28},{21,29},{22,30},{23,31}} | collective-permute-start | bytes 393224 | tf_op jit(solution)/shard_map/ppermute | solution.py:363
  12.4 1.0 %copy-start.2 = (bf16[128,1024]{1,0:T(8,128)(2,1)S(1)}, bf16[128,1024]{1,0:T(8,128)(2,1)}, u32[]{:S(2)}) copy-start(bf16[128,1024]{1,0:T(8,128)(2,1)} %q_ref.1) | copy-start | bytes 786436
  13.3 0.7 copy-start.6
  14.4 4.7 %collective-permute-start = (bf16[48,1024]{1,0:T(8,128)(2,1)S(1)}, bf16[48,1024]{1,0:T(8,128)(2,1)S(1)}, u32[]{:S(2)}, u32[]{:S(2)}) collective-permute-start(bf16[48,1024]{1,0:T(8,128)(2,1)S(1)} %get-tuple-element.23.after.q_own), channel_id=1, source_target_pairs={{0,4},{1,5},{2,6},{3,7},{4,0},{5,1},{6,2},{7,3},{8,12},{9,13},{10,... | collective-permute-start | bytes 294920 | tf_op jit(solution)/shard_map/ppermute | solution.py:363
  15.9 0.8 %copy-start.3 = (bf16[128,256]{1,0:T(8,128)(2,1)S(1)}, bf16[128,256]{1,0:T(8,128)(2,1)}, u32[]{:S(2)}) copy-start(bf16[128,256]{1,0:T(8,128)(2,1)} %refs_0_.3) | copy-start | bytes 196612
  16.7 0.8 %copy-start.4 = (bf16[128,256]{1,0:T(8,128)(2,1)S(1)}, bf16[128,256]{1,0:T(8,128)(2,1)}, u32[]{:S(2)}) copy-start(bf16[128,256]{1,0:T(8,128)(2,1)} %refs_1_.1) | copy-start | bytes 196612
  20.5 5.5 %collective-permute-start.5 = (bf16[48,1152]{1,0:T(8,128)(2,1)S(1)}, bf16[48,1152]{1,0:T(8,128)(2,1)S(1)}, u32[]{:S(2)}, u32[]{:S(2)}) collective-permute-start(bf16[48,1152]{1,0:T(8,128)(2,1)S(1)} %get-tuple-element.28.after), channel_id=1, source_target_pairs={{0,4},{1,5},{2,6},{3,7},{4,0},{5,1},{6,2},{7,3},{8,12},{9,13},{10,... | collective-permute-start | bytes 331784 | tf_op jit(solution)/shard_map/ppermute | solution.py:363
  22.1 3.4 %copy-start = (bf16[1024,4096]{1,0:T(8,128)(2,1)S(1)}, bf16[1024,4096]{1,0:T(8,128)(2,1)}, u32[]{:S(2)}) copy-start(bf16[1024,4096]{1,0:T(8,128)(2,1)} %refs_0_.4) | copy-start | bytes 25165828
  26.0 36.1 %slice-start = ((s8[4849664]{0:T(1024)(128)(4,1)}), s8[4194304]{0:T(1024)(128)(4,1)S(1)}, s32[]{:S(2)}) async-start(s8[4849664]{0:T(1024)(128)(4,1)} %bitcast.22), calls=%async_computation.1 | async-start | bytes 8388608
  26.0 4.9 %copy-start.1 = (bf16[128,4096]{1,0:T(8,128)(2,1)S(1)}, bf16[128,4096]{1,0:T(8,128)(2,1)}, u32[]{:S(2)}) copy-start(bf16[128,4096]{1,0:T(8,128)(2,1)} %res_ref.1) | copy-start | bytes 3145732
  26.0 4.9 %copy-start.7 = (s32[1024]{0:T(1024)S(1)}, s32[1024]{0:T(1024)}, u32[]{:S(2)}) copy-start(s32[1024]{0:T(1024)} %param.22) | copy-start | bytes 12292
  26.1 4.9 %copy-start.8 = (s32[1024]{0:T(1024)S(1)}, s32[1024]{0:T(1024)}, u32[]{:S(2)}) copy-start(s32[1024]{0:T(1024)} %param.21) | copy-start | bytes 12292
  26.1 4.8 %copy-start.9 = (s32[32]{0:T(128)S(1)}, s32[32]{0:T(128)}, u32[]{:S(2)}) copy-start(s32[32]{0:T(128)} %levels_ref.1) | copy-start | bytes 388
  26.1 10.3 %copy-start.5 = (f32[4096]{0:T(1024)S(1)}, f32[4096]{0:T(1024)}, u32[]{:S(2)}) copy-start(f32[4096]{0:T(1024)} %param.19) | copy-start | bytes 49156
  26.1 36.1 %slice-start.1 = ((s8[4849664]{0:T(1024)(128)(4,1)}), s8[655360]{0:T(1024)(128)(4,1)S(1)}, s32[]{:S(2)}) async-start(s8[4849664]{0:T(1024)(128)(4,1)} %bitcast.22), calls=%async_computation.2 | async-start | bytes 1310720
  27.8 1.5 %collective-permute-start.6 = (bf16[24,4096]{1,0:T(8,128)(2,1)S(1)}, bf16[24,4096]{1,0:T(8,128)(2,1)S(1)}, u32[]{:S(2)}, u32[]{:S(2)}) collective-permute-start(bf16[24,4096]{1,0:T(8,128)(2,1)S(1)} %get-tuple-element.29.after_ref), channel_id=1, source_target_pairs={{0,1},{1,0},{2,3},{3,2},{4,5},{5,4},{6,7},{7,6},{8,9},{9,8},{10,11... | collective-permute-start | bytes 589832 | tf_op jit(solution)/shard_map/ppermute | solution.py:363
  29.3 7.0 %collective-permute-start.7 = (bf16[24,4096]{1,0:T(8,128)(2,1)S(1)}, bf16[24,4096]{1,0:T(8,128)(2,1)S(1)}, u32[]{:S(2)}, u32[]{:S(2)}) collective-permute-start(bf16[24,4096]{1,0:T(8,128)(2,1)S(1)} %get-tuple-element.39), channel_id=1, source_target_pairs={{0,2},{1,3},{2,0},{3,1},{4,6},{5,7},{6,4},{7,5},{8,10},{9,11},{10,... | collective-permute-start | bytes 589832 | tf_op jit(solution)/shard_map/ppermute | solution.py:363
  36.6 10.8 %collective-permute-start.15 = (bf16[24,2048]{1,0:T(8,128)(2,1)S(1)}, bf16[24,2048]{1,0:T(8,128)(2,1)S(1)}, u32[]{:S(2)}, u32[]{:S(2)}) collective-permute-start(bf16[24,2048]{1,0:T(8,128)(2,1)S(1)} %get-tuple-element.36.after), channel_id=1, source_target_pairs={{0,16},{1,17},{2,18},{3,19},{4,20},{5,21},{6,22},{7,23},{8,24},{9,... | collective-permute-start | bytes 294920 | tf_op jit(solution)/shard_map/ppermute | solution.py:363
  40.6 8.9 %collective-permute-start.12 = (bf16[24,2048]{1,0:T(8,128)(2,1)S(1)}, bf16[24,2048]{1,0:T(8,128)(2,1)S(1)}, u32[]{:S(2)}, u32[]{:S(2)}) collective-permute-start(bf16[24,2048]{1,0:T(8,128)(2,1)S(1)} %get-tuple-element.36.after), channel_id=1, source_target_pairs={{0,24},{1,25},{2,26},{3,27},{4,28},{5,29},{6,30},{7,31},{8,16},{9,... | collective-permute-start | bytes 294920 | tf_op jit(solution)/shard_map/ppermute | solution.py:363
  40.8 9.4 %collective-permute-start.9 = (bf16[24,2048]{1,0:T(8,128)(2,1)S(1)}, bf16[24,2048]{1,0:T(8,128)(2,1)S(1)}, u32[]{:S(2)}, u32[]{:S(2)}) collective-permute-start(bf16[24,2048]{1,0:T(8,128)(2,1)S(1)} %get-tuple-element.36.after), channel_id=1, source_target_pairs={{0,8},{1,9},{2,10},{3,11},{4,12},{5,13},{6,14},{7,15},{8,0},{9,1},... | collective-permute-start | bytes 294920 | tf_op jit(solution)/shard_map/ppermute | solution.py:363
  47.4 5.7 %collective-permute-start.16 = (bf16[1,24,2048]{2,1,0:T(8,128)(2,1)S(1)}, bf16[1,24,2048]{2,1,0:T(8,128)(2,1)S(1)}, u32[]{:S(2)}, u32[]{:S(2)}) collective-permute-start(bf16[1,24,2048]{2,1,0:T(8,128)(2,1)S(1)} %bitcast.24), channel_id=1, source_target_pairs={{0,4},{1,3},{2,6},{3,1},{4,0},{5,7},{6,2},{7,5},{8,12},{9,11},{10,... | collective-permute-start | bytes 294920 | tf_op jit(solution)/shard_map/ppermute | solution.py:363
  48.2 15.0 %collective-permute-start.8 = (bf16[24,4096]{1,0:T(8,128)(2,1)S(1)}, bf16[24,4096]{1,0:T(8,128)(2,1)S(1)}, u32[]{:S(2)}, u32[]{:S(2)}) collective-permute-start(bf16[24,4096]{1,0:T(8,128)(2,1)S(1)} %get-tuple-element.35.refs_0_), channel_id=1, source_target_pairs={{0,4},{1,5},{2,6},{3,7},{4,0},{5,1},{6,2},{7,3},{8,12},{9,13},{10,... | collective-permute-start | bytes 589832 | tf_op jit(solution)/shard_map/ppermute | solution.py:363
  49.4 10.0 %collective-permute-start.13 = (bf16[1,24,2048]{2,1,0:T(8,128)(2,1)S(1)}, bf16[1,24,2048]{2,1,0:T(8,128)(2,1)S(1)}, u32[]{:S(2)}, u32[]{:S(2)}) collective-permute-start(bf16[1,24,2048]{2,1,0:T(8,128)(2,1)S(1)} %bitcast.26), channel_id=1, source_target_pairs={{0,4},{1,3},{2,6},{3,1},{4,0},{5,7},{6,2},{7,5},{8,12},{9,11},{10,... | collective-permute-start | bytes 294920 | tf_op jit(solution)/shard_map/ppermute | solution.py:363
  50.2 11.3 %collective-permute-start.10 = (bf16[1,24,2048]{2,1,0:T(8,128)(2,1)S(1)}, bf16[1,24,2048]{2,1,0:T(8,128)(2,1)S(1)}, u32[]{:S(2)}, u32[]{:S(2)}) collective-permute-start(bf16[1,24,2048]{2,1,0:T(8,128)(2,1)S(1)} %bitcast.28), channel_id=1, source_target_pairs={{0,4},{1,3},{2,6},{3,1},{4,0},{5,7},{6,2},{7,5},{8,12},{9,11},{10,... | collective-permute-start | bytes 294920 | tf_op jit(solution)/shard_map/ppermute | solution.py:363
  53.1 10.1 %collective-permute-start.17 = (bf16[2,1,24,2048]{3,2,1,0:T(8,128)(2,1)S(1)}, bf16[2,1,24,2048]{3,2,1,0:T(8,128)(2,1)S(1)}, u32[]{:S(2)}, u32[]{:S(2)}) collective-permute-start(bf16[2,1,24,2048]{3,2,1,0:T(8,128)(2,1)S(1)} %pad_maximum_fusion.2), channel_id=1, source_target_pairs={{0,2},{1,5},{2,0},{3,7},{4,6},{5,1},{6,4},{7,3},{8,10},{9,13},{10,... | collective-permute-start | bytes 589832 | tf_op jit(solution)/shard_map/ppermute | solution.py:363
  59.4 5.7 %collective-permute-start.14 = (bf16[2,1,24,2048]{3,2,1,0:T(8,128)(2,1)S(1)}, bf16[2,1,24,2048]{3,2,1,0:T(8,128)(2,1)S(1)}, u32[]{:S(2)}, u32[]{:S(2)}) collective-permute-start(bf16[2,1,24,2048]{3,2,1,0:T(8,128)(2,1)S(1)} %pad_maximum_fusion.1), channel_id=1, source_target_pairs={{0,2},{1,5},{2,0},{3,7},{4,6},{5,1},{6,4},{7,3},{8,10},{9,13},{10,... | collective-permute-start | bytes 589832 | tf_op jit(solution)/shard_map/ppermute | solution.py:363
  61.5 5.7 %collective-permute-start.11 = (bf16[2,1,24,2048]{3,2,1,0:T(8,128)(2,1)S(1)}, bf16[2,1,24,2048]{3,2,1,0:T(8,128)(2,1)S(1)}, u32[]{:S(2)}, u32[]{:S(2)}) collective-permute-start(bf16[2,1,24,2048]{3,2,1,0:T(8,128)(2,1)S(1)} %pad_maximum_fusion), channel_id=1, source_target_pairs={{0,2},{1,5},{2,0},{3,7},{4,6},{5,1},{6,4},{7,3},{8,10},{9,13},{10,... | collective-permute-start | bytes 589832 | tf_op jit(solution)/shard_map/ppermute | solution.py:363
